TPU v7x, 32 devices: a whole 2x2x4 slice. The times are simulated.
32 devices in a mesh: grp: 2 (over core), seq: 4 (over y, x), row: 4 (over z).
Axes of the slice: x: 2, y: 2, z: 4, core: 2. Of those that a mesh axis runs over, the one named last changes fastest.
Arguments:
- tokens: bfloat16 [512, 70, 1150], P(('grp', 'seq')), may hold values from -6 to 6
- in_mask: int32 [512, 1150], P(('grp', 'seq')), may hold values 0 or 1
- out_mask: int32 [512, 400], P(('grp', 'seq')), may hold values 0 or 1
- lengths: int32 [512], P(('grp', 'seq')), may hold values from 35 to 70, as said below
- groups: int32 [512], P(('grp', 'seq')), may hold values from 0 to 1, as said below
- input_gate_weight: bfloat16 [1600, 1150], P('row'), may hold values from -0.1875 to 0.1875
- w_recur: bfloat16 [1600, 400], P('row'), may hold values from -0.3125 to 0.3125
- weight_mask: int32 [1600, 400], P('row'), may hold values 0 or 1
- bias: float32 [1600], P('row'), may hold values from -3 to 3
- cotangent: bfloat16 [512, 70, 400], P(('grp', 'seq')), may hold values from -6 to 6
Outputs:
- input_grad: float32 [512, 70, 1150], P(('grp', 'seq', 'row'))
- grad_input_weight: float32 [2, 1600, 1150], P('grp', 'row')
- grad_recur_weight: float32 [2, 1600, 400], P('grp', 'row')
- grad_bias: float32 [2, 1600], P('grp', 'row')
- gram: float32 [2, 2], replicated
Inputs may be any that keep to these rules, and one draw needn't show every extreme that they name: `lengths`: each sequence has the full length or fewer steps; some sequence of the batch has exactly 70 steps and some exactly 35. Both groups have sequences.
All inputs are finite; a program needn't handle non-finite values. No bound on the sum of `in_mask` or of `out_mask` or of `weight_mask` on one device may be relied on, other than what follows from the above.
Results may differ from a plain program's by a relative error of at most 0.0063.
Values may be sent and summed in bfloat16 or wider, within the bound.
No kernel may reach another device: no remote copies, remote signals or barrier semaphores. Data moves between devices by JAX's collectives and lax.ppermute only.
A program may use at most 256 MiB of HBM per device.

v0:
```python
import functools

import jax
import jax.numpy as jnp
from jax import lax
from jax.experimental import pallas as pl
from jax.experimental.pallas import tpu as pltpu
from jax.sharding import PartitionSpec as P

ACTIVATION_COEF = 2.0
TAR_BETA = 1.0
KEEP_INPUT = 0.75
KEEP_OUTPUT = 0.6
KEEP_WEIGHT = 0.5
LANES = 128
TILE = 256
VMEM_LIMIT = 58 << 20
BF16 = jnp.bfloat16
F32 = jnp.float32
OVER_ROWS = (((0,), (0,)), ((), ()))


def ceil_to(value, step):
    return -(-value // step) * step


def dot(left, right):
    return jnp.dot(left, right, preferred_element_type=F32)


def flip(block, axis, bit):
    count = lax.axis_size(axis)
    return lax.ppermute(block, axis, [(at, at ^ bit) for at in range(count)])


def exchange_sum(block, axis):
    count = lax.axis_size(axis)
    if count not in (2, 4):
        return lax.psum(block, axis)
    parts = [block] + [flip(block, axis, bit) for bit in range(1, count)]
    while len(parts) > 1:
        parts = [parts[at] + parts[at + 1] for at in range(0, len(parts), 2)]
    return parts[0]


def sigmoid(value):
    return 0.5 * jnp.tanh(0.5 * value) + 0.5


class Columns:
    def __init__(self, hidden):
        self.hidden = hidden
        self.full = hidden // LANES
        self.rest = hidden - self.full * LANES
        assert 0 < 4 * self.rest <= LANES
        self.total = 4 * hidden
        self.order = (self.full,) + tuple(range(self.full))

    def units(self, j):
        return j * LANES, min((j + 1) * LANES, self.hidden)

    def gates(self, j):
        return 4 * j * LANES, min(4 * (j + 1) * LANES, self.total)

    def gate(self, j, q):
        width = LANES if j < self.full else self.rest
        start = 4 * j * LANES + q * width
        return start, start + width

    def pack(self, gated):
        parts = []
        for j in range(self.full + 1):
            first, last = self.units(j)
            parts.append(gated[:, first:last].reshape((-1,) + gated.shape[2:]))
        return jnp.concatenate(parts, 0)

    def unpack_lanes(self, packed):
        parts = []
        for q in range(4):
            for j in range(self.full + 1):
                first, last = self.gate(j, q)
                parts.append(packed[..., first:last])
        return jnp.concatenate(parts, -1)


def drop_kernel(width, tok_ref, scale_ref, drop_ref):
    scale = scale_ref[...]
    for k in range(tok_ref.shape[0]):
        drop_ref[k, :, :width] = (tok_ref[k].astype(F32) * scale).astype(BF16)
        drop_ref[k, :, width:] = jnp.ones_like(drop_ref[k, :, width:])


def shard_kernel(plan, at_ref, in_ref, rec_ref, mask_ref, bias_ref, own_ref, *mine_ref):
    width = in_ref.shape[1]
    hidden = rec_ref.shape[1]
    bias = bias_ref[...]
    high = bias.astype(BF16)
    scale = mask_ref[...].astype(F32) / KEEP_WEIGHT
    own_ref[:, :width] = in_ref[...]
    own_ref[:, width : width + 1] = high
    own_ref[:, width + 1 : width + 2] = (bias - high.astype(F32)).astype(BF16)
    own_ref[:, plan.wide : plan.wide + hidden] = (rec_ref[...].astype(F32) * scale).astype(BF16)
    own_ref[:, plan.wide + hidden :] = jnp.zeros_like(own_ref[:, plan.wide + hidden :])
    for ref in mine_ref:
        ref[...] = own_ref[plan.window(at_ref[1], at_ref[2])]


class Plan:
    def __init__(self, hidden, wide):
        self.hidden = hidden
        self.wide = wide
        self.columns = ceil_to(wide + hidden, LANES)
        self.row_step = hidden // 4 // 16 * 16
        self.rows = hidden - 3 * self.row_step
        tiles = self.columns // LANES
        self.column_step = tiles // 2 * LANES
        self.cut = self.columns - self.column_step

    def window(self, seq_at, grp_at):
        return (
            pl.ds(pl.multiple_of(seq_at * self.row_step, 16), self.rows),
            pl.ds(pl.multiple_of(grp_at * self.column_step, LANES), self.cut),
        )


def forward_kernel(cols, plan, sub, pieced, at_ref, first_ref, second_ref, third_ref, *refs):
    count = 5 if pieced else 1
    sources = refs[:count]
    act_ref, cell_ref, prev_ref, w_ref, rec_ref, turned, even, odd, cell_s, low_s = refs[count:]
    seqs, width = first_ref.shape[1:]
    steps = act_ref.shape[0]
    hidden = cols.hidden

    def columns_of(rows_ref, start, stop, first, last):
        parts = []
        for j in range(cols.full + 1):
            unit, _ = cols.units(j)
            for q in range(4):
                low, high = cols.gate(j, q)
                if low >= start and high <= stop:
                    parts.append(rows_ref[q, unit : unit + high - low, first:last])
        return jnp.concatenate(parts, 0)

    def turned_dot(left, right):
        return lax.dot_general(left, right, (((1,), (1,)), ((), ())), preferred_element_type=F32)

    @pl.when(pl.program_id(0) == 0)
    def _():
        if pieced:
            row_at, seq_at, grp_at = at_ref[0], at_ref[1], at_ref[2]
            w_ref[row_at] = sources[0][...]
            for (m, k), (batch, index) in PIECE_AT.items():
                for gi in range(2):
                    window = plan.window(seq_at ^ m, grp_at ^ gi)
                    w_ref[(row_at ^ k,) + window] = sources[1 + 2 * gi + batch][index]
        else:
            w_ref[...] = sources[0][...]
        rec_ref[...] = w_ref[:, :, width : width + hidden]
        line = lax.broadcasted_iota(jnp.int32, (hidden, hidden), 0)
        same = line == lax.broadcasted_iota(jnp.int32, (hidden, hidden), 1)
        turned[...] = turned_dot(
            same.astype(F32).astype(BF16), columns_of(rec_ref, 0, cols.total, 0, hidden)
        ).astype(BF16)
        cell_s[...] = jnp.zeros_like(cell_s)
        low_s[...] = jnp.zeros_like(low_s)
        even[...] = turned_dot(
            first_ref[...].reshape(sub * seqs, width), columns_of(w_ref, 0, cols.total, 0, width)
        )

    lane = lax.broadcasted_iota(jnp.int32, (1, 4 * cols.rest), 1)
    tanh_lane = (lane >= 2 * cols.rest) & (lane < 3 * cols.rest)
    rest_mul = jnp.where(tanh_lane, 1.0, 0.5)
    rest_add = jnp.where(tanh_lane, 0.0, 0.5)
    spans = [cols.units(j) for j in range(cols.full + 1)]
    cells = [cell_s[:, a:b] for a, b in spans]
    lows = [low_s[:, a:b] for a, b in spans]
    chunk = ceil_to(-(-cols.total // sub), TILE)
    for k in range(steps):
        u, v = divmod(k, sub)
        now, later = (even, odd) if u % 2 == 0 else (odd, even)
        start, stop = chunk * v, min(chunk * (v + 1), cols.total)
        if start < stop:
            rows = (second_ref, third_ref)[u][...].reshape(sub * seqs, width)
            later[:, start:stop] = turned_dot(rows, columns_of(w_ref, start, stop, 0, width))
        for (a, b), low in zip(spans, lows):
            prev_ref[k, :, a:b] = low
        low = jnp.concatenate(lows, 1)
        lows = [None] * len(spans)
        for j in cols.order:
            first, last = cols.gates(j)
            pre = now[v * seqs : (v + 1) * seqs, first:last] + dot(low, turned[:, first:last])
            if j < cols.full:
                gate_i, gate_f, gate_g, gate_o = (
                    pre[:, q * LANES : (q + 1) * LANES] for q in range(4)
                )
                gate_i, gate_f, gate_o = sigmoid(gate_i), sigmoid(gate_f), sigmoid(gate_o)
                gate_g = jnp.tanh(gate_g)
                for q, gate in enumerate((gate_i, gate_f, gate_g, gate_o)):
                    a, b = cols.gate(j, q)
                    act_ref[k, :, a:b] = gate
            else:
                act = rest_mul * jnp.tanh(rest_mul * pre) + rest_add
                act_ref[k, :, first:last] = act
                gate_i, gate_f, gate_g, gate_o = (
                    act[:, q * cols.rest : (q + 1) * cols.rest] for q in range(4)
                )
            a, b = spans[j]
            cells[j] = gate_f * cells[j] + gate_i * gate_g
            cell_ref[k, :, a:b] = cells[j]
            lows[j] = (gate_o * jnp.tanh(cells[j])).astype(BF16)
    for j, (a, b) in enumerate(spans):
        cell_s[:, a:b] = cells[j]
        low_s[:, a:b] = lows[j]


def backward_kernel(
    cols,
    own,
    row_ref,
    act_ref,
    cell_ref,
    before_ref,
    act_before_ref,
    cot_ref,
    scale_ref,
    coef_ref,
    smooth_ref,
    length_ref,
    rec_ref,
    grad_ref,
    *refs,
):
    own_ref = refs[0] if own else None
    cell_grad_s, recur_s, smooth_s = refs[-3:]
    steps = act_ref.shape[0]
    place = pl.program_id(0)
    block = pl.num_programs(0) - 1 - place

    @pl.when(place == 0)
    def _():
        cell_grad_s[...] = jnp.zeros_like(cell_grad_s)
        recur_s[...] = jnp.zeros_like(recur_s)
        smooth_s[...] = jnp.zeros_like(smooth_s)

    inner = (block > 0).astype(F32)
    spans = [cols.units(j) for j in range(cols.full + 1)]

    def gates_at(ref, k, j):
        if j < cols.full:
            return [ref[k, :, a:b] for a, b in (cols.gate(j, q) for q in range(4))]
        first, last = cols.gates(j)
        packed = ref[k, :, first:last]
        return [packed[:, q * cols.rest : (q + 1) * cols.rest] for q in range(4)]

    blocks = range(cols.full + 1)
    rec = jnp.concatenate([rec_ref[q, a:b] for a, b in spans for q in range(4)], 0)
    dcell = [cell_grad_s[:, a:b] for a, b in spans]
    recur = [recur_s[:, a:b] for a, b in spans]
    smooth_next = [smooth_s[:, a:b] for a, b in spans]
    gates = [gates_at(act_ref, steps - 1, j) for j in blocks]
    tanh_cell = [jnp.tanh(cell_ref[steps - 1, :, a:b]) for a, b in spans]
    hidden = [gates[j][3] * tanh_cell[j] for j in blocks]
    for k in range(steps - 1, -1, -1):
        parts = [None] * len(spans)
        for j in cols.order:
            a, b = spans[j]
            gate_i, gate_f, gate_g, gate_o = gates[j]
            if k > 0:
                cell_before = cell_ref[k - 1, :, a:b]
                gates[j] = gates_at(act_ref, k - 1, j)
            else:
                cell_before = before_ref[0, :, a:b] * inner
                gates[j] = gates_at(act_before_ref, 0, j)
            tanh_before = jnp.tanh(cell_before)
            hidden_before = gates[j][3] * tanh_before
            valid = length_ref[:, a:b] > block * steps + k
            smooth = smooth_ref[:, a:b] * (hidden[j] - hidden_before)
            if k == 0:
                smooth = smooth * inner
            smooth = jnp.where(valid, smooth, 0.0)
            direct = scale_ref[:, a:b] * cot_ref[k, :, a:b].astype(F32) + coef_ref[:, a:b] * hidden[j]
            direct = jnp.where(valid, direct, 0.0) + smooth - smooth_next[j]
            smooth_next[j] = smooth
            dhidden = direct + recur[j]
            total = dcell[j] + dhidden * (gate_o * (1.0 - tanh_cell[j] * tanh_cell[j]))
            grads = [
                (total * (gate_g * gate_i * (1.0 - gate_i))).astype(BF16),
                (total * (cell_before * gate_f * (1.0 - gate_f))).astype(BF16),
                (total * (gate_i * (1.0 - gate_g * gate_g))).astype(BF16),
                (dhidden * (tanh_cell[j] * gate_o * (1.0 - gate_o))).astype(BF16),
            ]
            parts[j] = jnp.concatenate(grads, 1)
            first, last = cols.gates(j)
            grad_ref[k, :, first:last] = parts[j]
            if own:
                mine = grads[3]
                for q in range(3):
                    mine = jnp.where(row_ref[0] == q, grads[q], mine)
                own_ref[k, :, a:b] = mine
            dcell[j] = total * gate_f
            tanh_cell[j] = tanh_before
            hidden[j] = hidden_before
        back = dot(jnp.concatenate(parts, 1), rec)
        recur = [back[:, a:b] for a, b in spans]
    for j, (a, b) in enumerate(spans):
        cell_grad_s[:, a:b] = dcell[j]
        recur_s[:, a:b] = recur[j]
        smooth_s[:, a:b] = smooth_next[j]


def weight_kernel(grp_ref, rows_ref, drop_ref, prev_ref, pick_ref, scale_ref, keep_ref, send_ref, sums):
    steps, seqs, own = rows_ref.shape
    width = drop_ref.shape[2]
    place = pl.program_id(0)

    @pl.when(place == 0)
    def _():
        sums[...] = jnp.zeros_like(sums)

    grads = rows_ref[...]
    first = (grads * pick_ref[...][None]).reshape(steps * seqs, own)
    second = grads.reshape(steps * seqs, own) - first
    drop = drop_ref[...].reshape(steps * seqs, width)
    prev = prev_ref[...].reshape(steps * seqs, prev_ref.shape[2])
    for at, part in enumerate((first, second)):
        sums[at, :own, :width] += lax.dot_general(
            part, drop, OVER_ROWS, preferred_element_type=F32
        )
        sums[at, :own, width:] += lax.dot_general(
            part, prev, OVER_ROWS, preferred_element_type=F32
        )

    @pl.when(place == pl.num_programs(0) - 1)
    def _():
        rows = keep_ref.shape[1]
        for at in range(2):
            sums[at, :own, width:] = sums[at, :own, width:] * scale_ref[...]
        for part in range(keep_ref.shape[0]):
            span = slice(part * rows, (part + 1) * rows)
            keep_ref[part] = sums[grp_ref[0], span]
            send_ref[part] = sums[1 - grp_ref[0], span].astype(BF16)


def params():
    return pltpu.CompilerParams(
        dimension_semantics=("arbitrary",), vmem_limit_bytes=VMEM_LIMIT
    )


def fixed(*shape):
    return pl.BlockSpec(shape, lambda *_: (0,) * len(shape))


def gather_pieces(mine, counts, beside):
    hold = lax.optimization_barrier
    one, two, beside, counts = hold(
        (flip(mine, "row", 1), flip(mine, "row", 2), beside, counts + flip(counts, "grp", 1))
    )
    near = jnp.stack([one, two])
    near_one, near_two, three, *others = hold(
        [flip(near, "seq", 1), flip(near, "seq", 2), flip(two, "row", 1)]
        + [flip(counts, "seq", bit) for bit in range(1, 4)]
    )
    counts = (counts + others[0]) + (others[1] + others[2])
    early = jnp.concatenate([near, near_one, near_two, three[None]], 0)
    across, diag_one, diag_two, *last = hold(
        [flip(early, "grp", 1), flip(near_two[0], "seq", 1), flip(near_one[1], "seq", 2)]
        + [flip(three, "seq", bit) for bit in range(1, 4)]
    )
    late = jnp.stack([diag_one, diag_two] + last)
    return early, late, across, flip(late, "grp", 1), counts, beside


PIECE_AT = {
    (0, 1): (0, 0),
    (0, 2): (0, 1),
    (1, 1): (0, 2),
    (1, 2): (0, 3),
    (2, 1): (0, 4),
    (2, 2): (0, 5),
    (0, 3): (0, 6),
    (3, 1): (1, 0),
    (3, 2): (1, 1),
    (1, 3): (1, 2),
    (2, 3): (1, 3),
    (3, 3): (1, 4),
}


def local(
    tokens,
    in_mask,
    out_mask,
    lengths,
    groups,
    input_gate_weight,
    w_recur,
    weight_mask,
    bias,
    cotangent,
):
    seq_count, time_steps, width_in = tokens.shape
    hidden = cotangent.shape[2]
    row_count = input_gate_weight.shape[0]
    row_at = lax.axis_index("row")
    grp_at = lax.axis_index("grp")
    seq_at = lax.axis_index("seq")
    rows_n, seq_n = lax.axis_size("row"), lax.axis_size("seq")
    cols = Columns(hidden)
    wide = ceil_to(width_in + 2, LANES)
    share = seq_count // rows_n
    own = row_count == hidden
    pieced = own and rows_n == 4 and seq_n == 4 and lax.axis_size("grp") == 2

    w_scale = weight_mask.astype(F32) / KEEP_WEIGHT
    plan = Plan(hidden, wide)
    at = jnp.stack([row_at, seq_at, grp_at]).astype(jnp.int32)
    own_weights, *mine = pl.pallas_call(
        functools.partial(shard_kernel, plan),
        grid_spec=pltpu.PrefetchScalarGridSpec(
            num_scalar_prefetch=1,
            grid=(1,),
            in_specs=[
                fixed(row_count, width_in),
                fixed(row_count, hidden),
                fixed(row_count, hidden),
                fixed(row_count, 1),
            ],
            out_specs=[fixed(row_count, plan.columns)] + [fixed(plan.rows, plan.cut)] * pieced,
        ),
        out_shape=[jax.ShapeDtypeStruct((row_count, plan.columns), BF16)]
        + [jax.ShapeDtypeStruct((plan.rows, plan.cut), BF16)] * pieced,
        compiler_params=params(),
        name="shard",
    )(at, input_gate_weight, w_recur, weight_mask, bias[:, None])
    sub = max(s for s in range(1, 8) if time_steps % (2 * s) == 0)
    steps = 2 * sub
    blocks = time_steps // steps

    def at_time(width):
        return pl.BlockSpec((steps, seq_count, width), lambda b, *_: (b, 0, 0))

    in_scale = in_mask.astype(F32) / KEEP_INPUT
    dropped = pl.pallas_call(
        functools.partial(drop_kernel, width_in),
        grid=(blocks,),
        in_specs=[at_time(width_in), fixed(seq_count, width_in)],
        out_specs=at_time(wide),
        out_shape=jax.ShapeDtypeStruct((time_steps, seq_count, wide), BF16),
        compiler_params=params(),
        name="drop",
    )(jnp.swapaxes(tokens, 0, 1), in_scale)
    cot_time = jnp.swapaxes(cotangent, 0, 1)

    group_hot = (groups[:, None] == jnp.arange(2)[None, :]).astype(F32)
    valid_count = jnp.clip(lengths, 0, time_steps).astype(F32)
    counts = jnp.sum(group_hot * valid_count[:, None], 0)
    if pieced:
        *pieces, counts, dropped = gather_pieces(mine[0], counts, dropped)
        sources = [own_weights] + pieces
    else:
        counts = lax.psum(counts, ("grp", "seq"))
        whole = lax.all_gather(own_weights, "row", axis=0, tiled=True)
        sources = [whole.reshape(4, hidden, plan.columns)]
    group_ratio = jnp.sum(counts) / counts
    seq_ratio = jnp.sum(group_hot * group_ratio[None, :], 1)
    out_scale = out_mask.astype(F32) / KEEP_OUTPUT
    act_coef = 2.0 * ACTIVATION_COEF * seq_ratio[:, None] * out_scale * out_scale
    smooth_coef = jnp.broadcast_to(2.0 * TAR_BETA * seq_ratio[:, None], (seq_count, hidden))
    length_wide = jnp.broadcast_to(lengths[:, None], (seq_count, hidden))

    acts, cells, prev_low, weights, w_rec = pl.pallas_call(
        functools.partial(forward_kernel, cols, plan, sub, pieced),
        grid_spec=pltpu.PrefetchScalarGridSpec(
            num_scalar_prefetch=1,
            grid=(blocks,),
            in_specs=[
                fixed(sub, seq_count, wide),
                pl.BlockSpec((sub, seq_count, wide), lambda b, *_: (2 * b + 1, 0, 0)),
                pl.BlockSpec(
                    (sub, seq_count, wide),
                    lambda b, *_: (jnp.minimum(2 * b + 2, 2 * blocks - 1), 0, 0),
                ),
            ]
            + [fixed(*source.shape) for source in sources],
            out_specs=[
                at_time(cols.total),
                at_time(hidden),
                at_time(hidden),
                fixed(4, hidden, plan.columns),
                fixed(4, hidden, hidden),
            ],
            scratch_shapes=[
                pltpu.VMEM((hidden, cols.total), BF16),
                pltpu.VMEM((sub * seq_count, cols.total), F32),
                pltpu.VMEM((sub * seq_count, cols.total), F32),
                pltpu.VMEM((seq_count, hidden), F32),
                pltpu.VMEM((seq_count, hidden), BF16),
            ],
        ),
        out_shape=[
            jax.ShapeDtypeStruct((time_steps, seq_count, cols.total), F32),
            jax.ShapeDtypeStruct((time_steps, seq_count, hidden), F32),
            jax.ShapeDtypeStruct((time_steps, seq_count, hidden), BF16),
            jax.ShapeDtypeStruct((4, hidden, plan.columns), BF16),
            jax.ShapeDtypeStruct((4, hidden, hidden), BF16),
        ],
        compiler_params=params(),
        name="forward",
    )(at, dropped, dropped, dropped, *sources)

    def back(b):
        return 2 * blocks - 1 - b

    def before(width):
        return pl.BlockSpec(
            (1, seq_count, width), lambda b, *_: (jnp.maximum(back(b) * sub - 1, 0), 0, 0)
        )

    def back_time(width):
        return pl.BlockSpec((sub, seq_count, width), lambda b, *_: (back(b), 0, 0))

    grad_specs = [back_time(cols.total)] + [back_time(hidden)] * own
    grad_shapes = [cols.total] + [hidden] * own
    grads, *own_rows = pl.pallas_call(
        functools.partial(backward_kernel, cols, own),
        grid_spec=pltpu.PrefetchScalarGridSpec(
            num_scalar_prefetch=1,
            grid=(2 * blocks,),
            in_specs=[
                back_time(cols.total),
                back_time(hidden),
                before(hidden),
                before(cols.total),
                back_time(hidden),
                fixed(seq_count, hidden),
                fixed(seq_count, hidden),
                fixed(seq_count, hidden),
                fixed(seq_count, hidden),
                fixed(4, hidden, hidden),
            ],
            out_specs=grad_specs,
            scratch_shapes=[pltpu.VMEM((seq_count, hidden), F32)] * 3,
        ),
        out_shape=[
            jax.ShapeDtypeStruct((time_steps, seq_count, width), BF16) for width in grad_shapes
        ],
        compiler_params=params(),
        name="backward",
    )(
        row_at[None],
        acts,
        cells,
        cells,
        acts,
        cot_time,
        out_scale,
        act_coef,
        smooth_coef,
        length_wide,
        w_rec,
    )

    if own:
        own_rows = own_rows[0]
    else:
        own_rows = lax.dynamic_slice_in_dim(
            cols.unpack_lanes(grads), row_at * row_count, row_count, 2
        )
    pick = jnp.broadcast_to((groups == 0).astype(BF16)[:, None], (seq_count, row_count))
    columns = wide + hidden
    part_rows = ceil_to(-(-row_count // seq_n), 8)
    keep, send = pl.pallas_call(
        weight_kernel,
        grid_spec=pltpu.PrefetchScalarGridSpec(
            num_scalar_prefetch=1,
            grid=(blocks,),
            in_specs=[
                at_time(row_count),
                at_time(wide),
                at_time(hidden),
                fixed(seq_count, row_count),
                fixed(row_count, hidden),
            ],
            out_specs=[fixed(seq_n, part_rows, columns)] * 2,
            scratch_shapes=[pltpu.VMEM((2, seq_n * part_rows, columns), F32)],
        ),
        out_shape=[
            jax.ShapeDtypeStruct((seq_n, part_rows, columns), F32),
            jax.ShapeDtypeStruct((seq_n, part_rows, columns), BF16),
        ],
        compiler_params=params(),
        name="weights",
    )(grp_at[None], own_rows, dropped, prev_low, pick, w_scale)

    both = (keep + flip(send, "grp", 1).astype(F32)).astype(BF16)
    swapped = lax.all_to_all(both, "seq", 0, 0, tiled=True)

    own_seqs = lax.dynamic_slice_in_dim(grads, row_at * share, share, 1)
    own_scale = lax.dynamic_slice_in_dim(in_scale, row_at * share, share, 0)
    w_in = cols.pack(weights[:, :, :width_in])
    input_time = jnp.einsum("tsr,rk->tsk", own_seqs, w_in, preferred_element_type=F32)
    input_grad = jnp.swapaxes(input_time * own_scale[None], 0, 1)
    swapped, input_grad = lax.optimization_barrier((swapped, input_grad))

    total = jnp.sum(swapped.astype(F32), 0).astype(BF16)
    everyone = lax.all_to_all(
        jnp.broadcast_to(total[None], (seq_n, part_rows, columns)), "seq", 0, 0, tiled=True
    )
    peer = flip(total, "grp", 1)
    ours, theirs = (
        jnp.concatenate([part[:, : width_in + 1], part[:, wide:]], 1).astype(F32)
        for part in (total, peer)
    )
    first = jnp.where(grp_at == 0, ours, theirs)
    second = jnp.where(grp_at == 0, theirs, ours)
    dots = [jnp.sum(a * b) for a, b in ((first, first), (first, second), (second, second))]
    gram = jnp.stack([dots[0], dots[1], dots[1], dots[2]]).reshape(2, 2)
    gram = exchange_sum(exchange_sum(gram, "seq"), "row")
    everyone, gram = lax.optimization_barrier((everyone, gram))
    everyone = everyone.reshape(seq_n * part_rows, columns)[:row_count].astype(F32)

    return (
        input_grad,
        everyone[None, :, :width_in],
        everyone[None, :, wide:],
        everyone[None, :, width_in],
        gram,
    )


def solution(mesh):
    return jax.shard_map(
        local,
        mesh=mesh,
        in_specs=(
            P(("grp", "seq"), None, None),
            P(("grp", "seq"), None),
            P(("grp", "seq"), None),
            P(("grp", "seq")),
            P(("grp", "seq")),
            P("row", None),
            P("row", None),
            P("row", None),
            P("row"),
            P(("grp", "seq"), None, None),
        ),
        out_specs=(
            P(("grp", "seq", "row"), None, None),
            P("grp", "row", None),
            P("grp", "row", None),
            P("grp", "row"),
            P(),
        ),
        check_vma=False,
    )
```

profile of v0, /device:TPU:0, one launch (start us, length us, event | category | flops | bytes accessed | tf_op | source)
XLA Modules:
  0.0 238.3 jit_solution(5740703054097813897)
XLA Ops:
  0.7 1.5 copy.16.bias_ref
  2.2 0.6 pad_add_fusion.at_ref
  2.8 3.7 %shard.1 = (bf16[400,1664]{1,0:T(8,128)(2,1)}, bf16[112,896]{1,0:T(8,128)(2,1)}) custom-call(s32[3]{0:T(128)} %pad_add_fusion.at_ref, bf16[400,1150]{1,0:T(8,128)(2,1)} %in_ref.1, bf16[400,400]{1,0:T(8,128)(2,1)} %rec_ref.1, s32[400,400]{1,0:T(8,128)} %mask_ref.1, f32[400,1]{1,0:T(8,128)} %copy.16.bias_ref), custom_call_target="tpu_custom_call" | custom-call | tf_op jit(solution)/shard_map/shard/pallas_call | solution.py:418
  6.5 3.0 %collective-permute-start = (bf16[112,896]{1,0:T(8,128)(2,1)}, bf16[112,896]{1,0:T(8,128)(2,1)S(1)}, u32[]{:S(2)}, u32[]{:S(2)}) collective-permute-start(bf16[112,896]{1,0:T(8,128)(2,1)} %get-tuple-element.36), channel_id=1, source_target_pairs={{0,1},{1,0},{2,3},{3,2},{4,5},{5,4},{6,7},{7,6},{8,9},{9,8},{10,11... | collective-permute-start | bytes 602120 | tf_op jit(solution)/shard_map/ppermute | solution.py:33
  9.5 2.6 %collective-permute-start.1 = (bf16[112,896]{1,0:T(8,128)(2,1)}, bf16[112,896]{1,0:T(8,128)(2,1)S(1)}, u32[]{:S(2)}, u32[]{:S(2)}) collective-permute-start(bf16[112,896]{1,0:T(8,128)(2,1)} %get-tuple-element.36), channel_id=1, source_target_pairs={{0,2},{1,3},{2,0},{3,1},{4,6},{5,7},{6,4},{7,5},{8,10},{9,11},{10,... | collective-permute-start | bytes 602120 | tf_op jit(solution)/shard_map/ppermute | solution.py:33
  12.1 0.1 select_reduce_fusion.1
  12.3 0.7 convert_multiply_fusion.1.scale_ref
  13.1 10.3 %drop.1.first_ref.second_ref.third_ref.drop_ref = bf16[70,64,1152]{2,1,0:T(8,128)(2,1)} custom-call(bf16[70,64,1150]{2,1,0:T(8,128)(2,1)} %bitcast.44, f32[64,1150]{1,0:T(8,128)} %convert_multiply_fusion.1.scale_ref), custom_call_target="tpu_custom_call" | custom-call | tf_op jit(solution)/shard_map/drop/pallas_call | solution.py:444
  23.5 1.6 collective-permute-start.3
  25.0 1.5 collective-permute-start.4
  26.6 0.5 collective-permute-start.6
  27.1 0.5 collective-permute-start.7
  27.6 0.4 collective-permute-start.5
  28.1 7.2 %collective-permute-done.6 = f32[2]{0:T(128)S(1)} collective-permute-done((f32[2]{0:T(128)S(1)}, f32[2]{0:T(128)S(1)}, u32[]{:S(2)}, u32[]{:S(2)}) %collective-permute-start.6) | collective-permute-done | bytes 40 | tf_op jit(solution)/shard_map/ppermute | solution.py:33
  35.3 2.4 %collective-permute-start.8 = (f32[2]{0:T(128)S(1)}, f32[2]{0:T(128)S(1)}, u32[]{:S(2)}, u32[]{:S(2)}) collective-permute-start(f32[2]{0:T(128)S(1)} %add.37), channel_id=1, source_target_pairs={{0,12},{4,8},{8,4},{12,0},{1,13},{5,9},{9,5},{13,1},{2,14},{6,10},... | collective-permute-start | bytes 32 | tf_op jit(solution)/shard_map/ppermute | solution.py:33
  37.8 2.0 collective-permute-done.8
  40.0 1.0 convert_multiply_fusion.scale_ref
  41.0 1.5 collective-permute-start.12
  42.5 1.5 collective-permute-start.13
  44.0 0.5 collective-permute-start.14
  44.5 1.6 collective-permute-start.10
  46.1 10.9 %collective-permute-done.10 = bf16[112,896]{1,0:T(8,128)(2,1)S(1)} collective-permute-done((bf16[112,896]{1,0:T(8,128)(2,1)S(1)}, bf16[112,896]{1,0:T(8,128)(2,1)S(1)}, u32[]{:S(2)}, u32[]{:S(2)}) %collective-permute-start.10) | collective-permute-done | bytes 200736 | tf_op jit(solution)/shard_map/ppermute | solution.py:33
  57.0 1.5 collective-permute-start.11
  58.5 5.1 %collective-permute-done.11 = bf16[112,896]{1,0:T(8,128)(2,1)S(1)} collective-permute-done((bf16[112,896]{1,0:T(8,128)(2,1)S(1)}, bf16[112,896]{1,0:T(8,128)(2,1)S(1)}, u32[]{:S(2)}, u32[]{:S(2)}) %collective-permute-start.11) | collective-permute-done | bytes 200736 | tf_op jit(solution)/shard_map/ppermute | solution.py:33
  63.9 0.8 fusion.9
  64.7 0.6 broadcast_divide_fusion
  65.5 0.7 multiply_multiply_fusion
  66.2 0.3 collective-permute-done.15.refs_4_
  66.5 0.9 copy-done.4
  67.4 51.5 %forward.1 = (f32[70,64,1600]{2,1,0:T(8,128)}, f32[70,64,400]{2,1,0:T(8,128)}, bf16[70,64,400]{2,1,0:T(8,128)(2,1)}, bf16[4,400,1664]{2,1,0:T(8,128)(2,1)}, bf16[4,400,400]{2,1,0:T(8,128)(2,1)}) custom-call(s32[3]{0:T(128)} %pad_add_fusion.at_ref, bf16[70,64,1152]{2,1,0:T(8,128)(2,1)} %drop.1.first_ref.second_ref.third_ref.drop_ref, ...), custom_call_target="tpu_custom_call" | custom-call | tf_op jit(solution)/shard_map/forward/pallas_call | solution.py:472
  118.9 0.7 broadcast_in_dim.24.smooth_ref
  119.7 0.7 broadcast_in_dim.25.length_ref
  120.4 35.0 %backward.1 = (bf16[70,64,1600]{2,1,0:T(8,128)(2,1)}, bf16[70,64,400]{2,1,0:T(8,128)(2,1)}) custom-call(s32[1]{0:T(128)} %bitcast.1.row_ref, f32[70,64,1600]{2,1,0:T(8,128)} %get-tuple-element.51.act_ref.act_before_ref, f32[70,64,400]{2,1,0:T(8,128)} %get-tuple-element.52.cell_ref.before_ref, f32[70,64,400]{2,1,0:T(8,128)} %get-tuple-element.52.cell_ref.before_ref, ...), custom_call_target="tpu_custom_call" | custom-call | tf_op jit(solution)/shard_map/backward/pallas_call | solution.py:525
  155.4 0.7 broadcast_in_dim.26.pick_ref
  156.1 21.8 %weights.1 = (f32[4,104,1552]{2,1,0:T(8,128)}, bf16[4,104,1552]{2,1,0:T(8,128)(2,1)}) custom-call(s32[1]{0:T(128)} %bitcast.grp_ref, bf16[70,64,400]{2,1,0:T(8,128)(2,1)} %get-tuple-element.57.rows_ref, bf16[70,64,1152]{2,1,0:T(8,128)(2,1)} %drop.1.first_ref.second_ref.third_ref.drop_ref, bf16[70,64,400]{2,1,0:T(8,128)(2,1)} %get-tuple-element.58.prev_ref, ...), custom_call_target="tpu_custom_call" | custom-call | tf_op jit(solution)/shard_map/weights/pallas_call | solution.py:573
  177.9 0.1 collective-permute-start.16
  178.0 0.9 constant_dynamic-slice_fusion
  178.9 2.3 collective-permute-done.16
  181.2 3.2 %add_convert_fusion = bf16[4,104,1552]{2,1,0:T(8,128)(2,1)} fusion(f32[4,104,1552]{2,1,0:T(8,128)} %get-tuple-element.59, bf16[4,104,1552]{2,1,0:T(8,128)(2,1)S(1)} %collective-permute-done.16), kind=kLoop, calls=%fused_computation.9 | loop fusion | flops 1936896 | bytes 5165056 | tf_op jit(solution)/shard_map/convert_element_type | solution.py:596
  184.4 3.6 %all-to-all-start = ((bf16[4,104,1552]{2,1,0:T(8,128)(2,1)}), bf16[4,104,1552]{2,1,0:T(8,128)(2,1)S(1)}, u32[]{:S(2)}, u32[]{:S(2)}) async-start(bf16[4,104,1552]{2,1,0:T(8,128)(2,1)} %add_convert_fusion), calls=%async_computation | async-start | bytes 2768896 | tf_op jit(solution)/shard_map/all_to_all | solution.py:597
  188.1 2.4 fusion.10
  190.4 0.9 slice.52
  191.4 9.8 %multiply_bitcast_fusion = f32[16,70,1150]{2,0,1:T(8,128)} fusion(bf16[70,64,1600]{2,1,0:T(8,128)(2,1)} %get-tuple-element.61, s32[]{:T(128)S(6)} %select_n.16, bf16[64,1150]{1,0:T(8,128)(2,1)S(1)} %bitcast.52, bf16[512,1150]{1,0:T(8,128)(2,1)S(1)} %bitcast.48, bf16[512,1150]{1,0:T(8,128)(2,1)S(1)} %bitcast.49, bf16[512,1150]{1,0:T(8,128)(2,1)S(1)} %bitcast.47, ...), kind=kOutput, calls=%fused_computation | convolution fusion | flops 4137607936 | bytes 12632964 | tf_op jit(solution)/shard_map/tsr,rk->tsk/dot_general | solution.py:602
  201.1 4.6 %all-to-all-done = bf16[4,104,1552]{2,1,0:T(8,128)(2,1)S(1)} async-done(((bf16[4,104,1552]{2,1,0:T(8,128)(2,1)}), bf16[4,104,1552]{2,1,0:T(8,128)(2,1)S(1)}, u32[]{:S(2)}, u32[]{:S(2)}) %all-to-all-start) | async-done | bytes 1291296 | tf_op jit(solution)/shard_map/all_to_all | solution.py:597
  205.8 0.2 reduce_sum.69
  206.0 1.2 broadcast_in_dim.27
  207.2 3.5 %all-to-all-start.1 = ((bf16[4,104,1552]{2,1,0:T(8,128)(2,1)}), bf16[4,104,1552]{2,1,0:T(8,128)(2,1)S(1)}, u32[]{:S(2)}, u32[]{:S(2)}) async-start(bf16[4,104,1552]{2,1,0:T(8,128)(2,1)} %broadcast_in_dim.27), calls=%async_computation.1 | async-start | bytes 2768896 | tf_op jit(solution)/shard_map/all_to_all | solution.py:607
  210.8 1.6 collective-permute-done.17
  212.5 1.0 multiply_reduce_fusion.2
  213.5 2.0 pad_maximum_fusion.3
  215.6 1.9 collective-permute-start.18
  217.5 1.5 collective-permute-start.19
  219.0 8.5 %collective-permute-done.18 = f32[2,2]{1,0:T(2,128)S(1)} collective-permute-done((f32[2,2]{1,0:T(2,128)S(1)}, f32[2,2]{1,0:T(2,128)S(1)}, u32[]{:S(2)}, u32[]{:S(2)}) %collective-permute-start.18) | collective-permute-done | bytes 48 | tf_op jit(solution)/shard_map/ppermute | solution.py:33
  227.6 0.9 collective-permute-done.20
  228.5 0.4 collective-permute-start.21
  228.9 0.1 collective-permute-start.22
  229.0 3.8 %collective-permute-start.23 = (f32[2,2]{1,0:T(2,128)S(1)}, f32[2,2]{1,0:T(2,128)S(1)}, u32[]{:S(2)}, u32[]{:S(2)}) collective-permute-start(f32[2,2]{1,0:T(2,128)S(1)} %add_add_fusion.1), channel_id=1, source_target_pairs={{0,3},{1,2},{2,1},{3,0},{4,7},{5,6},{6,5},{7,4},{8,11},{9,10},{10,... | collective-permute-start | bytes 56 | tf_op jit(solution)/shard_map/ppermute | solution.py:33
  232.9 0.5 collective-permute-done.22
  233.4 1.0 collective-permute-done.23
  234.4 0.6 add_add_fusion
  235.0 0.2 slice_convert_fusion
  235.2 1.4 slice_bitcast_fusion
  236.5 1.0 slice_bitcast_fusion.1
  237.5 0.8 slice_reduce_fusion
  (60 shorter events, 1.1 us)
Async XLA Ops:
  0.6 11.5 %copy-start.7 = (s32[64]{0:T(128)S(1)}, s32[64]{0:T(128)}, u32[]{:S(2)}) copy-start(s32[64]{0:T(128)} %param.13) | copy-start | bytes 772
  0.6 11.5 %copy-start.8 = (s32[64]{0:T(128)S(1)}, s32[64]{0:T(128)}, u32[]{:S(2)}) copy-start(s32[64]{0:T(128)} %param.14) | copy-start | bytes 772
  0.7 11.7 %copy-start.5 = (s32[64,1150]{1,0:T(8,128)S(1)}, s32[64,1150]{1,0:T(8,128)}, u32[]{:S(2)}) copy-start(s32[64,1150]{1,0:T(8,128)} %param.11) | copy-start | bytes 883204
  6.5 16.9 %collective-permute-start = (bf16[112,896]{1,0:T(8,128)(2,1)}, bf16[112,896]{1,0:T(8,128)(2,1)S(1)}, u32[]{:S(2)}, u32[]{:S(2)}) collective-permute-start(bf16[112,896]{1,0:T(8,128)(2,1)} %get-tuple-element.36), channel_id=1, source_target_pairs={{0,1},{1,0},{2,3},{3,2},{4,5},{5,4},{6,7},{7,6},{8,9},{9,8},{10,11... | collective-permute-start | bytes 602120 | tf_op jit(solution)/shard_map/ppermute | solution.py:33
  9.5 13.9 %collective-permute-start.1 = (bf16[112,896]{1,0:T(8,128)(2,1)}, bf16[112,896]{1,0:T(8,128)(2,1)S(1)}, u32[]{:S(2)}, u32[]{:S(2)}) collective-permute-start(bf16[112,896]{1,0:T(8,128)(2,1)} %get-tuple-element.36), channel_id=1, source_target_pairs={{0,2},{1,3},{2,0},{3,1},{4,6},{5,7},{6,4},{7,5},{8,10},{9,11},{10,... | collective-permute-start | bytes 602120 | tf_op jit(solution)/shard_map/ppermute | solution.py:33
  12.3 11.1 %collective-permute-start.2 = (f32[2]{0:T(128)S(1)}, f32[2]{0:T(128)S(1)}, u32[]{:S(2)}, u32[]{:S(2)}) collective-permute-start(f32[2]{0:T(128)S(1)} %select_reduce_fusion.1), channel_id=1, source_target_pairs={{0,16},{16,0},{1,17},{17,1},{2,18},{18,2},{3,19},{19,3},{4,20},{20... | collective-permute-start | bytes 32 | tf_op jit(solution)/shard_map/ppermute | solution.py:33
  23.4 16.6 %copy-start = (s32[400,400]{1,0:T(8,128)S(1)}, s32[400,400]{1,0:T(8,128)}, u32[]{:S(2)}) copy-start(s32[400,400]{1,0:T(8,128)} %mask_ref.1) | copy-start | bytes 1920004
  23.5 16.3 %collective-permute-start.3 = (bf16[2,112,896]{2,1,0:T(8,128)(2,1)S(1)}, bf16[2,112,896]{2,1,0:T(8,128)(2,1)S(1)}, u32[]{:S(2)}, u32[]{:S(2)}) collective-permute-start(bf16[2,112,896]{2,1,0:T(8,128)(2,1)S(1)} %pad_maximum_fusion), channel_id=1, source_target_pairs={{0,4},{4,0},{8,12},{12,8},{1,5},{5,1},{9,13},{13,9},{2,6},{6,2},{1... | collective-permute-start | bytes 1204232 | tf_op jit(solution)/shard_map/ppermute | solution.py:33
  25.0 14.7 %collective-permute-start.4 = (bf16[2,112,896]{2,1,0:T(8,128)(2,1)S(1)}, bf16[2,112,896]{2,1,0:T(8,128)(2,1)S(1)}, u32[]{:S(2)}, u32[]{:S(2)}) collective-permute-start(bf16[2,112,896]{2,1,0:T(8,128)(2,1)S(1)} %pad_maximum_fusion), channel_id=1, source_target_pairs={{0,8},{4,12},{8,0},{12,4},{1,9},{5,13},{9,1},{13,5},{2,10},{6,14},... | collective-permute-start | bytes 1204232 | tf_op jit(solution)/shard_map/ppermute | solution.py:33
  26.6 8.7 %collective-permute-start.6 = (f32[2]{0:T(128)S(1)}, f32[2]{0:T(128)S(1)}, u32[]{:S(2)}, u32[]{:S(2)}) collective-permute-start(f32[2]{0:T(128)S(1)} %add.37), channel_id=1, source_target_pairs={{0,4},{4,0},{8,12},{12,8},{1,5},{5,1},{9,13},{13,9},{2,6},{6,2},{1... | collective-permute-start | bytes 32 | tf_op jit(solution)/shard_map/ppermute | solution.py:33
  27.1 10.7 %collective-permute-start.7 = (f32[2]{0:T(128)S(1)}, f32[2]{0:T(128)S(1)}, u32[]{:S(2)}, u32[]{:S(2)}) collective-permute-start(f32[2]{0:T(128)S(1)} %add.37), channel_id=1, source_target_pairs={{0,8},{4,12},{8,0},{12,4},{1,9},{5,13},{9,1},{13,5},{2,10},{6,14},... | collective-permute-start | bytes 32 | tf_op jit(solution)/shard_map/ppermute | solution.py:33
  27.6 12.1 %collective-permute-start.5 = (bf16[112,896]{1,0:T(8,128)(2,1)S(1)}, bf16[112,896]{1,0:T(8,128)(2,1)S(1)}, u32[]{:S(2)}, u32[]{:S(2)}) collective-permute-start(bf16[112,896]{1,0:T(8,128)(2,1)S(1)} %collective-permute-done.1), channel_id=1, source_target_pairs={{0,1},{1,0},{2,3},{3,2},{4,5},{5,4},{6,7},{7,6},{8,9},{9,8},{10,11... | collective-permute-start | bytes 602120 | tf_op jit(solution)/shard_map/ppermute | solution.py:33
  35.3 4.4 %collective-permute-start.8 = (f32[2]{0:T(128)S(1)}, f32[2]{0:T(128)S(1)}, u32[]{:S(2)}, u32[]{:S(2)}) collective-permute-start(f32[2]{0:T(128)S(1)} %add.37), channel_id=1, source_target_pairs={{0,12},{4,8},{8,4},{12,0},{1,13},{5,9},{9,5},{13,1},{2,14},{6,10},... | collective-permute-start | bytes 32 | tf_op jit(solution)/shard_map/ppermute | solution.py:33
  39.9 23.9 %copy-start.1 = (bf16[7,112,896]{2,1,0:T(8,128)(2,1)}, bf16[7,112,896]{2,1,0:T(8,128)(2,1)S(1)}, u32[]{:S(2)}) copy-start(bf16[7,112,896]{2,1,0:T(8,128)(2,1)S(1)} %bitcast_dynamic-update-slice_fusion.5.refs_1_) | copy-start | bytes 4214788
  39.9 25.6 %copy-start.6 = (s32[64,400]{1,0:T(8,128)S(1)}, s32[64,400]{1,0:T(8,128)}, u32[]{:S(2)}) copy-start(s32[64,400]{1,0:T(8,128)} %param.12) | copy-start | bytes 307204
  39.9 23.7 %collective-permute-start.9 = (bf16[7,112,896]{2,1,0:T(8,128)(2,1)S(1)}, bf16[7,112,896]{2,1,0:T(8,128)(2,1)S(1)}, u32[]{:S(2)}, u32[]{:S(2)}) collective-permute-start(bf16[7,112,896]{2,1,0:T(8,128)(2,1)S(1)} %bitcast_dynamic-update-slice_fusion.5.refs_1_), channel_id=1, source_target_pairs={{0,16},{16,0},{1,17},{17,1},{2,18},{18,2},{3,19},{19,3},{4,20},{20... | collective-permute-start | bytes 4214792 | tf_op jit(solution)/shard_map/ppermute | solution.py:33
  41.0 22.6 %collective-permute-start.12 = (bf16[112,896]{1,0:T(8,128)(2,1)S(1)}, bf16[112,896]{1,0:T(8,128)(2,1)S(1)}, u32[]{:S(2)}, u32[]{:S(2)}) collective-permute-start(bf16[112,896]{1,0:T(8,128)(2,1)S(1)} %collective-permute-done.5), channel_id=1, source_target_pairs={{0,4},{4,0},{8,12},{12,8},{1,5},{5,1},{9,13},{13,9},{2,6},{6,2},{1... | collective-permute-start | bytes 602120 | tf_op jit(solution)/shard_map/ppermute | solution.py:33
  42.5 21.1 %collective-permute-start.13 = (bf16[112,896]{1,0:T(8,128)(2,1)S(1)}, bf16[112,896]{1,0:T(8,128)(2,1)S(1)}, u32[]{:S(2)}, u32[]{:S(2)}) collective-permute-start(bf16[112,896]{1,0:T(8,128)(2,1)S(1)} %collective-permute-done.5), channel_id=1, source_target_pairs={{0,8},{4,12},{8,0},{12,4},{1,9},{5,13},{9,1},{13,5},{2,10},{6,14},... | collective-permute-start | bytes 602120 | tf_op jit(solution)/shard_map/ppermute | solution.py:33
  44.0 19.6 %collective-permute-start.14 = (bf16[112,896]{1,0:T(8,128)(2,1)S(1)}, bf16[112,896]{1,0:T(8,128)(2,1)S(1)}, u32[]{:S(2)}, u32[]{:S(2)}) collective-permute-start(bf16[112,896]{1,0:T(8,128)(2,1)S(1)} %collective-permute-done.5), channel_id=1, source_target_pairs={{0,12},{4,8},{8,4},{12,0},{1,13},{5,9},{9,5},{13,1},{2,14},{6,10},... | collective-permute-start | bytes 602120 | tf_op jit(solution)/shard_map/ppermute | solution.py:33
  44.5 12.5 %collective-permute-start.10 = (bf16[112,896]{1,0:T(8,128)(2,1)S(1)}, bf16[112,896]{1,0:T(8,128)(2,1)S(1)}, u32[]{:S(2)}, u32[]{:S(2)}) collective-permute-start(bf16[112,896]{1,0:T(8,128)(2,1)S(1)} %slice_bitcast_fusion.3), channel_id=1, source_target_pairs={{0,4},{4,0},{8,12},{12,8},{1,5},{5,1},{9,13},{13,9},{2,6},{6,2},{1... | collective-permute-start | bytes 602120 | tf_op jit(solution)/shard_map/ppermute | solution.py:33
  57.0 6.6 %collective-permute-start.11 = (bf16[112,896]{1,0:T(8,128)(2,1)S(1)}, bf16[112,896]{1,0:T(8,128)(2,1)S(1)}, u32[]{:S(2)}, u32[]{:S(2)}) collective-permute-start(bf16[112,896]{1,0:T(8,128)(2,1)S(1)} %slice_bitcast_fusion.2), channel_id=1, source_target_pairs={{0,8},{4,12},{8,0},{12,4},{1,9},{5,13},{9,1},{13,5},{2,10},{6,14},... | collective-permute-start | bytes 602120 | tf_op jit(solution)/shard_map/ppermute | solution.py:33
  63.6 2.8 %copy-start.3 = (bf16[7,112,896]{2,1,0:T(8,128)(2,1)}, bf16[7,112,896]{2,1,0:T(8,128)(2,1)S(1)}, u32[]{:S(2)}) copy-start(bf16[7,112,896]{2,1,0:T(8,128)(2,1)S(1)} %collective-permute-done.9.refs_3_) | copy-start | bytes 4214788
  63.8 2.7 %copy-start.2 = (bf16[5,112,896]{2,1,0:T(8,128)(2,1)}, bf16[5,112,896]{2,1,0:T(8,128)(2,1)S(1)}, u32[]{:S(2)}) copy-start(bf16[5,112,896]{2,1,0:T(8,128)(2,1)S(1)} %bitcast_dynamic-update-slice_fusion.refs_2_) | copy-start | bytes 3010564
  63.8 2.7 %collective-permute-start.15 = (bf16[5,112,896]{2,1,0:T(8,128)(2,1)S(1)}, bf16[5,112,896]{2,1,0:T(8,128)(2,1)S(1)}, u32[]{:S(2)}, u32[]{:S(2)}) collective-permute-start(bf16[5,112,896]{2,1,0:T(8,128)(2,1)S(1)} %bitcast_dynamic-update-slice_fusion.refs_2_), channel_id=1, source_target_pairs={{0,16},{16,0},{1,17},{17,1},{2,18},{18,2},{3,19},{19,3},{4,20},{20... | collective-permute-start | bytes 3010568 | tf_op jit(solution)/shard_map/ppermute | solution.py:33
  66.5 1.0 copy-start.4
  177.9 3.4 %collective-permute-start.16 = (bf16[4,104,1552]{2,1,0:T(8,128)(2,1)}, bf16[4,104,1552]{2,1,0:T(8,128)(2,1)S(1)}, u32[]{:S(2)}, u32[]{:S(2)}) collective-permute-start(bf16[4,104,1552]{2,1,0:T(8,128)(2,1)} %get-tuple-element.60), channel_id=1, source_target_pairs={{0,16},{16,0},{1,17},{17,1},{2,18},{18,2},{3,19},{19,3},{4,20},{20... | collective-permute-start | bytes 3873800 | tf_op jit(solution)/shard_map/ppermute | solution.py:33
  184.4 21.3 %all-to-all-start = ((bf16[4,104,1552]{2,1,0:T(8,128)(2,1)}), bf16[4,104,1552]{2,1,0:T(8,128)(2,1)S(1)}, u32[]{:S(2)}, u32[]{:S(2)}) async-start(bf16[4,104,1552]{2,1,0:T(8,128)(2,1)} %add_convert_fusion), calls=%async_computation | async-start | bytes 2768896 | tf_op jit(solution)/shard_map/all_to_all | solution.py:597
  207.2 27.8 %all-to-all-start.1 = ((bf16[4,104,1552]{2,1,0:T(8,128)(2,1)}), bf16[4,104,1552]{2,1,0:T(8,128)(2,1)S(1)}, u32[]{:S(2)}, u32[]{:S(2)}) async-start(bf16[4,104,1552]{2,1,0:T(8,128)(2,1)} %broadcast_in_dim.27), calls=%async_computation.1 | async-start | bytes 2768896 | tf_op jit(solution)/shard_map/all_to_all | solution.py:607
  210.7 1.7 collective-permute-start.17
  215.6 12.0 %collective-permute-start.18 = (f32[2,2]{1,0:T(2,128)S(1)}, f32[2,2]{1,0:T(2,128)S(1)}, u32[]{:S(2)}, u32[]{:S(2)}) collective-permute-start(f32[2,2]{1,0:T(2,128)S(1)} %reshape.47), channel_id=1, source_target_pairs={{0,4},{4,0},{8,12},{12,8},{1,5},{5,1},{9,13},{13,9},{2,6},{6,2},{1... | collective-permute-start | bytes 56 | tf_op jit(solution)/shard_map/ppermute | solution.py:33
  217.5 10.1 %collective-permute-start.19 = (f32[2,2]{1,0:T(2,128)S(1)}, f32[2,2]{1,0:T(2,128)S(1)}, u32[]{:S(2)}, u32[]{:S(2)}) collective-permute-start(f32[2,2]{1,0:T(2,128)S(1)} %reshape.47), channel_id=1, source_target_pairs={{0,8},{4,12},{8,0},{12,4},{1,9},{5,13},{9,1},{13,5},{2,10},{6,14},... | collective-permute-start | bytes 56 | tf_op jit(solution)/shard_map/ppermute | solution.py:33
  218.9 9.5 %collective-permute-start.20 = (f32[2,2]{1,0:T(2,128)S(1)}, f32[2,2]{1,0:T(2,128)S(1)}, u32[]{:S(2)}, u32[]{:S(2)}) collective-permute-start(f32[2,2]{1,0:T(2,128)S(1)} %reshape.47), channel_id=1, source_target_pairs={{0,12},{4,8},{8,4},{12,0},{1,13},{5,9},{9,5},{13,1},{2,14},{6,10},... | collective-permute-start | bytes 56 | tf_op jit(solution)/shard_map/ppermute | solution.py:33
  228.5 4.4 %collective-permute-start.21 = (f32[2,2]{1,0:T(2,128)S(1)}, f32[2,2]{1,0:T(2,128)S(1)}, u32[]{:S(2)}, u32[]{:S(2)}) collective-permute-start(f32[2,2]{1,0:T(2,128)S(1)} %add_add_fusion.1), channel_id=1, source_target_pairs={{0,1},{1,0},{2,3},{3,2},{4,5},{5,4},{6,7},{7,6},{8,9},{9,8},{10,11... | collective-permute-start | bytes 56 | tf_op jit(solution)/shard_map/ppermute | solution.py:33
  228.9 4.5 %collective-permute-start.22 = (f32[2,2]{1,0:T(2,128)S(1)}, f32[2,2]{1,0:T(2,128)S(1)}, u32[]{:S(2)}, u32[]{:S(2)}) collective-permute-start(f32[2,2]{1,0:T(2,128)S(1)} %add_add_fusion.1), channel_id=1, source_target_pairs={{0,2},{1,3},{2,0},{3,1},{4,6},{5,7},{6,4},{7,5},{8,10},{9,11},{10,... | collective-permute-start | bytes 56 | tf_op jit(solution)/shard_map/ppermute | solution.py:33
  229.0 5.4 %collective-permute-start.23 = (f32[2,2]{1,0:T(2,128)S(1)}, f32[2,2]{1,0:T(2,128)S(1)}, u32[]{:S(2)}, u32[]{:S(2)}) collective-permute-start(f32[2,2]{1,0:T(2,128)S(1)} %add_add_fusion.1), channel_id=1, source_target_pairs={{0,3},{1,2},{2,1},{3,0},{4,7},{5,6},{6,5},{7,4},{8,11},{9,10},{10,... | collective-permute-start | bytes 56 | tf_op jit(solution)/shard_map/ppermute | solution.py:33
where the time goes:
time: 239 us; the launch traced here: 238 us
  Pallas kernels  122 us (51%)
  waiting for transfers between devices  45 us (19%)
  starting transfers between devices  34.7 us (15%)
  local copies, waits for them, and re-layouts  13.6 us (6%)
  other arithmetic  11.9 us (5%)
  matrix products  9.77 us (4%)
    pallas_call x1, Pallas kernels, local(): pl.pallas_call(functools.partial(forward_kernel, cols, plan, sub, pieced)...  51.5 us
    ppermute x24, waiting for transfers between devices, flip(): return lax.ppermute(block, axis, [(at, at ^ bit) for at in range(count)])  40.4 us
    pallas_call x1, Pallas kernels, local(): pl.pallas_call(functools.partial(backward_kernel, cols, own), grid_spec=p...  35 us
    ppermute x24, starting transfers between devices, flip(): return lax.ppermute(block, axis, [(at, at ^ bit) for at in range(count)])  27.5 us
    pallas_call x1, Pallas kernels, local(): pl.pallas_call(weight_kernel, grid_spec=pltpu.PrefetchScalarGridSpec(num_...  21.8 us
    pallas_call x1, Pallas kernels, local(): pl.pallas_call(functools.partial(drop_kernel, width_in), grid=(blocks,),...  10.3 us
    dot_general x1, matrix products, local(): jnp.einsum('tsr,rk->tsk', own_seqs, w_in, preferred_element_type=F32)  9.77 us
  transfers between devices with their start and end apart: 26, of which 12 were waited for; matrix products, arithmetic and copies ran while one was open for 9% of the time, Pallas kernels for 4%

commit v1 on v0

--- a/solution.py
+++ b/solution.py
@@ -90,37 +90,61 @@
         drop_ref[k, :, width:] = jnp.ones_like(drop_ref[k, :, width:])
 
 
+def turned_dot(left, right):
+    return lax.dot_general(left, right, (((1,), (1,)), ((), ())), preferred_element_type=F32)
+
+
+def identity(size):
+    line = lax.broadcasted_iota(jnp.int32, (size, size), 0)
+    same = line == lax.broadcasted_iota(jnp.int32, (size, size), 1)
+    return same.astype(F32).astype(BF16)
+
+
 def shard_kernel(plan, at_ref, in_ref, rec_ref, mask_ref, bias_ref, own_ref, *mine_ref):
-    width = in_ref.shape[1]
+    rows, width = in_ref.shape
     hidden = rec_ref.shape[1]
     bias = bias_ref[...]
     high = bias.astype(BF16)
+    pair = jnp.concatenate([high, (bias - high.astype(F32)).astype(BF16)], 0)
     scale = mask_ref[...].astype(F32) / KEEP_WEIGHT
     own_ref[:, :width] = in_ref[...]
-    own_ref[:, width : width + 1] = high
-    own_ref[:, width + 1 : width + 2] = (bias - high.astype(F32)).astype(BF16)
+    own_ref[:, width : width + 2] = turned_dot(identity(rows), pair).astype(BF16)
     own_ref[:, plan.wide : plan.wide + hidden] = (rec_ref[...].astype(F32) * scale).astype(BF16)
     own_ref[:, plan.wide + hidden :] = jnp.zeros_like(own_ref[:, plan.wide + hidden :])
     for ref in mine_ref:
-        ref[...] = own_ref[plan.window(at_ref[1], at_ref[2])]
+        ref[...] = own_ref[plan.window(at_ref[1], at_ref[2], 0, plan.rows)]
 
 
 class Plan:
     def __init__(self, hidden, wide):
-        self.hidden = hidden
         self.wide = wide
         self.columns = ceil_to(wide + hidden, LANES)
-        self.row_step = hidden // 4 // 16 * 16
-        self.rows = hidden - 3 * self.row_step
-        tiles = self.columns // LANES
-        self.column_step = tiles // 2 * LANES
+        self.row_step = hidden // 32 * 16
+        self.rows = hidden - self.row_step
+        self.first = ceil_to(self.rows // 2, 16)
+        self.column_step = self.columns // LANES // 2 * LANES
         self.cut = self.columns - self.column_step
 
-    def window(self, seq_at, grp_at):
+    def window(self, seq_at, grp_at, start, count):
+        half = (seq_at ^ (seq_at >> 1)) & 1
         return (
-            pl.ds(pl.multiple_of(seq_at * self.row_step, 16), self.rows),
+            pl.ds(pl.multiple_of(half * self.row_step + start, 16), count),
             pl.ds(pl.multiple_of(grp_at * self.column_step, LANES), self.cut),
         )
+
+    def places(self):
+        first, rest = self.first, self.rows - self.first
+        return [
+            (0, 1, 0, 0, self.rows),
+            (0, 2, 0, 0, self.rows),
+            (0, 1, 1, 0, first),
+            (0, 2, 1, 0, first),
+            (0, 1, 1, first, rest),
+            (0, 2, 1, first, rest),
+            (0, 3, 0, 0, self.rows),
+            (1, 3, 1, 0, first),
+            (1, 3, 1, first, rest),
+        ]
 
 
 def forward_kernel(cols, plan, sub, pieced, at_ref, first_ref, second_ref, third_ref, *refs):
@@ -141,25 +165,23 @@
                     parts.append(rows_ref[q, unit : unit + high - low, first:last])
         return jnp.concatenate(parts, 0)
 
-    def turned_dot(left, right):
-        return lax.dot_general(left, right, (((1,), (1,)), ((), ())), preferred_element_type=F32)
-
     @pl.when(pl.program_id(0) == 0)
     def _():
         if pieced:
             row_at, seq_at, grp_at = at_ref[0], at_ref[1], at_ref[2]
             w_ref[row_at] = sources[0][...]
-            for (m, k), (batch, index) in PIECE_AT.items():
-                for gi in range(2):
-                    window = plan.window(seq_at ^ m, grp_at ^ gi)
-                    w_ref[(row_at ^ k,) + window] = sources[1 + 2 * gi + batch][index]
+            for gi in range(2):
+                line = [0, 0]
+                for array, k, m, start, size in plan.places():
+                    window = plan.window(seq_at ^ m, grp_at ^ gi, start, size)
+                    piece = sources[1 + 2 * gi + array][line[array] : line[array] + size]
+                    w_ref[(row_at ^ k,) + window] = piece
+                    line[array] += size
         else:
             w_ref[...] = sources[0][...]
         rec_ref[...] = w_ref[:, :, width : width + hidden]
-        line = lax.broadcasted_iota(jnp.int32, (hidden, hidden), 0)
-        same = line == lax.broadcasted_iota(jnp.int32, (hidden, hidden), 1)
         turned[...] = turned_dot(
-            same.astype(F32).astype(BF16), columns_of(rec_ref, 0, cols.total, 0, hidden)
+            identity(hidden), columns_of(rec_ref, 0, cols.total, 0, hidden)
         ).astype(BF16)
         cell_s[...] = jnp.zeros_like(cell_s)
         low_s[...] = jnp.zeros_like(low_s)
@@ -308,9 +330,9 @@
         smooth_s[:, a:b] = smooth_next[j]
 
 
-def weight_kernel(grp_ref, rows_ref, drop_ref, prev_ref, pick_ref, scale_ref, keep_ref, send_ref, sums):
+def weight_kernel(data_n, grp_ref, rows_ref, pick_ref, *refs):
+    data, scale, (keep_ref, send_ref, sums) = refs[:data_n], refs[data_n:-3], refs[-3:]
     steps, seqs, own = rows_ref.shape
-    width = drop_ref.shape[2]
     place = pl.program_id(0)
 
     @pl.when(place == 0)
@@ -320,21 +342,23 @@
     grads = rows_ref[...]
     first = (grads * pick_ref[...][None]).reshape(steps * seqs, own)
     second = grads.reshape(steps * seqs, own) - first
-    drop = drop_ref[...].reshape(steps * seqs, width)
-    prev = prev_ref[...].reshape(steps * seqs, prev_ref.shape[2])
-    for at, part in enumerate((first, second)):
-        sums[at, :own, :width] += lax.dot_general(
-            part, drop, OVER_ROWS, preferred_element_type=F32
-        )
-        sums[at, :own, width:] += lax.dot_general(
-            part, prev, OVER_ROWS, preferred_element_type=F32
-        )
+    start = 0
+    for ref in data:
+        width = ref.shape[2]
+        values = ref[...].reshape(steps * seqs, width)
+        for at, part in enumerate((first, second)):
+            sums[at, :own, start : start + width] += lax.dot_general(
+                part, values, OVER_ROWS, preferred_element_type=F32
+            )
+        start += width
 
     @pl.when(place == pl.num_programs(0) - 1)
     def _():
         rows = keep_ref.shape[1]
-        for at in range(2):
-            sums[at, :own, width:] = sums[at, :own, width:] * scale_ref[...]
+        for ref in scale:
+            for at in range(2):
+                part = (at, slice(0, own), slice(start - width, start))
+                sums[part] = sums[part] * ref[...]
         for part in range(keep_ref.shape[0]):
             span = slice(part * rows, (part + 1) * rows)
             keep_ref[part] = sums[grp_ref[0], span]
@@ -351,40 +375,32 @@
     return pl.BlockSpec(shape, lambda *_: (0,) * len(shape))
 
 
-def gather_pieces(mine, counts, beside):
+def gather_pieces(plan, mine, counts, beside):
     hold = lax.optimization_barrier
+    cut = plan.cut
     one, two, beside, counts = hold(
         (flip(mine, "row", 1), flip(mine, "row", 2), beside, counts + flip(counts, "grp", 1))
     )
     near = jnp.stack([one, two])
-    near_one, near_two, three, *others = hold(
-        [flip(near, "seq", 1), flip(near, "seq", 2), flip(two, "row", 1)]
-        + [flip(counts, "seq", bit) for bit in range(1, 4)]
-    )
-    counts = (counts + others[0]) + (others[1] + others[2])
-    early = jnp.concatenate([near, near_one, near_two, three[None]], 0)
-    across, diag_one, diag_two, *last = hold(
-        [flip(early, "grp", 1), flip(near_two[0], "seq", 1), flip(near_one[1], "seq", 2)]
-        + [flip(three, "seq", bit) for bit in range(1, 4)]
-    )
-    late = jnp.stack([diag_one, diag_two] + last)
-    return early, late, across, flip(late, "grp", 1), counts, beside
-
-
-PIECE_AT = {
-    (0, 1): (0, 0),
-    (0, 2): (0, 1),
-    (1, 1): (0, 2),
-    (1, 2): (0, 3),
-    (2, 1): (0, 4),
-    (2, 2): (0, 5),
-    (0, 3): (0, 6),
-    (3, 1): (1, 0),
-    (3, 2): (1, 1),
-    (1, 3): (1, 2),
-    (2, 3): (1, 3),
-    (3, 3): (1, 4),
-}
+    near_x, near_y, three, counts = hold(
+        (
+            flip(near[:, : plan.first], "seq", 1),
+            flip(near[:, plan.first :], "seq", 2),
+            flip(two, "row", 1),
+            counts + flip(counts, "seq", 1),
+        )
+    )
+    early = jnp.concatenate([part.reshape(-1, cut) for part in (near, near_x, near_y, three)], 0)
+    last_x, last_y, early_other, counts = hold(
+        (
+            flip(three[: plan.first], "seq", 1),
+            flip(three[plan.first :], "seq", 2),
+            flip(early, "grp", 1),
+            counts + flip(counts, "seq", 2),
+        )
+    )
+    late = jnp.concatenate([last_x, last_y], 0)
+    return early, late, early_other, flip(late, "grp", 1), counts, beside
 
 
 def local(
@@ -424,7 +440,7 @@
                 fixed(row_count, width_in),
                 fixed(row_count, hidden),
                 fixed(row_count, hidden),
-                fixed(row_count, 1),
+                fixed(1, row_count),
             ],
             out_specs=[fixed(row_count, plan.columns)] + [fixed(plan.rows, plan.cut)] * pieced,
         ),
@@ -432,7 +448,7 @@
         + [jax.ShapeDtypeStruct((plan.rows, plan.cut), BF16)] * pieced,
         compiler_params=params(),
         name="shard",
-    )(at, input_gate_weight, w_recur, weight_mask, bias[:, None])
+    )(at, input_gate_weight, w_recur, weight_mask, bias[None])
     sub = max(s for s in range(1, 8) if time_steps % (2 * s) == 0)
     steps = 2 * sub
     blocks = time_steps // steps
@@ -456,7 +472,7 @@
     valid_count = jnp.clip(lengths, 0, time_steps).astype(F32)
     counts = jnp.sum(group_hot * valid_count[:, None], 0)
     if pieced:
-        *pieces, counts, dropped = gather_pieces(mine[0], counts, dropped)
+        *pieces, counts, dropped = gather_pieces(plan, mine[0], counts, dropped)
         sources = [own_weights] + pieces
     else:
         counts = lax.psum(counts, ("grp", "seq"))
@@ -568,45 +584,45 @@
             cols.unpack_lanes(grads), row_at * row_count, row_count, 2
         )
     pick = jnp.broadcast_to((groups == 0).astype(BF16)[:, None], (seq_count, row_count))
-    columns = wide + hidden
     part_rows = ceil_to(-(-row_count // seq_n), 8)
-    keep, send = pl.pallas_call(
-        weight_kernel,
-        grid_spec=pltpu.PrefetchScalarGridSpec(
-            num_scalar_prefetch=1,
-            grid=(blocks,),
-            in_specs=[
-                at_time(row_count),
-                at_time(wide),
-                at_time(hidden),
-                fixed(seq_count, row_count),
-                fixed(row_count, hidden),
+    def weight_sums(rows, data, specs, scale):
+        columns = sum(spec.block_shape[2] for spec in specs)
+        return pl.pallas_call(
+            functools.partial(weight_kernel, len(data)),
+            grid_spec=pltpu.PrefetchScalarGridSpec(
+                num_scalar_prefetch=1,
+                grid=(blocks,),
+                in_specs=[at_time(row_count), fixed(seq_count, row_count)]
+                + specs
+                + [fixed(*part.shape) for part in scale],
+                out_specs=[fixed(seq_n, part_rows, columns)] * 2,
+                scratch_shapes=[pltpu.VMEM((2, seq_n * part_rows, columns), F32)],
+            ),
+            out_shape=[
+                jax.ShapeDtypeStruct((seq_n, part_rows, columns), F32),
+                jax.ShapeDtypeStruct((seq_n, part_rows, columns), BF16),
             ],
-            out_specs=[fixed(seq_n, part_rows, columns)] * 2,
-            scratch_shapes=[pltpu.VMEM((2, seq_n * part_rows, columns), F32)],
-        ),
-        out_shape=[
-            jax.ShapeDtypeStruct((seq_n, part_rows, columns), F32),
-            jax.ShapeDtypeStruct((seq_n, part_rows, columns), BF16),
-        ],
-        compiler_params=params(),
-        name="weights",
-    )(grp_at[None], own_rows, dropped, prev_low, pick, w_scale)
-
-    both = (keep + flip(send, "grp", 1).astype(F32)).astype(BF16)
-    swapped = lax.all_to_all(both, "seq", 0, 0, tiled=True)
+            compiler_params=params(),
+            name="weights",
+        )(grp_at[None], rows, pick, *data, *scale)
+
+    hold = lax.optimization_barrier
+    keep, send = weight_sums(
+        own_rows, [dropped, prev_low], [at_time(wide), at_time(hidden)], [w_scale]
+    )
+    block = (keep + flip(send, "grp", 1).astype(F32)).astype(BF16)
+    swapped = lax.all_to_all(block, "seq", 0, 0, tiled=True)
 
     own_seqs = lax.dynamic_slice_in_dim(grads, row_at * share, share, 1)
     own_scale = lax.dynamic_slice_in_dim(in_scale, row_at * share, share, 0)
     w_in = cols.pack(weights[:, :, :width_in])
     input_time = jnp.einsum("tsr,rk->tsk", own_seqs, w_in, preferred_element_type=F32)
     input_grad = jnp.swapaxes(input_time * own_scale[None], 0, 1)
-    swapped, input_grad = lax.optimization_barrier((swapped, input_grad))
+    swapped, input_grad = hold((swapped, input_grad))
 
     total = jnp.sum(swapped.astype(F32), 0).astype(BF16)
-    everyone = lax.all_to_all(
-        jnp.broadcast_to(total[None], (seq_n, part_rows, columns)), "seq", 0, 0, tiled=True
-    )
+    copies = jnp.broadcast_to(total[None], (seq_n,) + total.shape)
+    parts = lax.all_to_all(copies, "seq", 0, 0, tiled=True)
     peer = flip(total, "grp", 1)
     ours, theirs = (
         jnp.concatenate([part[:, : width_in + 1], part[:, wide:]], 1).astype(F32)
@@ -616,10 +632,9 @@
     second = jnp.where(grp_at == 0, theirs, ours)
     dots = [jnp.sum(a * b) for a, b in ((first, first), (first, second), (second, second))]
     gram = jnp.stack([dots[0], dots[1], dots[1], dots[2]]).reshape(2, 2)
-    gram = exchange_sum(exchange_sum(gram, "seq"), "row")
-    everyone, gram = lax.optimization_barrier((everyone, gram))
-    everyone = everyone.reshape(seq_n * part_rows, columns)[:row_count].astype(F32)
-
+    gram = exchange_sum(exchange_sum(gram, "row"), "seq")
+    parts, gram = hold((parts, gram))
+    everyone = parts.reshape(seq_n * part_rows, wide + hidden)[:row_count].astype(F32)
     return (
         input_grad,
         everyone[None, :, :width_in],

time: 239 us -> 220 us (0.921)
  waiting for transfers between devices: 45 us -> 29.6 us
  starting transfers between devices: 34.7 us -> 29.1 us
  other arithmetic: 11.9 us -> 14.5 us
    ppermute x24 -> x20, waiting for transfers between devices: 40.4 us -> 24.7 us  [flip(): return lax.ppermute(block, axis, [(at, at ^ bit) for at in range(count)])]
    ppermute x24 -> x20, starting transfers between devices: 27.5 us -> 22 us  [flip(): return lax.ppermute(block, axis, [(at, at ^ bit) for at in range(count)])]
  transfers between devices with their start and end apart: 26 -> 22, of which waited for: 12 -> 12; matrix products, arithmetic and copies ran while one was open for 9% -> 11% of each run, Pallas kernels for 4% -> 5%
where the time goes in v1:
time: 220 us; the launch traced here: 219 us
  Pallas kernels  122 us (55%)
  waiting for transfers between devices  29.6 us (13%)
  starting transfers between devices  29.1 us (13%)
  other arithmetic  14.5 us (7%)
  local copies, waits for them, and re-layouts  12.8 us (6%)
  matrix products  9.77 us (4%)
    pallas_call x1, Pallas kernels, local(): pl.pallas_call(functools.partial(forward_kernel, cols, plan, sub, pieced)...  51.5 us
    pallas_call x1, Pallas kernels, local(): pl.pallas_call(functools.partial(backward_kernel, cols, own), grid_spec=p...  35 us
    ppermute x20, waiting for transfers between devices, flip(): return lax.ppermute(block, axis, [(at, at ^ bit) for at in range(count)])  24.7 us
    ppermute x20, starting transfers between devices, flip(): return lax.ppermute(block, axis, [(at, at ^ bit) for at in range(count)])  22 us
    pallas_call x1, Pallas kernels, weight_sums(): pl.pallas_call(functools.partial(weight_kernel, len(data)), grid_spec=plt...  21.8 us
    pallas_call x1, Pallas kernels, local(): pl.pallas_call(functools.partial(drop_kernel, width_in), grid=(blocks,),...  10.3 us
    dot_general x1, matrix products, local(): jnp.einsum('tsr,rk->tsk', own_seqs, w_in, preferred_element_type=F32)  9.77 us
    all_to_all x1, waiting for transfers between devices, local(): swapped = lax.all_to_all(block, 'seq', 0, 0, tiled=True)  4.94 us
  transfers between devices with their start and end apart: 22, of which 12 were waited for; matrix products, arithmetic and copies ran while one was open for 11% of the time, Pallas kernels for 5%

profile of v1, /device:TPU:0, one launch (start us, length us, event | category | flops | bytes accessed | tf_op | source)
XLA Modules:
  0.0 219.1 jit_solution(4337771344641932974)
XLA Ops:
  0.6 0.6 pad_add_fusion.at_ref
  1.3 3.9 %shard.1 = (bf16[400,1664]{1,0:T(8,128)(2,1)}, bf16[208,896]{1,0:T(8,128)(2,1)}) custom-call(s32[3]{0:T(128)} %pad_add_fusion.at_ref, bf16[400,1150]{1,0:T(8,128)(2,1)} %in_ref.1, bf16[400,400]{1,0:T(8,128)(2,1)} %rec_ref.1, s32[400,400]{1,0:T(8,128)} %mask_ref.1, f32[1,400]{1,0:T(1,128)} %bitcast.46), custom_call_target="tpu_custom_call" | custom-call | tf_op jit(solution)/shard_map/shard/pallas_call | solution.py:434
  5.2 3.0 %collective-permute-start = (bf16[208,896]{1,0:T(8,128)(2,1)}, bf16[208,896]{1,0:T(8,128)(2,1)S(1)}, u32[]{:S(2)}, u32[]{:S(2)}) collective-permute-start(bf16[208,896]{1,0:T(8,128)(2,1)} %get-tuple-element.32), channel_id=1, source_target_pairs={{0,1},{1,0},{2,3},{3,2},{4,5},{5,4},{6,7},{7,6},{8,9},{9,8},{10,11... | collective-permute-start | bytes 1118216 | tf_op jit(solution)/shard_map/ppermute | solution.py:33
  8.2 2.6 %collective-permute-start.1 = (bf16[208,896]{1,0:T(8,128)(2,1)}, bf16[208,896]{1,0:T(8,128)(2,1)S(1)}, u32[]{:S(2)}, u32[]{:S(2)}) collective-permute-start(bf16[208,896]{1,0:T(8,128)(2,1)} %get-tuple-element.32), channel_id=1, source_target_pairs={{0,2},{1,3},{2,0},{3,1},{4,6},{5,7},{6,4},{7,5},{8,10},{9,11},{10,... | collective-permute-start | bytes 1118216 | tf_op jit(solution)/shard_map/ppermute | solution.py:33
  10.8 0.7 clamp_convert_fusion
  11.5 0.8 select_reduce_fusion.1
  12.3 1.7 convert_multiply_fusion.1.scale_ref
  14.0 10.3 %drop.1.first_ref.second_ref.third_ref.refs_0_ = bf16[70,64,1152]{2,1,0:T(8,128)(2,1)} custom-call(bf16[70,64,1150]{2,1,0:T(8,128)(2,1)} %bitcast.29, f32[64,1150]{1,0:T(8,128)} %convert_multiply_fusion.1.scale_ref), custom_call_target="tpu_custom_call" | custom-call | tf_op jit(solution)/shard_map/drop/pallas_call | solution.py:460
  24.3 0.6 collective-permute-done
  24.9 2.5 %collective-permute-done.1 = bf16[208,896]{1,0:T(8,128)(2,1)S(1)} collective-permute-done((bf16[208,896]{1,0:T(8,128)(2,1)}, bf16[208,896]{1,0:T(8,128)(2,1)S(1)}, u32[]{:S(2)}, u32[]{:S(2)}) %collective-permute-start.1) | collective-permute-done | bytes 372768 | tf_op jit(solution)/shard_map/ppermute | solution.py:33
  27.5 0.4 collective-permute-start.5
  28.0 1.6 collective-permute-start.3
  29.6 1.6 collective-permute-start.4
  31.2 0.5 collective-permute-start.6
  31.8 6.1 %collective-permute-done.6 = f32[2]{0:T(128)S(1)} collective-permute-done((f32[2]{0:T(128)S(1)}, f32[2]{0:T(128)S(1)}, u32[]{:S(2)}, u32[]{:S(2)}) %collective-permute-start.6) | collective-permute-done | bytes 40 | tf_op jit(solution)/shard_map/ppermute | solution.py:33
  38.0 0.2 pad_maximum_fusion.refs_1_
  38.3 1.1 convert_multiply_fusion.refs_2_
  39.4 1.5 collective-permute-start.7
  41.0 1.5 collective-permute-start.8
  42.5 0.5 collective-permute-start.10
  43.0 4.4 %collective-permute-done.10 = f32[2]{0:T(128)S(1)} collective-permute-done((f32[2]{0:T(128)S(1)}, f32[2]{0:T(128)S(1)}, u32[]{:S(2)}, u32[]{:S(2)}) %collective-permute-start.10) | collective-permute-done | bytes 40 | tf_op jit(solution)/shard_map/ppermute | solution.py:33
  47.4 1.2 copy-done.2
  48.8 0.6 reduce_sum.67
  49.4 0.6 broadcast_divide_fusion
  50.0 0.1 select_reduce_fusion
  50.1 0.7 multiply_multiply_fusion
  50.9 0.7 copy-done.4
  51.6 51.5 %forward.1 = (f32[70,64,1600]{2,1,0:T(8,128)}, f32[70,64,400]{2,1,0:T(8,128)}, bf16[70,64,400]{2,1,0:T(8,128)(2,1)}, bf16[4,400,1664]{2,1,0:T(8,128)(2,1)}, bf16[4,400,400]{2,1,0:T(8,128)(2,1)}) custom-call(s32[3]{0:T(128)} %pad_add_fusion.at_ref, bf16[70,64,1152]{2,1,0:T(8,128)(2,1)} %drop.1.first_ref.second_ref.third_ref.refs_0_, ...), custom_call_target="tpu_custom_call" | custom-call | tf_op jit(solution)/shard_map/forward/pallas_call | solution.py:488
  103.1 0.7 broadcast_in_dim.21.smooth_ref
  103.8 0.7 broadcast_in_dim.22.length_ref
  104.5 35.0 %backward.1 = (bf16[70,64,1600]{2,1,0:T(8,128)(2,1)}, bf16[70,64,400]{2,1,0:T(8,128)(2,1)}) custom-call(s32[1]{0:T(128)} %bitcast.1.row_ref, f32[70,64,1600]{2,1,0:T(8,128)} %get-tuple-element.45.act_ref.act_before_ref, f32[70,64,400]{2,1,0:T(8,128)} %get-tuple-element.46.cell_ref.before_ref, f32[70,64,400]{2,1,0:T(8,128)} %get-tuple-element.46.cell_ref.before_ref, ...), custom_call_target="tpu_custom_call" | custom-call | tf_op jit(solution)/shard_map/backward/pallas_call | solution.py:541
  139.6 0.7 broadcast_in_dim.23.pick_ref
  140.3 21.8 %weights.1 = (f32[4,104,1552]{2,1,0:T(8,128)}, bf16[4,104,1552]{2,1,0:T(8,128)(2,1)}) custom-call(s32[1]{0:T(128)} %bitcast.grp_ref, bf16[70,64,400]{2,1,0:T(8,128)(2,1)} %get-tuple-element.49.rows_ref, bf16[64,400]{1,0:T(8,128)(2,1)} %broadcast_in_dim.23.pick_ref, bf16[70,64,1152]{2,1,0:T(8,128)(2,1)} %drop.1.first_ref.second_ref.third_ref.refs_0_, ...), custom_call_target="tpu_custom_call" | custom-call | tf_op jit(solution)/shard_map/weights/pallas_call | solution.py:590
  162.1 0.5 collective-permute-start.12
  162.6 0.9 constant_dynamic-slice_fusion
  163.5 2.1 collective-permute-done.12
  165.5 3.2 %add_convert_fusion = bf16[4,104,1552]{2,1,0:T(8,128)(2,1)} fusion(f32[4,104,1552]{2,1,0:T(8,128)} %get-tuple-element.51, bf16[4,104,1552]{2,1,0:T(8,128)(2,1)S(1)} %collective-permute-done.12), kind=kLoop, calls=%fused_computation.9 | loop fusion | flops 1936896 | bytes 5165056 | tf_op jit(solution)/shard_map/convert_element_type | solution.py:613
  168.7 3.5 %all-to-all-start = ((bf16[4,104,1552]{2,1,0:T(8,128)(2,1)}), bf16[4,104,1552]{2,1,0:T(8,128)(2,1)S(1)}, u32[]{:S(2)}, u32[]{:S(2)}) async-start(bf16[4,104,1552]{2,1,0:T(8,128)(2,1)} %add_convert_fusion), calls=%async_computation | async-start | bytes 2768896 | tf_op jit(solution)/shard_map/all_to_all | solution.py:614
  172.3 2.4 %fusion.11 = (bf16[4,128,1150]{2,1,0:T(8,128)(2,1)S(1)}, bf16[4,128,1150]{2,1,0:T(8,128)(2,1)S(1)}, bf16[4,128,1150]{2,1,0:T(8,128)(2,1)S(1)}) fusion(bf16[4,400,1664]{2,1,0:T(8,128)(2,1)} %get-tuple-element.54), kind=kLoop, calls=%fused_computation.50 | loop fusion | bytes 7065600 | tf_op jit(solution)/shard_map/slice | solution.py:74
  174.6 0.9 slice.60
  175.6 9.8 %multiply_bitcast_fusion = f32[16,70,1150]{2,0,1:T(8,128)} fusion(bf16[70,64,1600]{2,1,0:T(8,128)(2,1)} %get-tuple-element.53, s32[]{:T(128)S(6)} %select_n.16, bf16[64,1150]{1,0:T(8,128)(2,1)S(1)} %bitcast.44, bf16[512,1150]{1,0:T(8,128)(2,1)S(1)} %bitcast.40, bf16[512,1150]{1,0:T(8,128)(2,1)S(1)} %bitcast.41, bf16[512,1150]{1,0:T(8,128)(2,1)S(1)} %bitcast.39, ...), kind=kOutput, calls=%fused_computation | convolution fusion | flops 4137607936 | bytes 12632964 | tf_op jit(solution)/shard_map/tsr,rk->tsk/dot_general | solution.py:619
  185.3 4.9 %all-to-all-done = bf16[4,104,1552]{2,1,0:T(8,128)(2,1)S(1)} async-done(((bf16[4,104,1552]{2,1,0:T(8,128)(2,1)}), bf16[4,104,1552]{2,1,0:T(8,128)(2,1)S(1)}, u32[]{:S(2)}, u32[]{:S(2)}) %all-to-all-start) | async-done | bytes 1291296 | tf_op jit(solution)/shard_map/all_to_all | solution.py:614
  190.3 0.2 reduce_sum.69
  190.5 1.2 broadcast_in_dim.24
  191.7 3.5 %all-to-all-start.1 = ((bf16[4,104,1552]{2,1,0:T(8,128)(2,1)}), bf16[4,104,1552]{2,1,0:T(8,128)(2,1)S(1)}, u32[]{:S(2)}, u32[]{:S(2)}) async-start(bf16[4,104,1552]{2,1,0:T(8,128)(2,1)} %broadcast_in_dim.24), calls=%async_computation.1 | async-start | bytes 2768896 | tf_op jit(solution)/shard_map/all_to_all | solution.py:625
  195.4 1.6 collective-permute-done.13
  197.0 1.0 multiply_reduce_fusion.2
  198.0 2.0 pad_maximum_fusion.4
  200.1 0.3 collective-permute-start.14
  200.4 1.6 collective-permute-start.15
  202.0 2.5 %collective-permute-start.16 = (f32[2,2]{1,0:T(2,128)S(1)}, f32[2,2]{1,0:T(2,128)S(1)}, u32[]{:S(2)}, u32[]{:S(2)}) collective-permute-start(f32[2,2]{1,0:T(2,128)S(1)} %reshape.59), channel_id=1, source_target_pairs={{0,3},{1,2},{2,1},{3,0},{4,7},{5,6},{6,5},{7,4},{8,11},{9,10},{10,... | collective-permute-start | bytes 56 | tf_op jit(solution)/shard_map/ppermute | solution.py:33
  204.5 0.3 collective-permute-done.15
  204.8 2.5 %collective-permute-done.16 = f32[2,2]{1,0:T(2,128)S(1)} collective-permute-done((f32[2,2]{1,0:T(2,128)S(1)}, f32[2,2]{1,0:T(2,128)S(1)}, u32[]{:S(2)}, u32[]{:S(2)}) %collective-permute-start.16) | collective-permute-done | bytes 48 | tf_op jit(solution)/shard_map/ppermute | solution.py:33
  207.4 1.9 collective-permute-start.17
  209.3 1.5 collective-permute-start.18
  210.8 0.1 collective-permute-start.19
  210.9 1.7 collective-permute-done.17
  212.5 0.3 collective-permute-done.18
  212.9 2.4 %collective-permute-done.19 = f32[2,2]{1,0:T(2,128)S(1)} collective-permute-done((f32[2,2]{1,0:T(2,128)S(1)}, f32[2,2]{1,0:T(2,128)S(1)}, u32[]{:S(2)}, u32[]{:S(2)}) %collective-permute-start.19) | collective-permute-done | bytes 48 | tf_op jit(solution)/shard_map/ppermute | solution.py:33
  215.2 0.6 add_add_fusion
  215.8 0.2 slice_convert_fusion
  216.0 1.4 slice_bitcast_fusion
  217.3 1.0 slice_bitcast_fusion.1
  218.3 0.8 slice_reduce_fusion
  (46 shorter events, 0.8 us)
Async XLA Ops:
  5.2 19.8 %collective-permute-start = (bf16[208,896]{1,0:T(8,128)(2,1)}, bf16[208,896]{1,0:T(8,128)(2,1)S(1)}, u32[]{:S(2)}, u32[]{:S(2)}) collective-permute-start(bf16[208,896]{1,0:T(8,128)(2,1)} %get-tuple-element.32), channel_id=1, source_target_pairs={{0,1},{1,0},{2,3},{3,2},{4,5},{5,4},{6,7},{7,6},{8,9},{9,8},{10,11... | collective-permute-start | bytes 1118216 | tf_op jit(solution)/shard_map/ppermute | solution.py:33
  8.2 19.3 %collective-permute-start.1 = (bf16[208,896]{1,0:T(8,128)(2,1)}, bf16[208,896]{1,0:T(8,128)(2,1)S(1)}, u32[]{:S(2)}, u32[]{:S(2)}) collective-permute-start(bf16[208,896]{1,0:T(8,128)(2,1)} %get-tuple-element.32), channel_id=1, source_target_pairs={{0,2},{1,3},{2,0},{3,1},{4,6},{5,7},{6,4},{7,5},{8,10},{9,11},{10,... | collective-permute-start | bytes 1118216 | tf_op jit(solution)/shard_map/ppermute | solution.py:33
  12.2 12.1 %collective-permute-start.2 = (f32[2]{0:T(128)S(1)}, f32[2]{0:T(128)S(1)}, u32[]{:S(2)}, u32[]{:S(2)}) collective-permute-start(f32[2]{0:T(128)S(1)} %select_reduce_fusion.1), channel_id=1, source_target_pairs={{0,16},{16,0},{1,17},{17,1},{2,18},{18,2},{3,19},{19,3},{4,20},{20... | collective-permute-start | bytes 32 | tf_op jit(solution)/shard_map/ppermute | solution.py:33
  27.5 10.5 %collective-permute-start.5 = (bf16[208,896]{1,0:T(8,128)(2,1)S(1)}, bf16[208,896]{1,0:T(8,128)(2,1)S(1)}, u32[]{:S(2)}, u32[]{:S(2)}) collective-permute-start(bf16[208,896]{1,0:T(8,128)(2,1)S(1)} %collective-permute-done.1), channel_id=1, source_target_pairs={{0,1},{1,0},{2,3},{3,2},{4,5},{5,4},{6,7},{7,6},{8,9},{9,8},{10,11... | collective-permute-start | bytes 1118216 | tf_op jit(solution)/shard_map/ppermute | solution.py:33
  28.0 10.0 %collective-permute-start.3 = (bf16[2,112,896]{2,1,0:T(8,128)(2,1)S(1)}, bf16[2,112,896]{2,1,0:T(8,128)(2,1)S(1)}, u32[]{:S(2)}, u32[]{:S(2)}) collective-permute-start(bf16[2,112,896]{2,1,0:T(8,128)(2,1)S(1)} %fusion.7), channel_id=1, source_target_pairs={{0,4},{4,0},{8,12},{12,8},{1,5},{5,1},{9,13},{13,9},{2,6},{6,2},{1... | collective-permute-start | bytes 1204232 | tf_op jit(solution)/shard_map/ppermute | solution.py:33
  29.6 8.7 %copy-start.1 = (s32[400,400]{1,0:T(8,128)S(1)}, s32[400,400]{1,0:T(8,128)}, u32[]{:S(2)}) copy-start(s32[400,400]{1,0:T(8,128)} %mask_ref.1) | copy-start | bytes 1920004
  29.6 8.4 %collective-permute-start.4 = (bf16[2,96,896]{2,1,0:T(8,128)(2,1)S(1)}, bf16[2,96,896]{2,1,0:T(8,128)(2,1)S(1)}, u32[]{:S(2)}, u32[]{:S(2)}) collective-permute-start(bf16[2,96,896]{2,1,0:T(8,128)(2,1)S(1)} %fusion.8), channel_id=1, source_target_pairs={{0,8},{4,12},{8,0},{12,4},{1,9},{5,13},{9,1},{13,5},{2,10},{6,14},... | collective-permute-start | bytes 1032200 | tf_op jit(solution)/shard_map/ppermute | solution.py:33
  31.2 6.8 %collective-permute-start.6 = (f32[2]{0:T(128)S(1)}, f32[2]{0:T(128)S(1)}, u32[]{:S(2)}, u32[]{:S(2)}) collective-permute-start(f32[2]{0:T(128)S(1)} %add.34), channel_id=1, source_target_pairs={{0,4},{4,0},{8,12},{12,8},{1,5},{5,1},{9,13},{13,9},{2,6},{6,2},{1... | collective-permute-start | bytes 32 | tf_op jit(solution)/shard_map/ppermute | solution.py:33
  38.0 4.5 %copy-start.7 = (s32[64]{0:T(128)S(1)}, s32[64]{0:T(128)}, u32[]{:S(2)}) copy-start(s32[64]{0:T(128)} %param.14) | copy-start | bytes 772
  38.0 12.1 %copy-start.5 = (s32[64,400]{1,0:T(8,128)S(1)}, s32[64,400]{1,0:T(8,128)}, u32[]{:S(2)}) copy-start(s32[64,400]{1,0:T(8,128)} %param.12) | copy-start | bytes 307204
  38.2 12.7 %copy-start = (bf16[1040,896]{1,0:T(8,128)(2,1)}, bf16[1040,896]{1,0:T(8,128)(2,1)S(1)}, u32[]{:S(2)}) copy-start(bf16[1040,896]{1,0:T(8,128)(2,1)S(1)} %pad_maximum_fusion.refs_1_) | copy-start | bytes 5591044
  38.2 9.2 %collective-permute-start.9 = (bf16[1040,896]{1,0:T(8,128)(2,1)S(1)}, bf16[1040,896]{1,0:T(8,128)(2,1)S(1)}, u32[]{:S(2)}, u32[]{:S(2)}) collective-permute-start(bf16[1040,896]{1,0:T(8,128)(2,1)S(1)} %pad_maximum_fusion.refs_1_), channel_id=1, source_target_pairs={{0,16},{16,0},{1,17},{17,1},{2,18},{18,2},{3,19},{19,3},{4,20},{20... | collective-permute-start | bytes 5591048 | tf_op jit(solution)/shard_map/ppermute | solution.py:33
  39.4 7.9 %collective-permute-start.7 = (bf16[112,896]{1,0:T(8,128)(2,1)S(1)}, bf16[112,896]{1,0:T(8,128)(2,1)S(1)}, u32[]{:S(2)}, u32[]{:S(2)}) collective-permute-start(bf16[112,896]{1,0:T(8,128)(2,1)S(1)} %slice.55), channel_id=1, source_target_pairs={{0,4},{4,0},{8,12},{12,8},{1,5},{5,1},{9,13},{13,9},{2,6},{6,2},{1... | collective-permute-start | bytes 602120 | tf_op jit(solution)/shard_map/ppermute | solution.py:33
  41.0 6.4 %collective-permute-start.8 = (bf16[96,896]{1,0:T(8,128)(2,1)S(1)}, bf16[96,896]{1,0:T(8,128)(2,1)S(1)}, u32[]{:S(2)}, u32[]{:S(2)}) collective-permute-start(bf16[96,896]{1,0:T(8,128)(2,1)S(1)} %slice.56), channel_id=1, source_target_pairs={{0,8},{4,12},{8,0},{12,4},{1,9},{5,13},{9,1},{13,5},{2,10},{6,14},... | collective-permute-start | bytes 516104 | tf_op jit(solution)/shard_map/ppermute | solution.py:33
  42.5 4.9 %collective-permute-start.10 = (f32[2]{0:T(128)S(1)}, f32[2]{0:T(128)S(1)}, u32[]{:S(2)}, u32[]{:S(2)}) collective-permute-start(f32[2]{0:T(128)S(1)} %add.35), channel_id=1, source_target_pairs={{0,8},{4,12},{8,0},{12,4},{1,9},{5,13},{9,1},{13,5},{2,10},{6,14},... | collective-permute-start | bytes 32 | tf_op jit(solution)/shard_map/ppermute | solution.py:33
  47.4 1.2 copy-start.2
  48.7 2.2 copy-start.3
  48.7 2.2 collective-permute-start.11
  50.9 0.7 copy-start.4
  51.6 52.2 %copy-start.6 = (s32[64]{0:T(128)S(1)}, s32[64]{0:T(128)}, u32[]{:S(2)}) copy-start(s32[64]{0:T(128)} %param.13) | copy-start | bytes 772
  162.1 3.5 %collective-permute-start.12 = (bf16[4,104,1552]{2,1,0:T(8,128)(2,1)}, bf16[4,104,1552]{2,1,0:T(8,128)(2,1)S(1)}, u32[]{:S(2)}, u32[]{:S(2)}) collective-permute-start(bf16[4,104,1552]{2,1,0:T(8,128)(2,1)} %get-tuple-element.52), channel_id=1, source_target_pairs={{0,16},{16,0},{1,17},{17,1},{2,18},{18,2},{3,19},{19,3},{4,20},{20... | collective-permute-start | bytes 3873800 | tf_op jit(solution)/shard_map/ppermute | solution.py:33
  168.7 21.6 %all-to-all-start = ((bf16[4,104,1552]{2,1,0:T(8,128)(2,1)}), bf16[4,104,1552]{2,1,0:T(8,128)(2,1)S(1)}, u32[]{:S(2)}, u32[]{:S(2)}) async-start(bf16[4,104,1552]{2,1,0:T(8,128)(2,1)} %add_convert_fusion), calls=%async_computation | async-start | bytes 2768896 | tf_op jit(solution)/shard_map/all_to_all | solution.py:614
  191.7 24.1 %all-to-all-start.1 = ((bf16[4,104,1552]{2,1,0:T(8,128)(2,1)}), bf16[4,104,1552]{2,1,0:T(8,128)(2,1)S(1)}, u32[]{:S(2)}, u32[]{:S(2)}) async-start(bf16[4,104,1552]{2,1,0:T(8,128)(2,1)} %broadcast_in_dim.24), calls=%async_computation.1 | async-start | bytes 2768896 | tf_op jit(solution)/shard_map/all_to_all | solution.py:625
  195.2 1.7 collective-permute-start.13
  200.1 4.4 %collective-permute-start.14 = (f32[2,2]{1,0:T(2,128)S(1)}, f32[2,2]{1,0:T(2,128)S(1)}, u32[]{:S(2)}, u32[]{:S(2)}) collective-permute-start(f32[2,2]{1,0:T(2,128)S(1)} %reshape.59), channel_id=1, source_target_pairs={{0,1},{1,0},{2,3},{3,2},{4,5},{5,4},{6,7},{7,6},{8,9},{9,8},{10,11... | collective-permute-start | bytes 56 | tf_op jit(solution)/shard_map/ppermute | solution.py:33
  200.4 4.5 %collective-permute-start.15 = (f32[2,2]{1,0:T(2,128)S(1)}, f32[2,2]{1,0:T(2,128)S(1)}, u32[]{:S(2)}, u32[]{:S(2)}) collective-permute-start(f32[2,2]{1,0:T(2,128)S(1)} %reshape.59), channel_id=1, source_target_pairs={{0,2},{1,3},{2,0},{3,1},{4,6},{5,7},{6,4},{7,5},{8,10},{9,11},{10,... | collective-permute-start | bytes 56 | tf_op jit(solution)/shard_map/ppermute | solution.py:33
  202.0 5.4 %collective-permute-start.16 = (f32[2,2]{1,0:T(2,128)S(1)}, f32[2,2]{1,0:T(2,128)S(1)}, u32[]{:S(2)}, u32[]{:S(2)}) collective-permute-start(f32[2,2]{1,0:T(2,128)S(1)} %reshape.59), channel_id=1, source_target_pairs={{0,3},{1,2},{2,1},{3,0},{4,7},{5,6},{6,5},{7,4},{8,11},{9,10},{10,... | collective-permute-start | bytes 56 | tf_op jit(solution)/shard_map/ppermute | solution.py:33
  207.4 5.2 %collective-permute-start.17 = (f32[2,2]{1,0:T(2,128)S(1)}, f32[2,2]{1,0:T(2,128)S(1)}, u32[]{:S(2)}, u32[]{:S(2)}) collective-permute-start(f32[2,2]{1,0:T(2,128)S(1)} %add_add_fusion.1), channel_id=1, source_target_pairs={{0,4},{4,0},{8,12},{12,8},{1,5},{5,1},{9,13},{13,9},{2,6},{6,2},{1... | collective-permute-start | bytes 56 | tf_op jit(solution)/shard_map/ppermute | solution.py:33
  209.3 3.6 %collective-permute-start.18 = (f32[2,2]{1,0:T(2,128)S(1)}, f32[2,2]{1,0:T(2,128)S(1)}, u32[]{:S(2)}, u32[]{:S(2)}) collective-permute-start(f32[2,2]{1,0:T(2,128)S(1)} %add_add_fusion.1), channel_id=1, source_target_pairs={{0,8},{4,12},{8,0},{12,4},{1,9},{5,13},{9,1},{13,5},{2,10},{6,14},... | collective-permute-start | bytes 56 | tf_op jit(solution)/shard_map/ppermute | solution.py:33
  210.8 4.5 %collective-permute-start.19 = (f32[2,2]{1,0:T(2,128)S(1)}, f32[2,2]{1,0:T(2,128)S(1)}, u32[]{:S(2)}, u32[]{:S(2)}) collective-permute-start(f32[2,2]{1,0:T(2,128)S(1)} %add_add_fusion.1), channel_id=1, source_target_pairs={{0,12},{4,8},{8,4},{12,0},{1,13},{5,9},{9,5},{13,1},{2,14},{6,10},... | collective-permute-start | bytes 56 | tf_op jit(solution)/shard_map/ppermute | solution.py:33

commit v2 on v1

--- a/solution.py
+++ b/solution.py
@@ -14,7 +14,6 @@
 KEEP_WEIGHT = 0.5
 LANES = 128
 TILE = 256
-VMEM_LIMIT = 58 << 20
 BF16 = jnp.bfloat16
 F32 = jnp.float32
 OVER_ROWS = (((0,), (0,)), ((), ()))
@@ -83,8 +82,8 @@
         return jnp.concatenate(parts, -1)
 
 
-def drop_kernel(width, tok_ref, scale_ref, drop_ref):
-    scale = scale_ref[...]
+def drop_kernel(width, tok_ref, mask_ref, drop_ref):
+    scale = mask_ref[...].astype(F32) * (1.0 / KEEP_INPUT)
     for k in range(tok_ref.shape[0]):
         drop_ref[k, :, :width] = (tok_ref[k].astype(F32) * scale).astype(BF16)
         drop_ref[k, :, width:] = jnp.ones_like(drop_ref[k, :, width:])
@@ -150,7 +149,9 @@
 def forward_kernel(cols, plan, sub, pieced, at_ref, first_ref, second_ref, third_ref, *refs):
     count = 5 if pieced else 1
     sources = refs[:count]
-    act_ref, cell_ref, prev_ref, w_ref, rec_ref, turned, even, odd, cell_s, low_s = refs[count:]
+    act_ref, cell_ref, prev_ref, w_out, rec_out, w_ref, turned, even, odd, cell_s, low_s, sems = refs[
+        count:
+    ]
     seqs, width = first_ref.shape[1:]
     steps = act_ref.shape[0]
     hidden = cols.hidden
@@ -164,6 +165,11 @@
                 if low >= start and high <= stop:
                     parts.append(rows_ref[q, unit : unit + high - low, first:last])
         return jnp.concatenate(parts, 0)
+
+    copies = [
+        pltpu.make_async_copy(w_ref.at[:, :, :width], w_out, sems.at[0]),
+        pltpu.make_async_copy(w_ref.at[:, :, width:], rec_out, sems.at[1]),
+    ]
 
     @pl.when(pl.program_id(0) == 0)
     def _():
@@ -179,9 +185,10 @@
                     line[array] += size
         else:
             w_ref[...] = sources[0][...]
-        rec_ref[...] = w_ref[:, :, width : width + hidden]
+        for copy in copies:
+            copy.start()
         turned[...] = turned_dot(
-            identity(hidden), columns_of(rec_ref, 0, cols.total, 0, hidden)
+            identity(hidden), columns_of(w_ref, 0, cols.total, width, width + hidden)
         ).astype(BF16)
         cell_s[...] = jnp.zeros_like(cell_s)
         low_s[...] = jnp.zeros_like(low_s)
@@ -234,116 +241,165 @@
         cell_s[:, a:b] = cells[j]
         low_s[:, a:b] = lows[j]
 
+    @pl.when(pl.program_id(0) == pl.num_programs(0) - 1)
+    def _():
+        for copy in copies:
+            copy.wait()
+
 
 def backward_kernel(
     cols,
     own,
-    row_ref,
+    at_ref,
     act_ref,
     cell_ref,
     before_ref,
     act_before_ref,
     cot_ref,
-    scale_ref,
-    coef_ref,
-    smooth_ref,
-    length_ref,
+    mask_ref,
+    ratio_ref,
+    length_row_ref,
     rec_ref,
-    grad_ref,
     *refs,
 ):
-    own_ref = refs[0] if own else None
-    cell_grad_s, recur_s, smooth_s = refs[-3:]
-    steps = act_ref.shape[0]
+    grad_ref = refs[6 if own else 0]
+    if own:
+        drop_ref, prev_ref, drop_end_ref, prev_end_ref, group_ref, weight_mask_ref = refs[:6]
+        keep_ref, send_ref = refs[7:9]
+        own_s, sides, pick, sums = refs[9:13]
+    dcell_s, recur_s, smooth_s, tanh_s, scale_s, coef_s, smooth_coef_s, length_s = refs[-8:]
+    steps, seqs, _ = act_ref.shape
+    hidden_n = cols.hidden
     place = pl.program_id(0)
     block = pl.num_programs(0) - 1 - place
+    spans = [cols.units(j) for j in range(cols.full + 1)]
 
     @pl.when(place == 0)
     def _():
-        cell_grad_s[...] = jnp.zeros_like(cell_grad_s)
+        dcell_s[...] = jnp.zeros_like(dcell_s)
         recur_s[...] = jnp.zeros_like(recur_s)
         smooth_s[...] = jnp.zeros_like(smooth_s)
+        tanh_s[...] = jnp.tanh(cell_ref[steps - 1])
+        ratio = column_of(ratio_ref[...])
+        length_s[...] = column_of(length_row_ref[...])
+        smooth_coef_s[...] = 2.0 * TAR_BETA * ratio
+        scale_s[...] = mask_ref[...].astype(F32) * (1.0 / KEEP_OUTPUT)
+        for a, b in spans:
+            scale = scale_s[:, a:b]
+            coef_s[:, a:b] = 2.0 * ACTIVATION_COEF * ratio[:, : b - a] * scale * scale
+        if own:
+            sums[...] = jnp.zeros_like(sums)
+            sides[...] = jnp.zeros_like(sides)
+            first = (group_ref[...] == 0.0).astype(F32).astype(BF16)
+            for k in range(steps):
+                pick[:, k * seqs : (k + 1) * seqs] = first
 
     inner = (block > 0).astype(F32)
-    spans = [cols.units(j) for j in range(cols.full + 1)]
-
-    def gates_at(ref, k, j):
+    rec = jnp.concatenate([rec_ref[q, a:b, :hidden_n] for a, b in spans for q in range(4)], 0)
+    jobs = []
+    if own:
+        width = drop_ref.shape[2]
+        for kind, count in enumerate((width, hidden_n)):
+            for start in range(0, count, TILE):
+                jobs += [(kind, start, min(start + TILE, count), q) for q in range(2)]
+
+    def weight_job(n, data):
+        kind, start, stop, q = jobs[n]
+        values = data[kind][...].reshape(steps * seqs, data[kind].shape[2])[:, start:stop]
+        base = kind * width
+        sums[q, :hidden_n, base + start : base + stop] += dot(sides[q], values)
+
+    def gates_at(k, j):
         if j < cols.full:
-            return [ref[k, :, a:b] for a, b in (cols.gate(j, q) for q in range(4))]
+            return [act_ref[k, :, a:b] for a, b in (cols.gate(j, q) for q in range(4))]
         first, last = cols.gates(j)
-        packed = ref[k, :, first:last]
+        packed = act_ref[k, :, first:last]
         return [packed[:, q * cols.rest : (q + 1) * cols.rest] for q in range(4)]
 
-    blocks = range(cols.full + 1)
-    rec = jnp.concatenate([rec_ref[q, a:b] for a, b in spans for q in range(4)], 0)
-    dcell = [cell_grad_s[:, a:b] for a, b in spans]
-    recur = [recur_s[:, a:b] for a, b in spans]
-    smooth_next = [smooth_s[:, a:b] for a, b in spans]
-    gates = [gates_at(act_ref, steps - 1, j) for j in blocks]
-    tanh_cell = [jnp.tanh(cell_ref[steps - 1, :, a:b]) for a, b in spans]
-    hidden = [gates[j][3] * tanh_cell[j] for j in blocks]
     for k in range(steps - 1, -1, -1):
-        parts = [None] * len(spans)
+        late = steps - 1 - k
+        for n in range(late * len(jobs) // steps, (late + 1) * len(jobs) // steps):
+            weight_job(n, (drop_ref, prev_ref))
         for j in cols.order:
             a, b = spans[j]
-            gate_i, gate_f, gate_g, gate_o = gates[j]
+            gate_i, gate_f, gate_g, gate_o = gates_at(k, j)
+            tanh_cell = tanh_s[:, a:b]
+            hidden = gate_o * tanh_cell
+            low, high = cols.gate(j, 3)
             if k > 0:
                 cell_before = cell_ref[k - 1, :, a:b]
-                gates[j] = gates_at(act_ref, k - 1, j)
+                out_before = act_ref[k - 1, :, low:high]
             else:
                 cell_before = before_ref[0, :, a:b] * inner
-                gates[j] = gates_at(act_before_ref, 0, j)
+                out_before = act_before_ref[0, :, low:high]
             tanh_before = jnp.tanh(cell_before)
-            hidden_before = gates[j][3] * tanh_before
-            valid = length_ref[:, a:b] > block * steps + k
-            smooth = smooth_ref[:, a:b] * (hidden[j] - hidden_before)
+            tanh_s[:, a:b] = tanh_before
+            valid = length_s[:, : b - a] > (block * steps + k).astype(F32)
+            smooth = smooth_coef_s[:, : b - a] * (hidden - out_before * tanh_before)
             if k == 0:
                 smooth = smooth * inner
             smooth = jnp.where(valid, smooth, 0.0)
-            direct = scale_ref[:, a:b] * cot_ref[k, :, a:b].astype(F32) + coef_ref[:, a:b] * hidden[j]
-            direct = jnp.where(valid, direct, 0.0) + smooth - smooth_next[j]
-            smooth_next[j] = smooth
-            dhidden = direct + recur[j]
-            total = dcell[j] + dhidden * (gate_o * (1.0 - tanh_cell[j] * tanh_cell[j]))
+            direct = scale_s[:, a:b] * cot_ref[k, :, a:b].astype(F32) + coef_s[:, a:b] * hidden
+            direct = jnp.where(valid, direct, 0.0) + smooth - smooth_s[:, a:b]
+            smooth_s[:, a:b] = smooth
+            dhidden = direct + recur_s[:, a:b]
+            total = dcell_s[:, a:b] + dhidden * (gate_o * (1.0 - tanh_cell * tanh_cell))
+            dcell_s[:, a:b] = total * gate_f
             grads = [
                 (total * (gate_g * gate_i * (1.0 - gate_i))).astype(BF16),
                 (total * (cell_before * gate_f * (1.0 - gate_f))).astype(BF16),
                 (total * (gate_i * (1.0 - gate_g * gate_g))).astype(BF16),
-                (dhidden * (tanh_cell[j] * gate_o * (1.0 - gate_o))).astype(BF16),
+                (dhidden * (tanh_cell * gate_o * (1.0 - gate_o))).astype(BF16),
             ]
-            parts[j] = jnp.concatenate(grads, 1)
             first, last = cols.gates(j)
-            grad_ref[k, :, first:last] = parts[j]
+            grad_ref[k, :, first:last] = jnp.concatenate(grads, 1)
             if own:
                 mine = grads[3]
                 for q in range(3):
-                    mine = jnp.where(row_ref[0] == q, grads[q], mine)
-                own_ref[k, :, a:b] = mine
-            dcell[j] = total * gate_f
-            tanh_cell[j] = tanh_before
-            hidden[j] = hidden_before
-        back = dot(jnp.concatenate(parts, 1), rec)
-        recur = [back[:, a:b] for a, b in spans]
-    for j, (a, b) in enumerate(spans):
-        cell_grad_s[:, a:b] = dcell[j]
-        recur_s[:, a:b] = recur[j]
-        smooth_s[:, a:b] = smooth_next[j]
-
-
-def weight_kernel(data_n, grp_ref, rows_ref, pick_ref, *refs):
-    data, scale, (keep_ref, send_ref, sums) = refs[:data_n], refs[data_n:-3], refs[-3:]
+                    mine = jnp.where(at_ref[0] == q, grads[q], mine)
+                own_s[k * seqs : (k + 1) * seqs, a:b] = mine
+        recur_s[...] = dot(grad_ref[k], rec)
+    if own:
+        turned = own_s[...].T
+        first = turned * pick[...]
+        sides[0] = first
+        sides[1] = turned - first
+
+        @pl.when(block == 0)
+        def _():
+            for n in range(len(jobs)):
+                weight_job(n, (drop_end_ref, prev_end_ref))
+            scale = weight_mask_ref[...].astype(F32) * (1.0 / KEEP_WEIGHT)
+            for q in range(2):
+                sums[q, :hidden_n, width:] = sums[q, :hidden_n, width:] * scale
+            hand_out(at_ref[2], sums, keep_ref, send_ref)
+
+
+def hand_out(grp_at, sums, keep_ref, send_ref):
+    rows = keep_ref.shape[1]
+    for part in range(keep_ref.shape[0]):
+        span = slice(part * rows, (part + 1) * rows)
+        keep_ref[part] = sums[grp_at, span]
+        send_ref[part] = sums[1 - grp_at, span].astype(BF16)
+
+
+def weight_kernel(grp_ref, rows_ref, group_ref, drop_ref, prev_ref, mask_ref, keep_ref, send_ref, sums, pick):
     steps, seqs, own = rows_ref.shape
     place = pl.program_id(0)
 
     @pl.when(place == 0)
     def _():
         sums[...] = jnp.zeros_like(sums)
+        one = (column_of(group_ref[...]) == 0.0).astype(F32).astype(BF16)
+        for at in range(0, own, LANES):
+            width = min(LANES, own - at)
+            pick[:, at : at + width] = one[:, :width]
 
     grads = rows_ref[...]
-    first = (grads * pick_ref[...][None]).reshape(steps * seqs, own)
+    first = (grads * pick[...][None]).reshape(steps * seqs, own)
     second = grads.reshape(steps * seqs, own) - first
     start = 0
-    for ref in data:
+    for ref in (drop_ref, prev_ref):
         width = ref.shape[2]
         values = ref[...].reshape(steps * seqs, width)
         for at, part in enumerate((first, second)):
@@ -354,25 +410,25 @@
 
     @pl.when(place == pl.num_programs(0) - 1)
     def _():
-        rows = keep_ref.shape[1]
-        for ref in scale:
-            for at in range(2):
-                part = (at, slice(0, own), slice(start - width, start))
-                sums[part] = sums[part] * ref[...]
-        for part in range(keep_ref.shape[0]):
-            span = slice(part * rows, (part + 1) * rows)
-            keep_ref[part] = sums[grp_ref[0], span]
-            send_ref[part] = sums[1 - grp_ref[0], span].astype(BF16)
-
-
-def params():
+        scale = mask_ref[...].astype(F32) * (1.0 / KEEP_WEIGHT)
+        for at in range(2):
+            part = (at, slice(0, own), slice(start - width, start))
+            sums[part] = sums[part] * scale
+        hand_out(grp_ref[0], sums, keep_ref, send_ref)
+
+
+def params(megabytes):
     return pltpu.CompilerParams(
-        dimension_semantics=("arbitrary",), vmem_limit_bytes=VMEM_LIMIT
+        dimension_semantics=("arbitrary",), vmem_limit_bytes=megabytes << 20
     )
 
 
 def fixed(*shape):
-    return pl.BlockSpec(shape, lambda *_: (0,) * len(shape))
+    return pl.BlockSpec(shape, lambda *_: (0,) * len(shape), pipeline_mode=pl.Buffered(1))
+
+
+def column_of(row):
+    return jnp.broadcast_to(row, (LANES, row.shape[1])).T
 
 
 def gather_pieces(plan, mine, counts, beside):
@@ -428,7 +484,6 @@
     own = row_count == hidden
     pieced = own and rows_n == 4 and seq_n == 4 and lax.axis_size("grp") == 2
 
-    w_scale = weight_mask.astype(F32) / KEEP_WEIGHT
     plan = Plan(hidden, wide)
     at = jnp.stack([row_at, seq_at, grp_at]).astype(jnp.int32)
     own_weights, *mine = pl.pallas_call(
@@ -446,7 +501,7 @@
         ),
         out_shape=[jax.ShapeDtypeStruct((row_count, plan.columns), BF16)]
         + [jax.ShapeDtypeStruct((plan.rows, plan.cut), BF16)] * pieced,
-        compiler_params=params(),
+        compiler_params=params(58),
         name="shard",
     )(at, input_gate_weight, w_recur, weight_mask, bias[None])
     sub = max(s for s in range(1, 8) if time_steps % (2 * s) == 0)
@@ -456,16 +511,15 @@
     def at_time(width):
         return pl.BlockSpec((steps, seq_count, width), lambda b, *_: (b, 0, 0))
 
-    in_scale = in_mask.astype(F32) / KEEP_INPUT
     dropped = pl.pallas_call(
         functools.partial(drop_kernel, width_in),
         grid=(blocks,),
         in_specs=[at_time(width_in), fixed(seq_count, width_in)],
         out_specs=at_time(wide),
         out_shape=jax.ShapeDtypeStruct((time_steps, seq_count, wide), BF16),
-        compiler_params=params(),
+        compiler_params=params(58),
         name="drop",
-    )(jnp.swapaxes(tokens, 0, 1), in_scale)
+    )(jnp.swapaxes(tokens, 0, 1), in_mask)
     cot_time = jnp.swapaxes(cotangent, 0, 1)
 
     group_hot = (groups[:, None] == jnp.arange(2)[None, :]).astype(F32)
@@ -480,10 +534,6 @@
         sources = [whole.reshape(4, hidden, plan.columns)]
     group_ratio = jnp.sum(counts) / counts
     seq_ratio = jnp.sum(group_hot * group_ratio[None, :], 1)
-    out_scale = out_mask.astype(F32) / KEEP_OUTPUT
-    act_coef = 2.0 * ACTIVATION_COEF * seq_ratio[:, None] * out_scale * out_scale
-    smooth_coef = jnp.broadcast_to(2.0 * TAR_BETA * seq_ratio[:, None], (seq_count, hidden))
-    length_wide = jnp.broadcast_to(lengths[:, None], (seq_count, hidden))
 
     acts, cells, prev_low, weights, w_rec = pl.pallas_call(
         functools.partial(forward_kernel, cols, plan, sub, pieced),
@@ -503,46 +553,78 @@
                 at_time(cols.total),
                 at_time(hidden),
                 at_time(hidden),
-                fixed(4, hidden, plan.columns),
-                fixed(4, hidden, hidden),
+                pl.BlockSpec(memory_space=pl.ANY),
+                pl.BlockSpec(memory_space=pl.ANY),
             ],
             scratch_shapes=[
+                pltpu.VMEM((4, hidden, plan.columns), BF16),
                 pltpu.VMEM((hidden, cols.total), BF16),
                 pltpu.VMEM((sub * seq_count, cols.total), F32),
                 pltpu.VMEM((sub * seq_count, cols.total), F32),
                 pltpu.VMEM((seq_count, hidden), F32),
                 pltpu.VMEM((seq_count, hidden), BF16),
+                pltpu.SemaphoreType.DMA((2,)),
             ],
         ),
         out_shape=[
             jax.ShapeDtypeStruct((time_steps, seq_count, cols.total), F32),
             jax.ShapeDtypeStruct((time_steps, seq_count, hidden), F32),
             jax.ShapeDtypeStruct((time_steps, seq_count, hidden), BF16),
-            jax.ShapeDtypeStruct((4, hidden, plan.columns), BF16),
-            jax.ShapeDtypeStruct((4, hidden, hidden), BF16),
+            jax.ShapeDtypeStruct((4, hidden, wide), BF16),
+            jax.ShapeDtypeStruct((4, hidden, plan.columns - wide), BF16),
         ],
-        compiler_params=params(),
+        compiler_params=params(58),
         name="forward",
     )(at, dropped, dropped, dropped, *sources)
 
     def back(b):
-        return 2 * blocks - 1 - b
+        return blocks - 1 - b
 
     def before(width):
         return pl.BlockSpec(
-            (1, seq_count, width), lambda b, *_: (jnp.maximum(back(b) * sub - 1, 0), 0, 0)
+            (1, seq_count, width), lambda b, *_: (jnp.maximum(back(b) * steps - 1, 0), 0, 0)
         )
 
     def back_time(width):
-        return pl.BlockSpec((sub, seq_count, width), lambda b, *_: (back(b), 0, 0))
-
-    grad_specs = [back_time(cols.total)] + [back_time(hidden)] * own
-    grad_shapes = [cols.total] + [hidden] * own
-    grads, *own_rows = pl.pallas_call(
+        return pl.BlockSpec((steps, seq_count, width), lambda b, *_: (back(b), 0, 0))
+
+    def later_time(width):
+        return pl.BlockSpec(
+            (steps, seq_count, width), lambda b, *_: (jnp.minimum(back(b) + 1, blocks - 1), 0, 0)
+        )
+
+    part_rows = ceil_to(-(-row_count // seq_n), 8)
+    columns = wide + hidden
+    group_row = groups.astype(F32)[None]
+    sum_specs = [fixed(seq_n, part_rows, columns)] * 2
+    sum_shapes = [
+        jax.ShapeDtypeStruct((seq_n, part_rows, columns), F32),
+        jax.ShapeDtypeStruct((seq_n, part_rows, columns), BF16),
+    ]
+    sum_scratch = pltpu.VMEM((2, seq_n * part_rows, columns), F32)
+    per_unit = pltpu.VMEM((seq_count, hidden), F32)
+    own_specs, own_arrays, own_scratch = [], [], []
+    if own:
+        own_specs = [
+            later_time(wide),
+            later_time(hidden),
+            fixed(steps, seq_count, wide),
+            fixed(steps, seq_count, hidden),
+            fixed(1, seq_count),
+            fixed(row_count, hidden),
+        ]
+        own_arrays = [dropped, prev_low, dropped, prev_low, group_row, weight_mask]
+        own_scratch = [
+            pltpu.VMEM((steps * seq_count, hidden), BF16),
+            pltpu.VMEM((2, hidden, steps * seq_count), BF16),
+            pltpu.VMEM((1, steps * seq_count), BF16),
+            sum_scratch,
+        ]
+    grads, *sums = pl.pallas_call(
         functools.partial(backward_kernel, cols, own),
         grid_spec=pltpu.PrefetchScalarGridSpec(
             num_scalar_prefetch=1,
-            grid=(2 * blocks,),
+            grid=(blocks,),
             in_specs=[
                 back_time(cols.total),
                 back_time(hidden),
@@ -550,71 +632,65 @@
                 before(cols.total),
                 back_time(hidden),
                 fixed(seq_count, hidden),
-                fixed(seq_count, hidden),
-                fixed(seq_count, hidden),
-                fixed(seq_count, hidden),
-                fixed(4, hidden, hidden),
-            ],
-            out_specs=grad_specs,
-            scratch_shapes=[pltpu.VMEM((seq_count, hidden), F32)] * 3,
+                fixed(1, seq_count),
+                fixed(1, seq_count),
+                fixed(4, hidden, plan.columns - wide),
+            ]
+            + own_specs,
+            out_specs=[back_time(cols.total)] + sum_specs * own,
+            scratch_shapes=own_scratch
+            + [per_unit] * 6
+            + [pltpu.VMEM((seq_count, LANES), F32)] * 2,
         ),
-        out_shape=[
-            jax.ShapeDtypeStruct((time_steps, seq_count, width), BF16) for width in grad_shapes
-        ],
-        compiler_params=params(),
+        out_shape=[jax.ShapeDtypeStruct((time_steps, seq_count, cols.total), BF16)]
+        + sum_shapes * own,
+        compiler_params=params(58),
         name="backward",
     )(
-        row_at[None],
+        at,
         acts,
         cells,
         cells,
         acts,
         cot_time,
-        out_scale,
-        act_coef,
-        smooth_coef,
-        length_wide,
+        out_mask,
+        seq_ratio[None],
+        lengths.astype(F32)[None],
         w_rec,
+        *own_arrays,
     )
 
-    if own:
-        own_rows = own_rows[0]
-    else:
+    if not own:
         own_rows = lax.dynamic_slice_in_dim(
             cols.unpack_lanes(grads), row_at * row_count, row_count, 2
         )
-    pick = jnp.broadcast_to((groups == 0).astype(BF16)[:, None], (seq_count, row_count))
-    part_rows = ceil_to(-(-row_count // seq_n), 8)
-    def weight_sums(rows, data, specs, scale):
-        columns = sum(spec.block_shape[2] for spec in specs)
-        return pl.pallas_call(
-            functools.partial(weight_kernel, len(data)),
+        sums = pl.pallas_call(
+            weight_kernel,
             grid_spec=pltpu.PrefetchScalarGridSpec(
                 num_scalar_prefetch=1,
                 grid=(blocks,),
-                in_specs=[at_time(row_count), fixed(seq_count, row_count)]
-                + specs
-                + [fixed(*part.shape) for part in scale],
-                out_specs=[fixed(seq_n, part_rows, columns)] * 2,
-                scratch_shapes=[pltpu.VMEM((2, seq_n * part_rows, columns), F32)],
+                in_specs=[
+                    at_time(row_count),
+                    fixed(1, seq_count),
+                    at_time(wide),
+                    at_time(hidden),
+                    fixed(row_count, hidden),
+                ],
+                out_specs=sum_specs,
+                scratch_shapes=[sum_scratch, pltpu.VMEM((seq_count, row_count), BF16)],
             ),
-            out_shape=[
-                jax.ShapeDtypeStruct((seq_n, part_rows, columns), F32),
-                jax.ShapeDtypeStruct((seq_n, part_rows, columns), BF16),
-            ],
-            compiler_params=params(),
+            out_shape=sum_shapes,
+            compiler_params=params(58),
             name="weights",
-        )(grp_at[None], rows, pick, *data, *scale)
+        )(grp_at[None], own_rows, group_row, dropped, prev_low, weight_mask)
+    keep, send = sums
 
     hold = lax.optimization_barrier
-    keep, send = weight_sums(
-        own_rows, [dropped, prev_low], [at_time(wide), at_time(hidden)], [w_scale]
-    )
     block = (keep + flip(send, "grp", 1).astype(F32)).astype(BF16)
     swapped = lax.all_to_all(block, "seq", 0, 0, tiled=True)
 
     own_seqs = lax.dynamic_slice_in_dim(grads, row_at * share, share, 1)
-    own_scale = lax.dynamic_slice_in_dim(in_scale, row_at * share, share, 0)
+    own_scale = lax.dynamic_slice_in_dim(in_mask, row_at * share, share, 0).astype(F32) / KEEP_INPUT
     w_in = cols.pack(weights[:, :, :width_in])
     input_time = jnp.einsum("tsr,rk->tsk", own_seqs, w_in, preferred_element_type=F32)
     input_grad = jnp.swapaxes(input_time * own_scale[None], 0, 1)

time: 220 us -> 212 us (0.964)
  Pallas kernels: 122 us -> 118 us
  local copies, waits for them, and re-layouts: 12.8 us -> 9.81 us
    pallas_call x1 -> x0, Pallas kernels: 21.8 us -> none  [weight_sums(): pl.pallas_call(functools.partial(weight_kernel, len(data)), grid_spec=plt...]
    pallas_call x1, Pallas kernels: 35 us -> 54 us  [local(): pl.pallas_call(functools.partial(backward_kernel, cols, own), grid_spec=p...]
where the time goes in v2:
time: 212 us
  Pallas kernels  118 us (56%)
  waiting for transfers between devices  30.6 us (14%)
  starting transfers between devices  29.4 us (14%)
  other arithmetic  13.5 us (6%)
  local copies, waits for them, and re-layouts  9.81 us (5%)
  matrix products  9.77 us (5%)
    pallas_call x1, Pallas kernels, local(): pl.pallas_call(functools.partial(backward_kernel, cols, own), grid_spec=p...  54 us
    pallas_call x1, Pallas kernels, local(): pl.pallas_call(functools.partial(forward_kernel, cols, plan, sub, pieced)...  49.5 us
    ppermute x20, waiting for transfers between devices, flip(): return lax.ppermute(block, axis, [(at, at ^ bit) for at in range(count)])  25.9 us
    ppermute x20, starting transfers between devices, flip(): return lax.ppermute(block, axis, [(at, at ^ bit) for at in range(count)])  22.1 us
    pallas_call x1, Pallas kernels, local(): pl.pallas_call(functools.partial(drop_kernel, width_in), grid=(blocks,),...  10.4 us
    dot_general x1, matrix products, local(): jnp.einsum('tsr,rk->tsk', own_seqs, w_in, preferred_element_type=F32)  9.77 us
    all_to_all x1, waiting for transfers between devices, local(): swapped = lax.all_to_all(block, 'seq', 0, 0, tiled=True)  4.74 us
  transfers between devices with their start and end apart: 22, of which 12 were waited for; matrix products, arithmetic and copies ran while one was open for 11% of the time, Pallas kernels for 5%

profile of v2, /device:TPU:0, one launch (start us, length us, event | category | flops | bytes accessed | tf_op | source)
XLA Modules:
  0.0 211.8 jit_solution(8375158793320905148)
XLA Ops:
  0.6 0.7 pad_add_fusion.at_ref
  1.3 3.9 %shard.1 = (bf16[400,1664]{1,0:T(8,128)(2,1)}, bf16[208,896]{1,0:T(8,128)(2,1)}) custom-call(s32[3]{0:T(128)} %pad_add_fusion.at_ref, bf16[400,1150]{1,0:T(8,128)(2,1)} %in_ref.1, bf16[400,400]{1,0:T(8,128)(2,1)} %rec_ref.1, s32[400,400]{1,0:T(8,128)} %refs_5_.1, f32[1,400]{1,0:T(1,128)} %bitcast.51), custom_call_target="tpu_custom_call" | custom-call | tf_op jit(solution)/shard_map/shard/pallas_call | solution.py:489
  5.2 3.0 %collective-permute-start = (bf16[208,896]{1,0:T(8,128)(2,1)}, bf16[208,896]{1,0:T(8,128)(2,1)S(1)}, u32[]{:S(2)}, u32[]{:S(2)}) collective-permute-start(bf16[208,896]{1,0:T(8,128)(2,1)} %get-tuple-element.31), channel_id=1, source_target_pairs={{0,1},{1,0},{2,3},{3,2},{4,5},{5,4},{6,7},{7,6},{8,9},{9,8},{10,11... | collective-permute-start | bytes 1118216 | tf_op jit(solution)/shard_map/ppermute | solution.py:32
  8.2 2.6 %collective-permute-start.1 = (bf16[208,896]{1,0:T(8,128)(2,1)}, bf16[208,896]{1,0:T(8,128)(2,1)S(1)}, u32[]{:S(2)}, u32[]{:S(2)}) collective-permute-start(bf16[208,896]{1,0:T(8,128)(2,1)} %get-tuple-element.31), channel_id=1, source_target_pairs={{0,2},{1,3},{2,0},{3,1},{4,6},{5,7},{6,4},{7,5},{8,10},{9,11},{10,... | collective-permute-start | bytes 1118216 | tf_op jit(solution)/shard_map/ppermute | solution.py:32
  10.8 1.2 convert_bitcast_fusion.1
  12.1 0.8 select_reduce_fusion.1
  12.8 0.1 collective-permute-start.2
  12.9 10.4 %drop.1.first_ref.second_ref.third_ref.refs_0_.refs_2_ = bf16[70,64,1152]{2,1,0:T(8,128)(2,1)} custom-call(bf16[70,64,1150]{2,1,0:T(8,128)(2,1)} %bitcast.34, s32[64,1150]{1,0:T(8,128)} %mask_ref.4), custom_call_target="tpu_custom_call" | custom-call | tf_op jit(solution)/shard_map/drop/pallas_call | solution.py:514
  23.3 1.7 collective-permute-done
  25.0 2.5 %collective-permute-done.1 = bf16[208,896]{1,0:T(8,128)(2,1)S(1)} collective-permute-done((bf16[208,896]{1,0:T(8,128)(2,1)}, bf16[208,896]{1,0:T(8,128)(2,1)S(1)}, u32[]{:S(2)}, u32[]{:S(2)}) %collective-permute-start.1) | collective-permute-done | bytes 372768 | tf_op jit(solution)/shard_map/ppermute | solution.py:32
  27.5 0.4 collective-permute-start.5
  28.0 1.6 collective-permute-start.3
  29.6 1.6 collective-permute-start.4
  31.2 0.5 collective-permute-start.6
  31.7 0.1 pad_maximum_fusion.1
  31.8 6.1 %collective-permute-done.6 = f32[2]{0:T(128)S(1)} collective-permute-done((f32[2]{0:T(128)S(1)}, f32[2]{0:T(128)S(1)}, u32[]{:S(2)}, u32[]{:S(2)}) %collective-permute-start.6) | collective-permute-done | bytes 40 | tf_op jit(solution)/shard_map/ppermute | solution.py:32
  38.0 0.1 pad_maximum_fusion.refs_1_
  38.2 0.1 collective-permute-start.9
  38.3 1.6 collective-permute-start.7
  39.8 1.6 collective-permute-start.8
  41.4 0.5 collective-permute-start.10
  41.9 4.5 %collective-permute-done.10 = f32[2]{0:T(128)S(1)} collective-permute-done((f32[2]{0:T(128)S(1)}, f32[2]{0:T(128)S(1)}, u32[]{:S(2)}, u32[]{:S(2)}) %collective-permute-start.10) | collective-permute-done | bytes 40 | tf_op jit(solution)/shard_map/ppermute | solution.py:32
  46.5 1.2 copy-done.1
  47.8 0.1 collective-permute-start.11
  47.9 0.5 convert_bitcast_fusion.refs_4_
  48.4 0.6 reduce_sum.67
  49.0 0.6 broadcast_divide_fusion
  49.7 0.7 select_reduce_fusion
  50.3 0.7 copy-done.3
  51.1 49.5 %forward.1 = (f32[70,64,1600]{2,1,0:T(8,128)}, f32[70,64,400]{2,1,0:T(8,128)}, bf16[70,64,400]{2,1,0:T(8,128)(2,1)}, bf16[4,400,1152]{2,1,0:T(8,128)(2,1)}, bf16[4,400,512]{2,1,0:T(8,128)(2,1)}) custom-call(s32[3]{0:T(128)} %pad_add_fusion.at_ref, bf16[70,64,1152]{2,1,0:T(8,128)(2,1)} %drop.1.first_ref.second_ref.third_ref.refs_0_.refs_2_, ...), custom_call_target="tpu_custom_call" | custom-call | tf_op jit(solution)/shard_map/forward/pallas_call | solution.py:538
  100.6 54.0 %backward.1 = (bf16[70,64,1600]{2,1,0:T(8,128)(2,1)}, f32[4,104,1552]{2,1,0:T(8,128)}, bf16[4,104,1552]{2,1,0:T(8,128)(2,1)}) custom-call(s32[3]{0:T(128)} %pad_add_fusion.at_ref, f32[70,64,1600]{2,1,0:T(8,128)} %get-tuple-element.44.act_ref.act_before_ref, f32[70,64,400]{2,1,0:T(8,128)} %get-tuple-element.45.cell_ref.before_ref, ...), custom_call_target="tpu_custom_call" | custom-call | tf_op jit(solution)/shard_map/backward/pallas_call | solution.py:623
  154.6 0.5 collective-permute-start.12
  155.2 0.9 convert_multiply_fusion
  156.1 2.1 collective-permute-done.12
  158.1 3.2 %add_convert_fusion = bf16[4,104,1552]{2,1,0:T(8,128)(2,1)} fusion(f32[4,104,1552]{2,1,0:T(8,128)} %get-tuple-element.49, bf16[4,104,1552]{2,1,0:T(8,128)(2,1)S(1)} %collective-permute-done.12), kind=kLoop, calls=%fused_computation.9 | loop fusion | flops 1936896 | bytes 5165056 | tf_op jit(solution)/shard_map/convert_element_type | solution.py:689
  161.3 3.8 %all-to-all-start = ((bf16[4,104,1552]{2,1,0:T(8,128)(2,1)}), bf16[4,104,1552]{2,1,0:T(8,128)(2,1)S(1)}, u32[]{:S(2)}, u32[]{:S(2)}) async-start(bf16[4,104,1552]{2,1,0:T(8,128)(2,1)} %add_convert_fusion), calls=%async_computation | async-start | bytes 2768896 | tf_op jit(solution)/shard_map/all_to_all | solution.py:690
  165.1 2.3 %fusion.11 = (bf16[4,128,1150]{2,1,0:T(8,128)(2,1)S(1)}, bf16[4,128,1150]{2,1,0:T(8,128)(2,1)S(1)}, bf16[4,128,1150]{2,1,0:T(8,128)(2,1)S(1)}) fusion(bf16[4,400,1152]{2,1,0:T(8,128)(2,1)} %get-tuple-element.52), kind=kLoop, calls=%fused_computation.45 | loop fusion | bytes 7065600 | tf_op jit(solution)/shard_map/slice | solution.py:73
  167.5 0.9 slice.60
  168.4 9.8 %multiply_bitcast_fusion = f32[16,70,1150]{2,0,1:T(8,128)} fusion(bf16[70,64,1600]{2,1,0:T(8,128)(2,1)} %get-tuple-element.51, s32[]{:T(128)S(6)} %select_n.16, bf16[64,1150]{1,0:T(8,128)(2,1)S(1)} %bitcast.49, bf16[512,1150]{1,0:T(8,128)(2,1)S(1)} %bitcast.45, bf16[512,1150]{1,0:T(8,128)(2,1)S(1)} %bitcast.46, bf16[512,1150]{1,0:T(8,128)(2,1)S(1)} %bitcast.44, ...), kind=kOutput, calls=%fused_computation | convolution fusion | flops 4137607936 | bytes 12632964 | tf_op jit(solution)/shard_map/tsr,rk->tsk/dot_general | solution.py:695
  178.2 4.7 %all-to-all-done = bf16[4,104,1552]{2,1,0:T(8,128)(2,1)S(1)} async-done(((bf16[4,104,1552]{2,1,0:T(8,128)(2,1)}), bf16[4,104,1552]{2,1,0:T(8,128)(2,1)S(1)}, u32[]{:S(2)}, u32[]{:S(2)}) %all-to-all-start) | async-done | bytes 1291296 | tf_op jit(solution)/shard_map/all_to_all | solution.py:690
  182.9 0.2 reduce_sum.69
  183.1 1.2 broadcast_in_dim.33
  184.3 3.5 %all-to-all-start.1 = ((bf16[4,104,1552]{2,1,0:T(8,128)(2,1)}), bf16[4,104,1552]{2,1,0:T(8,128)(2,1)S(1)}, u32[]{:S(2)}, u32[]{:S(2)}) async-start(bf16[4,104,1552]{2,1,0:T(8,128)(2,1)} %broadcast_in_dim.33), calls=%async_computation.1 | async-start | bytes 2768896 | tf_op jit(solution)/shard_map/all_to_all | solution.py:701
  187.9 0.1 collective-permute-start.13
  188.0 1.6 collective-permute-done.13
  189.6 1.0 multiply_reduce_fusion.2
  190.6 2.0 pad_maximum_fusion.4
  192.6 0.1 reshape.49
  192.7 0.3 collective-permute-start.14
  193.0 1.6 collective-permute-start.15
  194.6 2.5 %collective-permute-start.16 = (f32[2,2]{1,0:T(2,128)S(1)}, f32[2,2]{1,0:T(2,128)S(1)}, u32[]{:S(2)}, u32[]{:S(2)}) collective-permute-start(f32[2,2]{1,0:T(2,128)S(1)} %reshape.49), channel_id=1, source_target_pairs={{0,3},{1,2},{2,1},{3,0},{4,7},{5,6},{6,5},{7,4},{8,11},{9,10},{10,... | collective-permute-start | bytes 56 | tf_op jit(solution)/shard_map/ppermute | solution.py:32
  197.1 0.4 collective-permute-done.15
  197.5 2.5 %collective-permute-done.16 = f32[2,2]{1,0:T(2,128)S(1)} collective-permute-done((f32[2,2]{1,0:T(2,128)S(1)}, f32[2,2]{1,0:T(2,128)S(1)}, u32[]{:S(2)}, u32[]{:S(2)}) %collective-permute-start.16) | collective-permute-done | bytes 48 | tf_op jit(solution)/shard_map/ppermute | solution.py:32
  200.0 1.9 collective-permute-start.17
  201.9 1.5 collective-permute-start.18
  203.4 0.1 collective-permute-start.19
  203.5 1.7 collective-permute-done.17
  205.1 0.3 collective-permute-done.18
  205.5 2.4 %collective-permute-done.19 = f32[2,2]{1,0:T(2,128)S(1)} collective-permute-done((f32[2,2]{1,0:T(2,128)S(1)}, f32[2,2]{1,0:T(2,128)S(1)}, u32[]{:S(2)}, u32[]{:S(2)}) %collective-permute-start.19) | collective-permute-done | bytes 48 | tf_op jit(solution)/shard_map/ppermute | solution.py:32
  207.8 0.6 add_add_fusion
  208.4 0.2 slice_convert_fusion
  208.6 1.4 slice_bitcast_fusion
  209.9 1.0 slice_bitcast_fusion.1
  210.9 0.8 slice_reduce_fusion
  (32 shorter events, 0.3 us)
Async XLA Ops:
  5.2 19.8 %collective-permute-start = (bf16[208,896]{1,0:T(8,128)(2,1)}, bf16[208,896]{1,0:T(8,128)(2,1)S(1)}, u32[]{:S(2)}, u32[]{:S(2)}) collective-permute-start(bf16[208,896]{1,0:T(8,128)(2,1)} %get-tuple-element.31), channel_id=1, source_target_pairs={{0,1},{1,0},{2,3},{3,2},{4,5},{5,4},{6,7},{7,6},{8,9},{9,8},{10,11... | collective-permute-start | bytes 1118216 | tf_op jit(solution)/shard_map/ppermute | solution.py:32
  8.2 19.3 %collective-permute-start.1 = (bf16[208,896]{1,0:T(8,128)(2,1)}, bf16[208,896]{1,0:T(8,128)(2,1)S(1)}, u32[]{:S(2)}, u32[]{:S(2)}) collective-permute-start(bf16[208,896]{1,0:T(8,128)(2,1)} %get-tuple-element.31), channel_id=1, source_target_pairs={{0,2},{1,3},{2,0},{3,1},{4,6},{5,7},{6,4},{7,5},{8,10},{9,11},{10,... | collective-permute-start | bytes 1118216 | tf_op jit(solution)/shard_map/ppermute | solution.py:32
  12.8 10.5 %collective-permute-start.2 = (f32[2]{0:T(128)S(1)}, f32[2]{0:T(128)S(1)}, u32[]{:S(2)}, u32[]{:S(2)}) collective-permute-start(f32[2]{0:T(128)S(1)} %select_reduce_fusion.1), channel_id=1, source_target_pairs={{0,16},{16,0},{1,17},{17,1},{2,18},{18,2},{3,19},{19,3},{4,20},{20... | collective-permute-start | bytes 32 | tf_op jit(solution)/shard_map/ppermute | solution.py:32
  27.5 10.5 %collective-permute-start.5 = (bf16[208,896]{1,0:T(8,128)(2,1)S(1)}, bf16[208,896]{1,0:T(8,128)(2,1)S(1)}, u32[]{:S(2)}, u32[]{:S(2)}) collective-permute-start(bf16[208,896]{1,0:T(8,128)(2,1)S(1)} %collective-permute-done.1), channel_id=1, source_target_pairs={{0,1},{1,0},{2,3},{3,2},{4,5},{5,4},{6,7},{7,6},{8,9},{9,8},{10,11... | collective-permute-start | bytes 1118216 | tf_op jit(solution)/shard_map/ppermute | solution.py:32
  28.0 10.0 %collective-permute-start.3 = (bf16[2,112,896]{2,1,0:T(8,128)(2,1)S(1)}, bf16[2,112,896]{2,1,0:T(8,128)(2,1)S(1)}, u32[]{:S(2)}, u32[]{:S(2)}) collective-permute-start(bf16[2,112,896]{2,1,0:T(8,128)(2,1)S(1)} %fusion.7), channel_id=1, source_target_pairs={{0,4},{4,0},{8,12},{12,8},{1,5},{5,1},{9,13},{13,9},{2,6},{6,2},{1... | collective-permute-start | bytes 1204232 | tf_op jit(solution)/shard_map/ppermute | solution.py:32
  29.6 8.4 %collective-permute-start.4 = (bf16[2,96,896]{2,1,0:T(8,128)(2,1)S(1)}, bf16[2,96,896]{2,1,0:T(8,128)(2,1)S(1)}, u32[]{:S(2)}, u32[]{:S(2)}) collective-permute-start(bf16[2,96,896]{2,1,0:T(8,128)(2,1)S(1)} %fusion.8), channel_id=1, source_target_pairs={{0,8},{4,12},{8,0},{12,4},{1,9},{5,13},{9,1},{13,5},{2,10},{6,14},... | collective-permute-start | bytes 1032200 | tf_op jit(solution)/shard_map/ppermute | solution.py:32
  31.2 6.8 %collective-permute-start.6 = (f32[2]{0:T(128)S(1)}, f32[2]{0:T(128)S(1)}, u32[]{:S(2)}, u32[]{:S(2)}) collective-permute-start(f32[2]{0:T(128)S(1)} %add.34), channel_id=1, source_target_pairs={{0,4},{4,0},{8,12},{12,8},{1,5},{5,1},{9,13},{13,9},{2,6},{6,2},{1... | collective-permute-start | bytes 32 | tf_op jit(solution)/shard_map/ppermute | solution.py:32
  31.8 16.0 %copy-start.4 = (s32[64]{0:T(128)S(1)}, s32[64]{0:T(128)}, u32[]{:S(2)}) copy-start(s32[64]{0:T(128)} %param.14) | copy-start | bytes 772
  38.1 12.2 %copy-start = (bf16[1040,896]{1,0:T(8,128)(2,1)}, bf16[1040,896]{1,0:T(8,128)(2,1)S(1)}, u32[]{:S(2)}) copy-start(bf16[1040,896]{1,0:T(8,128)(2,1)S(1)} %pad_maximum_fusion.refs_1_) | copy-start | bytes 5591044
  38.2 8.3 %collective-permute-start.9 = (bf16[1040,896]{1,0:T(8,128)(2,1)S(1)}, bf16[1040,896]{1,0:T(8,128)(2,1)S(1)}, u32[]{:S(2)}, u32[]{:S(2)}) collective-permute-start(bf16[1040,896]{1,0:T(8,128)(2,1)S(1)} %pad_maximum_fusion.refs_1_), channel_id=1, source_target_pairs={{0,16},{16,0},{1,17},{17,1},{2,18},{18,2},{3,19},{19,3},{4,20},{20... | collective-permute-start | bytes 5591048 | tf_op jit(solution)/shard_map/ppermute | solution.py:32
  38.3 8.2 %collective-permute-start.7 = (bf16[112,896]{1,0:T(8,128)(2,1)S(1)}, bf16[112,896]{1,0:T(8,128)(2,1)S(1)}, u32[]{:S(2)}, u32[]{:S(2)}) collective-permute-start(bf16[112,896]{1,0:T(8,128)(2,1)S(1)} %slice.55), channel_id=1, source_target_pairs={{0,4},{4,0},{8,12},{12,8},{1,5},{5,1},{9,13},{13,9},{2,6},{6,2},{1... | collective-permute-start | bytes 602120 | tf_op jit(solution)/shard_map/ppermute | solution.py:32
  39.8 6.6 %collective-permute-start.8 = (bf16[96,896]{1,0:T(8,128)(2,1)S(1)}, bf16[96,896]{1,0:T(8,128)(2,1)S(1)}, u32[]{:S(2)}, u32[]{:S(2)}) collective-permute-start(bf16[96,896]{1,0:T(8,128)(2,1)S(1)} %slice.56), channel_id=1, source_target_pairs={{0,8},{4,12},{8,0},{12,4},{1,9},{5,13},{9,1},{13,5},{2,10},{6,14},... | collective-permute-start | bytes 516104 | tf_op jit(solution)/shard_map/ppermute | solution.py:32
  41.4 5.0 %collective-permute-start.10 = (f32[2]{0:T(128)S(1)}, f32[2]{0:T(128)S(1)}, u32[]{:S(2)}, u32[]{:S(2)}) collective-permute-start(f32[2]{0:T(128)S(1)} %add.35), channel_id=1, source_target_pairs={{0,8},{4,12},{8,0},{12,4},{1,9},{5,13},{9,1},{13,5},{2,10},{6,14},... | collective-permute-start | bytes 32 | tf_op jit(solution)/shard_map/ppermute | solution.py:32
  46.5 1.2 copy-start.1
  47.8 2.6 %copy-start.2 = (bf16[208,896]{1,0:T(8,128)(2,1)}, bf16[208,896]{1,0:T(8,128)(2,1)S(1)}, u32[]{:S(2)}) copy-start(bf16[208,896]{1,0:T(8,128)(2,1)S(1)} %constant_dynamic-update-slice_fusion.refs_2_) | copy-start | bytes 1118212
  47.8 2.5 %collective-permute-start.11 = (bf16[208,896]{1,0:T(8,128)(2,1)S(1)}, bf16[208,896]{1,0:T(8,128)(2,1)S(1)}, u32[]{:S(2)}, u32[]{:S(2)}) collective-permute-start(bf16[208,896]{1,0:T(8,128)(2,1)S(1)} %constant_dynamic-update-slice_fusion.refs_2_), channel_id=1, source_target_pairs={{0,16},{16,0},{1,17},{17,1},{2,18},{18,2},{3,19},{19,3},{4,20},{20... | collective-permute-start | bytes 1118216 | tf_op jit(solution)/shard_map/ppermute | solution.py:32
  50.3 0.8 copy-start.3
  154.6 3.5 %collective-permute-start.12 = (bf16[4,104,1552]{2,1,0:T(8,128)(2,1)}, bf16[4,104,1552]{2,1,0:T(8,128)(2,1)S(1)}, u32[]{:S(2)}, u32[]{:S(2)}) collective-permute-start(bf16[4,104,1552]{2,1,0:T(8,128)(2,1)} %get-tuple-element.50), channel_id=1, source_target_pairs={{0,16},{16,0},{1,17},{17,1},{2,18},{18,2},{3,19},{19,3},{4,20},{20... | collective-permute-start | bytes 3873800 | tf_op jit(solution)/shard_map/ppermute | solution.py:32
  161.3 21.6 %all-to-all-start = ((bf16[4,104,1552]{2,1,0:T(8,128)(2,1)}), bf16[4,104,1552]{2,1,0:T(8,128)(2,1)S(1)}, u32[]{:S(2)}, u32[]{:S(2)}) async-start(bf16[4,104,1552]{2,1,0:T(8,128)(2,1)} %add_convert_fusion), calls=%async_computation | async-start | bytes 2768896 | tf_op jit(solution)/shard_map/all_to_all | solution.py:690
  184.3 24.1 %all-to-all-start.1 = ((bf16[4,104,1552]{2,1,0:T(8,128)(2,1)}), bf16[4,104,1552]{2,1,0:T(8,128)(2,1)S(1)}, u32[]{:S(2)}, u32[]{:S(2)}) async-start(bf16[4,104,1552]{2,1,0:T(8,128)(2,1)} %broadcast_in_dim.33), calls=%async_computation.1 | async-start | bytes 2768896 | tf_op jit(solution)/shard_map/all_to_all | solution.py:701
  187.9 1.7 collective-permute-start.13
  192.7 4.4 %collective-permute-start.14 = (f32[2,2]{1,0:T(2,128)S(1)}, f32[2,2]{1,0:T(2,128)S(1)}, u32[]{:S(2)}, u32[]{:S(2)}) collective-permute-start(f32[2,2]{1,0:T(2,128)S(1)} %reshape.49), channel_id=1, source_target_pairs={{0,1},{1,0},{2,3},{3,2},{4,5},{5,4},{6,7},{7,6},{8,9},{9,8},{10,11... | collective-permute-start | bytes 56 | tf_op jit(solution)/shard_map/ppermute | solution.py:32
  193.0 4.5 %collective-permute-start.15 = (f32[2,2]{1,0:T(2,128)S(1)}, f32[2,2]{1,0:T(2,128)S(1)}, u32[]{:S(2)}, u32[]{:S(2)}) collective-permute-start(f32[2,2]{1,0:T(2,128)S(1)} %reshape.49), channel_id=1, source_target_pairs={{0,2},{1,3},{2,0},{3,1},{4,6},{5,7},{6,4},{7,5},{8,10},{9,11},{10,... | collective-permute-start | bytes 56 | tf_op jit(solution)/shard_map/ppermute | solution.py:32
  194.6 5.4 %collective-permute-start.16 = (f32[2,2]{1,0:T(2,128)S(1)}, f32[2,2]{1,0:T(2,128)S(1)}, u32[]{:S(2)}, u32[]{:S(2)}) collective-permute-start(f32[2,2]{1,0:T(2,128)S(1)} %reshape.49), channel_id=1, source_target_pairs={{0,3},{1,2},{2,1},{3,0},{4,7},{5,6},{6,5},{7,4},{8,11},{9,10},{10,... | collective-permute-start | bytes 56 | tf_op jit(solution)/shard_map/ppermute | solution.py:32
  200.0 5.1 %collective-permute-start.17 = (f32[2,2]{1,0:T(2,128)S(1)}, f32[2,2]{1,0:T(2,128)S(1)}, u32[]{:S(2)}, u32[]{:S(2)}) collective-permute-start(f32[2,2]{1,0:T(2,128)S(1)} %add_add_fusion.1), channel_id=1, source_target_pairs={{0,4},{4,0},{8,12},{12,8},{1,5},{5,1},{9,13},{13,9},{2,6},{6,2},{1... | collective-permute-start | bytes 56 | tf_op jit(solution)/shard_map/ppermute | solution.py:32
  201.9 3.6 %collective-permute-start.18 = (f32[2,2]{1,0:T(2,128)S(1)}, f32[2,2]{1,0:T(2,128)S(1)}, u32[]{:S(2)}, u32[]{:S(2)}) collective-permute-start(f32[2,2]{1,0:T(2,128)S(1)} %add_add_fusion.1), channel_id=1, source_target_pairs={{0,8},{4,12},{8,0},{12,4},{1,9},{5,13},{9,1},{13,5},{2,10},{6,14},... | collective-permute-start | bytes 56 | tf_op jit(solution)/shard_map/ppermute | solution.py:32
  203.4 4.5 %collective-permute-start.19 = (f32[2,2]{1,0:T(2,128)S(1)}, f32[2,2]{1,0:T(2,128)S(1)}, u32[]{:S(2)}, u32[]{:S(2)}) collective-permute-start(f32[2,2]{1,0:T(2,128)S(1)} %add_add_fusion.1), channel_id=1, source_target_pairs={{0,12},{4,8},{8,4},{12,0},{1,13},{5,9},{9,5},{13,1},{2,14},{6,10},... | collective-permute-start | bytes 56 | tf_op jit(solution)/shard_map/ppermute | solution.py:32

commit v3 on v2

--- a/solution.py
+++ b/solution.py
@@ -577,20 +577,24 @@
         name="forward",
     )(at, dropped, dropped, dropped, *sources)
 
+    back_steps = sub
+    back_blocks = time_steps // back_steps
+
     def back(b):
-        return blocks - 1 - b
+        return back_blocks - 1 - b
 
     def before(width):
         return pl.BlockSpec(
-            (1, seq_count, width), lambda b, *_: (jnp.maximum(back(b) * steps - 1, 0), 0, 0)
+            (1, seq_count, width), lambda b, *_: (jnp.maximum(back(b) * back_steps - 1, 0), 0, 0)
         )
 
     def back_time(width):
-        return pl.BlockSpec((steps, seq_count, width), lambda b, *_: (back(b), 0, 0))
+        return pl.BlockSpec((back_steps, seq_count, width), lambda b, *_: (back(b), 0, 0))
 
     def later_time(width):
         return pl.BlockSpec(
-            (steps, seq_count, width), lambda b, *_: (jnp.minimum(back(b) + 1, blocks - 1), 0, 0)
+            (back_steps, seq_count, width),
+            lambda b, *_: (jnp.minimum(back(b) + 1, back_blocks - 1), 0, 0),
         )
 
     part_rows = ceil_to(-(-row_count // seq_n), 8)
@@ -608,23 +612,23 @@
         own_specs = [
             later_time(wide),
             later_time(hidden),
-            fixed(steps, seq_count, wide),
-            fixed(steps, seq_count, hidden),
+            fixed(back_steps, seq_count, wide),
+            fixed(back_steps, seq_count, hidden),
             fixed(1, seq_count),
             fixed(row_count, hidden),
         ]
         own_arrays = [dropped, prev_low, dropped, prev_low, group_row, weight_mask]
         own_scratch = [
-            pltpu.VMEM((steps * seq_count, hidden), BF16),
-            pltpu.VMEM((2, hidden, steps * seq_count), BF16),
-            pltpu.VMEM((1, steps * seq_count), BF16),
+            pltpu.VMEM((back_steps * seq_count, hidden), BF16),
+            pltpu.VMEM((2, hidden, back_steps * seq_count), BF16),
+            pltpu.VMEM((1, back_steps * seq_count), BF16),
             sum_scratch,
         ]
     grads, *sums = pl.pallas_call(
         functools.partial(backward_kernel, cols, own),
         grid_spec=pltpu.PrefetchScalarGridSpec(
             num_scalar_prefetch=1,
-            grid=(blocks,),
+            grid=(back_blocks,),
             in_specs=[
                 back_time(cols.total),
                 back_time(hidden),

time: 212 us -> 209 us (0.986)
  Pallas kernels: 118 us -> 115 us
    pallas_call x1, Pallas kernels: 54 us -> 51 us  [local(): pl.pallas_call(functools.partial(backward_kernel, cols, own), grid_spec=p...]
where the time goes in v3:
time: 209 us
  Pallas kernels  115 us (55%)
  waiting for transfers between devices  30.8 us (15%)
  starting transfers between devices  29.2 us (14%)
  other arithmetic  13.5 us (6%)
  local copies, waits for them, and re-layouts  9.81 us (5%)
  matrix products  9.77 us (5%)
    pallas_call x1, Pallas kernels, local(): pl.pallas_call(functools.partial(backward_kernel, cols, own), grid_spec=p...  51 us
    pallas_call x1, Pallas kernels, local(): pl.pallas_call(functools.partial(forward_kernel, cols, plan, sub, pieced)...  49.5 us
    ppermute x20, waiting for transfers between devices, flip(): return lax.ppermute(block, axis, [(at, at ^ bit) for at in range(count)])  25.9 us
    ppermute x20, starting transfers between devices, flip(): return lax.ppermute(block, axis, [(at, at ^ bit) for at in range(count)])  22.1 us
    pallas_call x1, Pallas kernels, local(): pl.pallas_call(functools.partial(drop_kernel, width_in), grid=(blocks,),...  10.4 us
    dot_general x1, matrix products, local(): jnp.einsum('tsr,rk->tsk', own_seqs, w_in, preferred_element_type=F32)  9.77 us
    all_to_all x1, waiting for transfers between devices, local(): swapped = lax.all_to_all(block, 'seq', 0, 0, tiled=True)  4.96 us
  transfers between devices with their start and end apart: 22, of which 12 were waited for; matrix products, arithmetic and copies ran while one was open for 11% of the time, Pallas kernels for 5%

profile of v3, /device:TPU:0, one launch (start us, length us, event | category | flops | bytes accessed | tf_op | source)
XLA Modules:
  0.0 208.7 jit_solution(3595550345622400187)
XLA Ops:
  0.6 0.7 pad_add_fusion.at_ref
  1.3 3.9 %shard.1 = (bf16[400,1664]{1,0:T(8,128)(2,1)}, bf16[208,896]{1,0:T(8,128)(2,1)}) custom-call(s32[3]{0:T(128)} %pad_add_fusion.at_ref, bf16[400,1150]{1,0:T(8,128)(2,1)} %in_ref.1, bf16[400,400]{1,0:T(8,128)(2,1)} %rec_ref.1, s32[400,400]{1,0:T(8,128)} %refs_5_.1, f32[1,400]{1,0:T(1,128)} %bitcast.51), custom_call_target="tpu_custom_call" | custom-call | tf_op jit(solution)/shard_map/shard/pallas_call | solution.py:489
  5.2 3.0 %collective-permute-start = (bf16[208,896]{1,0:T(8,128)(2,1)}, bf16[208,896]{1,0:T(8,128)(2,1)S(1)}, u32[]{:S(2)}, u32[]{:S(2)}) collective-permute-start(bf16[208,896]{1,0:T(8,128)(2,1)} %get-tuple-element.31), channel_id=1, source_target_pairs={{0,1},{1,0},{2,3},{3,2},{4,5},{5,4},{6,7},{7,6},{8,9},{9,8},{10,11... | collective-permute-start | bytes 1118216 | tf_op jit(solution)/shard_map/ppermute | solution.py:32
  8.2 2.6 %collective-permute-start.1 = (bf16[208,896]{1,0:T(8,128)(2,1)}, bf16[208,896]{1,0:T(8,128)(2,1)S(1)}, u32[]{:S(2)}, u32[]{:S(2)}) collective-permute-start(bf16[208,896]{1,0:T(8,128)(2,1)} %get-tuple-element.31), channel_id=1, source_target_pairs={{0,2},{1,3},{2,0},{3,1},{4,6},{5,7},{6,4},{7,5},{8,10},{9,11},{10,... | collective-permute-start | bytes 1118216 | tf_op jit(solution)/shard_map/ppermute | solution.py:32
  10.8 1.2 convert_bitcast_fusion.1
  12.1 0.8 select_reduce_fusion.1
  12.8 0.1 collective-permute-start.2
  12.9 10.4 %drop.1.first_ref.second_ref.third_ref.refs_0_.refs_2_ = bf16[70,64,1152]{2,1,0:T(8,128)(2,1)} custom-call(bf16[70,64,1150]{2,1,0:T(8,128)(2,1)} %bitcast.34, s32[64,1150]{1,0:T(8,128)} %mask_ref.4), custom_call_target="tpu_custom_call" | custom-call | tf_op jit(solution)/shard_map/drop/pallas_call | solution.py:514
  23.3 1.7 collective-permute-done
  25.0 2.5 %collective-permute-done.1 = bf16[208,896]{1,0:T(8,128)(2,1)S(1)} collective-permute-done((bf16[208,896]{1,0:T(8,128)(2,1)}, bf16[208,896]{1,0:T(8,128)(2,1)S(1)}, u32[]{:S(2)}, u32[]{:S(2)}) %collective-permute-start.1) | collective-permute-done | bytes 372768 | tf_op jit(solution)/shard_map/ppermute | solution.py:32
  27.5 0.4 collective-permute-start.5
  28.0 1.6 collective-permute-start.3
  29.6 1.6 collective-permute-start.4
  31.2 0.5 collective-permute-start.6
  31.7 0.1 pad_maximum_fusion.1
  31.8 6.1 %collective-permute-done.6 = f32[2]{0:T(128)S(1)} collective-permute-done((f32[2]{0:T(128)S(1)}, f32[2]{0:T(128)S(1)}, u32[]{:S(2)}, u32[]{:S(2)}) %collective-permute-start.6) | collective-permute-done | bytes 40 | tf_op jit(solution)/shard_map/ppermute | solution.py:32
  38.0 0.1 pad_maximum_fusion.refs_1_
  38.2 0.1 collective-permute-start.9
  38.3 1.6 collective-permute-start.7
  39.8 1.6 collective-permute-start.8
  41.4 0.5 collective-permute-start.10
  41.9 4.5 %collective-permute-done.10 = f32[2]{0:T(128)S(1)} collective-permute-done((f32[2]{0:T(128)S(1)}, f32[2]{0:T(128)S(1)}, u32[]{:S(2)}, u32[]{:S(2)}) %collective-permute-start.10) | collective-permute-done | bytes 40 | tf_op jit(solution)/shard_map/ppermute | solution.py:32
  46.5 1.2 copy-done.1
  47.8 0.1 collective-permute-start.11
  47.9 0.5 convert_bitcast_fusion.refs_4_
  48.4 0.6 reduce_sum.67
  49.0 0.6 broadcast_divide_fusion
  49.7 0.7 select_reduce_fusion
  50.3 0.7 copy-done.3
  51.1 49.5 %forward.1 = (f32[70,64,1600]{2,1,0:T(8,128)}, f32[70,64,400]{2,1,0:T(8,128)}, bf16[70,64,400]{2,1,0:T(8,128)(2,1)}, bf16[4,400,1152]{2,1,0:T(8,128)(2,1)}, bf16[4,400,512]{2,1,0:T(8,128)(2,1)}) custom-call(s32[3]{0:T(128)} %pad_add_fusion.at_ref, bf16[70,64,1152]{2,1,0:T(8,128)(2,1)} %drop.1.first_ref.second_ref.third_ref.refs_0_.refs_2_, ...), custom_call_target="tpu_custom_call" | custom-call | tf_op jit(solution)/shard_map/forward/pallas_call | solution.py:538
  100.6 51.0 %backward.1 = (bf16[70,64,1600]{2,1,0:T(8,128)(2,1)}, f32[4,104,1552]{2,1,0:T(8,128)}, bf16[4,104,1552]{2,1,0:T(8,128)(2,1)}) custom-call(s32[3]{0:T(128)} %pad_add_fusion.at_ref, f32[70,64,1600]{2,1,0:T(8,128)} %get-tuple-element.44.act_ref.act_before_ref, f32[70,64,400]{2,1,0:T(8,128)} %get-tuple-element.45.cell_ref.before_ref, ...), custom_call_target="tpu_custom_call" | custom-call | tf_op jit(solution)/shard_map/backward/pallas_call | solution.py:627
  151.5 0.5 collective-permute-start.12
  152.1 0.9 convert_multiply_fusion
  153.0 2.1 collective-permute-done.12
  155.1 3.2 %add_convert_fusion = bf16[4,104,1552]{2,1,0:T(8,128)(2,1)} fusion(f32[4,104,1552]{2,1,0:T(8,128)} %get-tuple-element.49, bf16[4,104,1552]{2,1,0:T(8,128)(2,1)S(1)} %collective-permute-done.12), kind=kLoop, calls=%fused_computation.9 | loop fusion | flops 1936896 | bytes 5165056 | tf_op jit(solution)/shard_map/convert_element_type | solution.py:693
  158.2 3.5 %all-to-all-start = ((bf16[4,104,1552]{2,1,0:T(8,128)(2,1)}), bf16[4,104,1552]{2,1,0:T(8,128)(2,1)S(1)}, u32[]{:S(2)}, u32[]{:S(2)}) async-start(bf16[4,104,1552]{2,1,0:T(8,128)(2,1)} %add_convert_fusion), calls=%async_computation | async-start | bytes 2768896 | tf_op jit(solution)/shard_map/all_to_all | solution.py:694
  161.8 2.3 %fusion.11 = (bf16[4,128,1150]{2,1,0:T(8,128)(2,1)S(1)}, bf16[4,128,1150]{2,1,0:T(8,128)(2,1)S(1)}, bf16[4,128,1150]{2,1,0:T(8,128)(2,1)S(1)}) fusion(bf16[4,400,1152]{2,1,0:T(8,128)(2,1)} %get-tuple-element.52), kind=kLoop, calls=%fused_computation.45 | loop fusion | bytes 7065600 | tf_op jit(solution)/shard_map/slice | solution.py:73
  164.1 0.9 slice.60
  165.1 9.8 %multiply_bitcast_fusion = f32[16,70,1150]{2,0,1:T(8,128)} fusion(bf16[70,64,1600]{2,1,0:T(8,128)(2,1)} %get-tuple-element.51, s32[]{:T(128)S(6)} %select_n.16, bf16[64,1150]{1,0:T(8,128)(2,1)S(1)} %bitcast.49, bf16[512,1150]{1,0:T(8,128)(2,1)S(1)} %bitcast.45, bf16[512,1150]{1,0:T(8,128)(2,1)S(1)} %bitcast.46, bf16[512,1150]{1,0:T(8,128)(2,1)S(1)} %bitcast.44, ...), kind=kOutput, calls=%fused_computation | convolution fusion | flops 4137607936 | bytes 12632964 | tf_op jit(solution)/shard_map/tsr,rk->tsk/dot_general | solution.py:699
  174.8 5.0 %all-to-all-done = bf16[4,104,1552]{2,1,0:T(8,128)(2,1)S(1)} async-done(((bf16[4,104,1552]{2,1,0:T(8,128)(2,1)}), bf16[4,104,1552]{2,1,0:T(8,128)(2,1)S(1)}, u32[]{:S(2)}, u32[]{:S(2)}) %all-to-all-start) | async-done | bytes 1291296 | tf_op jit(solution)/shard_map/all_to_all | solution.py:694
  179.8 0.2 reduce_sum.69
  180.0 1.2 broadcast_in_dim.33
  181.2 3.5 %all-to-all-start.1 = ((bf16[4,104,1552]{2,1,0:T(8,128)(2,1)}), bf16[4,104,1552]{2,1,0:T(8,128)(2,1)S(1)}, u32[]{:S(2)}, u32[]{:S(2)}) async-start(bf16[4,104,1552]{2,1,0:T(8,128)(2,1)} %broadcast_in_dim.33), calls=%async_computation.1 | async-start | bytes 2768896 | tf_op jit(solution)/shard_map/all_to_all | solution.py:705
  184.8 0.1 collective-permute-start.13
  184.9 1.6 collective-permute-done.13
  186.5 1.0 multiply_reduce_fusion.2
  187.5 2.0 pad_maximum_fusion.4
  189.5 0.1 reshape.49
  189.6 0.3 collective-permute-start.14
  189.9 1.6 collective-permute-start.15
  191.5 2.5 %collective-permute-start.16 = (f32[2,2]{1,0:T(2,128)S(1)}, f32[2,2]{1,0:T(2,128)S(1)}, u32[]{:S(2)}, u32[]{:S(2)}) collective-permute-start(f32[2,2]{1,0:T(2,128)S(1)} %reshape.49), channel_id=1, source_target_pairs={{0,3},{1,2},{2,1},{3,0},{4,7},{5,6},{6,5},{7,4},{8,11},{9,10},{10,... | collective-permute-start | bytes 56 | tf_op jit(solution)/shard_map/ppermute | solution.py:32
  194.0 0.4 collective-permute-done.15
  194.4 2.5 %collective-permute-done.16 = f32[2,2]{1,0:T(2,128)S(1)} collective-permute-done((f32[2,2]{1,0:T(2,128)S(1)}, f32[2,2]{1,0:T(2,128)S(1)}, u32[]{:S(2)}, u32[]{:S(2)}) %collective-permute-start.16) | collective-permute-done | bytes 48 | tf_op jit(solution)/shard_map/ppermute | solution.py:32
  196.9 1.9 collective-permute-start.17
  198.8 1.5 collective-permute-start.18
  200.3 0.1 collective-permute-start.19
  200.4 1.6 collective-permute-done.17
  202.0 0.4 collective-permute-done.18
  202.4 2.4 %collective-permute-done.19 = f32[2,2]{1,0:T(2,128)S(1)} collective-permute-done((f32[2,2]{1,0:T(2,128)S(1)}, f32[2,2]{1,0:T(2,128)S(1)}, u32[]{:S(2)}, u32[]{:S(2)}) %collective-permute-start.19) | collective-permute-done | bytes 48 | tf_op jit(solution)/shard_map/ppermute | solution.py:32
  204.8 0.6 add_add_fusion
  205.3 0.2 slice_convert_fusion
  205.5 1.4 slice_bitcast_fusion
  206.9 1.0 slice_bitcast_fusion.1
  207.8 0.8 slice_reduce_fusion
  (32 shorter events, 0.3 us)
Async XLA Ops:
  5.2 19.8 %collective-permute-start = (bf16[208,896]{1,0:T(8,128)(2,1)}, bf16[208,896]{1,0:T(8,128)(2,1)S(1)}, u32[]{:S(2)}, u32[]{:S(2)}) collective-permute-start(bf16[208,896]{1,0:T(8,128)(2,1)} %get-tuple-element.31), channel_id=1, source_target_pairs={{0,1},{1,0},{2,3},{3,2},{4,5},{5,4},{6,7},{7,6},{8,9},{9,8},{10,11... | collective-permute-start | bytes 1118216 | tf_op jit(solution)/shard_map/ppermute | solution.py:32
  8.2 19.3 %collective-permute-start.1 = (bf16[208,896]{1,0:T(8,128)(2,1)}, bf16[208,896]{1,0:T(8,128)(2,1)S(1)}, u32[]{:S(2)}, u32[]{:S(2)}) collective-permute-start(bf16[208,896]{1,0:T(8,128)(2,1)} %get-tuple-element.31), channel_id=1, source_target_pairs={{0,2},{1,3},{2,0},{3,1},{4,6},{5,7},{6,4},{7,5},{8,10},{9,11},{10,... | collective-permute-start | bytes 1118216 | tf_op jit(solution)/shard_map/ppermute | solution.py:32
  12.8 10.5 %collective-permute-start.2 = (f32[2]{0:T(128)S(1)}, f32[2]{0:T(128)S(1)}, u32[]{:S(2)}, u32[]{:S(2)}) collective-permute-start(f32[2]{0:T(128)S(1)} %select_reduce_fusion.1), channel_id=1, source_target_pairs={{0,16},{16,0},{1,17},{17,1},{2,18},{18,2},{3,19},{19,3},{4,20},{20... | collective-permute-start | bytes 32 | tf_op jit(solution)/shard_map/ppermute | solution.py:32
  27.5 10.5 %collective-permute-start.5 = (bf16[208,896]{1,0:T(8,128)(2,1)S(1)}, bf16[208,896]{1,0:T(8,128)(2,1)S(1)}, u32[]{:S(2)}, u32[]{:S(2)}) collective-permute-start(bf16[208,896]{1,0:T(8,128)(2,1)S(1)} %collective-permute-done.1), channel_id=1, source_target_pairs={{0,1},{1,0},{2,3},{3,2},{4,5},{5,4},{6,7},{7,6},{8,9},{9,8},{10,11... | collective-permute-start | bytes 1118216 | tf_op jit(solution)/shard_map/ppermute | solution.py:32
  28.0 10.0 %collective-permute-start.3 = (bf16[2,112,896]{2,1,0:T(8,128)(2,1)S(1)}, bf16[2,112,896]{2,1,0:T(8,128)(2,1)S(1)}, u32[]{:S(2)}, u32[]{:S(2)}) collective-permute-start(bf16[2,112,896]{2,1,0:T(8,128)(2,1)S(1)} %fusion.7), channel_id=1, source_target_pairs={{0,4},{4,0},{8,12},{12,8},{1,5},{5,1},{9,13},{13,9},{2,6},{6,2},{1... | collective-permute-start | bytes 1204232 | tf_op jit(solution)/shard_map/ppermute | solution.py:32
  29.6 8.4 %collective-permute-start.4 = (bf16[2,96,896]{2,1,0:T(8,128)(2,1)S(1)}, bf16[2,96,896]{2,1,0:T(8,128)(2,1)S(1)}, u32[]{:S(2)}, u32[]{:S(2)}) collective-permute-start(bf16[2,96,896]{2,1,0:T(8,128)(2,1)S(1)} %fusion.8), channel_id=1, source_target_pairs={{0,8},{4,12},{8,0},{12,4},{1,9},{5,13},{9,1},{13,5},{2,10},{6,14},... | collective-permute-start | bytes 1032200 | tf_op jit(solution)/shard_map/ppermute | solution.py:32
  31.2 6.8 %collective-permute-start.6 = (f32[2]{0:T(128)S(1)}, f32[2]{0:T(128)S(1)}, u32[]{:S(2)}, u32[]{:S(2)}) collective-permute-start(f32[2]{0:T(128)S(1)} %add.34), channel_id=1, source_target_pairs={{0,4},{4,0},{8,12},{12,8},{1,5},{5,1},{9,13},{13,9},{2,6},{6,2},{1... | collective-permute-start | bytes 32 | tf_op jit(solution)/shard_map/ppermute | solution.py:32
  31.8 16.0 %copy-start.4 = (s32[64]{0:T(128)S(1)}, s32[64]{0:T(128)}, u32[]{:S(2)}) copy-start(s32[64]{0:T(128)} %param.14) | copy-start | bytes 772
  38.1 12.2 %copy-start = (bf16[1040,896]{1,0:T(8,128)(2,1)}, bf16[1040,896]{1,0:T(8,128)(2,1)S(1)}, u32[]{:S(2)}) copy-start(bf16[1040,896]{1,0:T(8,128)(2,1)S(1)} %pad_maximum_fusion.refs_1_) | copy-start | bytes 5591044
  38.2 8.3 %collective-permute-start.9 = (bf16[1040,896]{1,0:T(8,128)(2,1)S(1)}, bf16[1040,896]{1,0:T(8,128)(2,1)S(1)}, u32[]{:S(2)}, u32[]{:S(2)}) collective-permute-start(bf16[1040,896]{1,0:T(8,128)(2,1)S(1)} %pad_maximum_fusion.refs_1_), channel_id=1, source_target_pairs={{0,16},{16,0},{1,17},{17,1},{2,18},{18,2},{3,19},{19,3},{4,20},{20... | collective-permute-start | bytes 5591048 | tf_op jit(solution)/shard_map/ppermute | solution.py:32
  38.3 8.2 %collective-permute-start.7 = (bf16[112,896]{1,0:T(8,128)(2,1)S(1)}, bf16[112,896]{1,0:T(8,128)(2,1)S(1)}, u32[]{:S(2)}, u32[]{:S(2)}) collective-permute-start(bf16[112,896]{1,0:T(8,128)(2,1)S(1)} %slice.55), channel_id=1, source_target_pairs={{0,4},{4,0},{8,12},{12,8},{1,5},{5,1},{9,13},{13,9},{2,6},{6,2},{1... | collective-permute-start | bytes 602120 | tf_op jit(solution)/shard_map/ppermute | solution.py:32
  39.8 6.6 %collective-permute-start.8 = (bf16[96,896]{1,0:T(8,128)(2,1)S(1)}, bf16[96,896]{1,0:T(8,128)(2,1)S(1)}, u32[]{:S(2)}, u32[]{:S(2)}) collective-permute-start(bf16[96,896]{1,0:T(8,128)(2,1)S(1)} %slice.56), channel_id=1, source_target_pairs={{0,8},{4,12},{8,0},{12,4},{1,9},{5,13},{9,1},{13,5},{2,10},{6,14},... | collective-permute-start | bytes 516104 | tf_op jit(solution)/shard_map/ppermute | solution.py:32
  41.4 5.0 %collective-permute-start.10 = (f32[2]{0:T(128)S(1)}, f32[2]{0:T(128)S(1)}, u32[]{:S(2)}, u32[]{:S(2)}) collective-permute-start(f32[2]{0:T(128)S(1)} %add.35), channel_id=1, source_target_pairs={{0,8},{4,12},{8,0},{12,4},{1,9},{5,13},{9,1},{13,5},{2,10},{6,14},... | collective-permute-start | bytes 32 | tf_op jit(solution)/shard_map/ppermute | solution.py:32
  46.5 1.2 copy-start.1
  47.8 2.6 %copy-start.2 = (bf16[208,896]{1,0:T(8,128)(2,1)}, bf16[208,896]{1,0:T(8,128)(2,1)S(1)}, u32[]{:S(2)}) copy-start(bf16[208,896]{1,0:T(8,128)(2,1)S(1)} %constant_dynamic-update-slice_fusion.refs_2_) | copy-start | bytes 1118212
  47.8 2.5 %collective-permute-start.11 = (bf16[208,896]{1,0:T(8,128)(2,1)S(1)}, bf16[208,896]{1,0:T(8,128)(2,1)S(1)}, u32[]{:S(2)}, u32[]{:S(2)}) collective-permute-start(bf16[208,896]{1,0:T(8,128)(2,1)S(1)} %constant_dynamic-update-slice_fusion.refs_2_), channel_id=1, source_target_pairs={{0,16},{16,0},{1,17},{17,1},{2,18},{18,2},{3,19},{19,3},{4,20},{20... | collective-permute-start | bytes 1118216 | tf_op jit(solution)/shard_map/ppermute | solution.py:32
  50.3 0.8 copy-start.3
  151.5 3.5 %collective-permute-start.12 = (bf16[4,104,1552]{2,1,0:T(8,128)(2,1)}, bf16[4,104,1552]{2,1,0:T(8,128)(2,1)S(1)}, u32[]{:S(2)}, u32[]{:S(2)}) collective-permute-start(bf16[4,104,1552]{2,1,0:T(8,128)(2,1)} %get-tuple-element.50), channel_id=1, source_target_pairs={{0,16},{16,0},{1,17},{17,1},{2,18},{18,2},{3,19},{19,3},{4,20},{20... | collective-permute-start | bytes 3873800 | tf_op jit(solution)/shard_map/ppermute | solution.py:32
  158.2 21.6 %all-to-all-start = ((bf16[4,104,1552]{2,1,0:T(8,128)(2,1)}), bf16[4,104,1552]{2,1,0:T(8,128)(2,1)S(1)}, u32[]{:S(2)}, u32[]{:S(2)}) async-start(bf16[4,104,1552]{2,1,0:T(8,128)(2,1)} %add_convert_fusion), calls=%async_computation | async-start | bytes 2768896 | tf_op jit(solution)/shard_map/all_to_all | solution.py:694
  181.2 24.1 %all-to-all-start.1 = ((bf16[4,104,1552]{2,1,0:T(8,128)(2,1)}), bf16[4,104,1552]{2,1,0:T(8,128)(2,1)S(1)}, u32[]{:S(2)}, u32[]{:S(2)}) async-start(bf16[4,104,1552]{2,1,0:T(8,128)(2,1)} %broadcast_in_dim.33), calls=%async_computation.1 | async-start | bytes 2768896 | tf_op jit(solution)/shard_map/all_to_all | solution.py:705
  184.8 1.7 collective-permute-start.13
  189.6 4.4 %collective-permute-start.14 = (f32[2,2]{1,0:T(2,128)S(1)}, f32[2,2]{1,0:T(2,128)S(1)}, u32[]{:S(2)}, u32[]{:S(2)}) collective-permute-start(f32[2,2]{1,0:T(2,128)S(1)} %reshape.49), channel_id=1, source_target_pairs={{0,1},{1,0},{2,3},{3,2},{4,5},{5,4},{6,7},{7,6},{8,9},{9,8},{10,11... | collective-permute-start | bytes 56 | tf_op jit(solution)/shard_map/ppermute | solution.py:32
  189.9 4.5 %collective-permute-start.15 = (f32[2,2]{1,0:T(2,128)S(1)}, f32[2,2]{1,0:T(2,128)S(1)}, u32[]{:S(2)}, u32[]{:S(2)}) collective-permute-start(f32[2,2]{1,0:T(2,128)S(1)} %reshape.49), channel_id=1, source_target_pairs={{0,2},{1,3},{2,0},{3,1},{4,6},{5,7},{6,4},{7,5},{8,10},{9,11},{10,... | collective-permute-start | bytes 56 | tf_op jit(solution)/shard_map/ppermute | solution.py:32
  191.5 5.4 %collective-permute-start.16 = (f32[2,2]{1,0:T(2,128)S(1)}, f32[2,2]{1,0:T(2,128)S(1)}, u32[]{:S(2)}, u32[]{:S(2)}) collective-permute-start(f32[2,2]{1,0:T(2,128)S(1)} %reshape.49), channel_id=1, source_target_pairs={{0,3},{1,2},{2,1},{3,0},{4,7},{5,6},{6,5},{7,4},{8,11},{9,10},{10,... | collective-permute-start | bytes 56 | tf_op jit(solution)/shard_map/ppermute | solution.py:32
  196.9 5.1 %collective-permute-start.17 = (f32[2,2]{1,0:T(2,128)S(1)}, f32[2,2]{1,0:T(2,128)S(1)}, u32[]{:S(2)}, u32[]{:S(2)}) collective-permute-start(f32[2,2]{1,0:T(2,128)S(1)} %add_add_fusion.1), channel_id=1, source_target_pairs={{0,4},{4,0},{8,12},{12,8},{1,5},{5,1},{9,13},{13,9},{2,6},{6,2},{1... | collective-permute-start | bytes 56 | tf_op jit(solution)/shard_map/ppermute | solution.py:32
  198.8 3.6 %collective-permute-start.18 = (f32[2,2]{1,0:T(2,128)S(1)}, f32[2,2]{1,0:T(2,128)S(1)}, u32[]{:S(2)}, u32[]{:S(2)}) collective-permute-start(f32[2,2]{1,0:T(2,128)S(1)} %add_add_fusion.1), channel_id=1, source_target_pairs={{0,8},{4,12},{8,0},{12,4},{1,9},{5,13},{9,1},{13,5},{2,10},{6,14},... | collective-permute-start | bytes 56 | tf_op jit(solution)/shard_map/ppermute | solution.py:32
  200.3 4.5 %collective-permute-start.19 = (f32[2,2]{1,0:T(2,128)S(1)}, f32[2,2]{1,0:T(2,128)S(1)}, u32[]{:S(2)}, u32[]{:S(2)}) collective-permute-start(f32[2,2]{1,0:T(2,128)S(1)} %add_add_fusion.1), channel_id=1, source_target_pairs={{0,12},{4,8},{8,4},{12,0},{1,13},{5,9},{9,5},{13,1},{2,14},{6,10},... | collective-permute-start | bytes 56 | tf_op jit(solution)/shard_map/ppermute | solution.py:32

commit v4 on v3

--- a/solution.py
+++ b/solution.py
@@ -712,8 +712,10 @@
     second = jnp.where(grp_at == 0, theirs, ours)
     dots = [jnp.sum(a * b) for a, b in ((first, first), (first, second), (second, second))]
     gram = jnp.stack([dots[0], dots[1], dots[1], dots[2]]).reshape(2, 2)
-    gram = exchange_sum(exchange_sum(gram, "row"), "seq")
-    parts, gram = hold((parts, gram))
+    gram = exchange_sum(gram, "row")
+    first, *rest = [flip(gram, "seq", bit) for bit in range(1, seq_n)]
+    parts, first = hold((parts, first))
+    gram = (gram + first) + (rest[0] + rest[1])
     everyone = parts.reshape(seq_n * part_rows, wide + hidden)[:row_count].astype(F32)
     return (
         input_grad,

time: 209 us -> 207 us (level)
  waiting for transfers between devices: 30.8 us -> 28.1 us
    ppermute x20, waiting for transfers between devices: 25.9 us -> 23.2 us  [flip(): return lax.ppermute(block, axis, [(at, at ^ bit) for at in range(count)])]
  transfers between devices with their start and end apart: 22 -> 22, of which waited for: 12 -> 10; matrix products, arithmetic and copies ran while one was open for 11% -> 12% of each run, Pallas kernels for 5% -> 5%
where the time goes in v4:
time: 207 us; the launch traced here: 206 us
  Pallas kernels  115 us (56%)
  starting transfers between devices  29.2 us (14%)
  waiting for transfers between devices  28.1 us (14%)
  other arithmetic  13.5 us (7%)
  local copies, waits for them, and re-layouts  9.81 us (5%)
  matrix products  9.77 us (5%)
    pallas_call x1, Pallas kernels, local(): pl.pallas_call(functools.partial(backward_kernel, cols, own), grid_spec=p...  51 us
    pallas_call x1, Pallas kernels, local(): pl.pallas_call(functools.partial(forward_kernel, cols, plan, sub, pieced)...  49.5 us
    ppermute x20, waiting for transfers between devices, flip(): return lax.ppermute(block, axis, [(at, at ^ bit) for at in range(count)])  23.2 us
    ppermute x20, starting transfers between devices, flip(): return lax.ppermute(block, axis, [(at, at ^ bit) for at in range(count)])  22.1 us
    pallas_call x1, Pallas kernels, local(): pl.pallas_call(functools.partial(drop_kernel, width_in), grid=(blocks,),...  10.4 us
    dot_general x1, matrix products, local(): jnp.einsum('tsr,rk->tsk', own_seqs, w_in, preferred_element_type=F32)  9.77 us
    all_to_all x1, waiting for transfers between devices, local(): swapped = lax.all_to_all(block, 'seq', 0, 0, tiled=True)  4.96 us
  transfers between devices with their start and end apart: 22, of which 10 were waited for; matrix products, arithmetic and copies ran while one was open for 12% of the time, Pallas kernels for 5%

profile of v4, /device:TPU:0, one launch (start us, length us, event | category | flops | bytes accessed | tf_op | source)
XLA Modules:
  0.0 206.0 jit_solution(13242082971981723563)
XLA Ops:
  0.6 0.7 pad_add_fusion.at_ref
  1.3 3.9 %shard.1 = (bf16[400,1664]{1,0:T(8,128)(2,1)}, bf16[208,896]{1,0:T(8,128)(2,1)}) custom-call(s32[3]{0:T(128)} %pad_add_fusion.at_ref, bf16[400,1150]{1,0:T(8,128)(2,1)} %in_ref.1, bf16[400,400]{1,0:T(8,128)(2,1)} %rec_ref.1, s32[400,400]{1,0:T(8,128)} %refs_5_.1, f32[1,400]{1,0:T(1,128)} %bitcast.51), custom_call_target="tpu_custom_call" | custom-call | tf_op jit(solution)/shard_map/shard/pallas_call | solution.py:489
  5.2 3.0 %collective-permute-start = (bf16[208,896]{1,0:T(8,128)(2,1)}, bf16[208,896]{1,0:T(8,128)(2,1)S(1)}, u32[]{:S(2)}, u32[]{:S(2)}) collective-permute-start(bf16[208,896]{1,0:T(8,128)(2,1)} %get-tuple-element.31), channel_id=1, source_target_pairs={{0,1},{1,0},{2,3},{3,2},{4,5},{5,4},{6,7},{7,6},{8,9},{9,8},{10,11... | collective-permute-start | bytes 1118216 | tf_op jit(solution)/shard_map/ppermute | solution.py:32
  8.2 2.6 %collective-permute-start.1 = (bf16[208,896]{1,0:T(8,128)(2,1)}, bf16[208,896]{1,0:T(8,128)(2,1)S(1)}, u32[]{:S(2)}, u32[]{:S(2)}) collective-permute-start(bf16[208,896]{1,0:T(8,128)(2,1)} %get-tuple-element.31), channel_id=1, source_target_pairs={{0,2},{1,3},{2,0},{3,1},{4,6},{5,7},{6,4},{7,5},{8,10},{9,11},{10,... | collective-permute-start | bytes 1118216 | tf_op jit(solution)/shard_map/ppermute | solution.py:32
  10.8 1.2 convert_bitcast_fusion.1
  12.1 0.8 select_reduce_fusion.1
  12.8 0.1 collective-permute-start.2
  12.9 10.4 %drop.1.first_ref.second_ref.third_ref.refs_0_.refs_2_ = bf16[70,64,1152]{2,1,0:T(8,128)(2,1)} custom-call(bf16[70,64,1150]{2,1,0:T(8,128)(2,1)} %bitcast.34, s32[64,1150]{1,0:T(8,128)} %mask_ref.4), custom_call_target="tpu_custom_call" | custom-call | tf_op jit(solution)/shard_map/drop/pallas_call | solution.py:514
  23.3 1.7 collective-permute-done
  25.0 2.5 %collective-permute-done.1 = bf16[208,896]{1,0:T(8,128)(2,1)S(1)} collective-permute-done((bf16[208,896]{1,0:T(8,128)(2,1)}, bf16[208,896]{1,0:T(8,128)(2,1)S(1)}, u32[]{:S(2)}, u32[]{:S(2)}) %collective-permute-start.1) | collective-permute-done | bytes 372768 | tf_op jit(solution)/shard_map/ppermute | solution.py:32
  27.5 0.4 collective-permute-start.5
  28.0 1.6 collective-permute-start.3
  29.6 1.6 collective-permute-start.4
  31.2 0.5 collective-permute-start.6
  31.7 0.1 pad_maximum_fusion.1
  31.8 0.0 copy-start.4
  31.8 6.1 %collective-permute-done.6 = f32[2]{0:T(128)S(1)} collective-permute-done((f32[2]{0:T(128)S(1)}, f32[2]{0:T(128)S(1)}, u32[]{:S(2)}, u32[]{:S(2)}) %collective-permute-start.6) | collective-permute-done | bytes 40 | tf_op jit(solution)/shard_map/ppermute | solution.py:32
  38.0 0.0 collective-permute-done.4
  38.0 0.1 pad_maximum_fusion.refs_1_
  38.2 0.1 collective-permute-start.9
  38.3 1.6 collective-permute-start.7
  39.8 1.6 collective-permute-start.8
  41.4 0.5 collective-permute-start.10
  41.9 4.5 %collective-permute-done.10 = f32[2]{0:T(128)S(1)} collective-permute-done((f32[2]{0:T(128)S(1)}, f32[2]{0:T(128)S(1)}, u32[]{:S(2)}, u32[]{:S(2)}) %collective-permute-start.10) | collective-permute-done | bytes 40 | tf_op jit(solution)/shard_map/ppermute | solution.py:32
  46.5 1.2 copy-done.1
  47.8 0.1 collective-permute-start.11
  47.9 0.5 convert_bitcast_fusion.refs_4_
  48.4 0.6 reduce_sum.67
  49.0 0.6 broadcast_divide_fusion
  49.7 0.7 select_reduce_fusion
  50.3 0.7 copy-done.3
  51.1 49.5 %forward.1 = (f32[70,64,1600]{2,1,0:T(8,128)}, f32[70,64,400]{2,1,0:T(8,128)}, bf16[70,64,400]{2,1,0:T(8,128)(2,1)}, bf16[4,400,1152]{2,1,0:T(8,128)(2,1)}, bf16[4,400,512]{2,1,0:T(8,128)(2,1)}) custom-call(s32[3]{0:T(128)} %pad_add_fusion.at_ref, bf16[70,64,1152]{2,1,0:T(8,128)(2,1)} %drop.1.first_ref.second_ref.third_ref.refs_0_.refs_2_, ...), custom_call_target="tpu_custom_call" | custom-call | tf_op jit(solution)/shard_map/forward/pallas_call | solution.py:538
  100.6 51.0 %backward.1 = (bf16[70,64,1600]{2,1,0:T(8,128)(2,1)}, f32[4,104,1552]{2,1,0:T(8,128)}, bf16[4,104,1552]{2,1,0:T(8,128)(2,1)}) custom-call(s32[3]{0:T(128)} %pad_add_fusion.at_ref, f32[70,64,1600]{2,1,0:T(8,128)} %get-tuple-element.44.act_ref.act_before_ref, f32[70,64,400]{2,1,0:T(8,128)} %get-tuple-element.45.cell_ref.before_ref, ...), custom_call_target="tpu_custom_call" | custom-call | tf_op jit(solution)/shard_map/backward/pallas_call | solution.py:627
  151.5 0.5 collective-permute-start.12
  152.1 0.9 convert_multiply_fusion
  153.0 2.1 %collective-permute-done.12 = bf16[4,104,1552]{2,1,0:T(8,128)(2,1)S(1)} collective-permute-done((bf16[4,104,1552]{2,1,0:T(8,128)(2,1)}, bf16[4,104,1552]{2,1,0:T(8,128)(2,1)S(1)}, u32[]{:S(2)}, u32[]{:S(2)}) %collective-permute-start.12) | collective-permute-done | bytes 1291296 | tf_op jit(solution)/shard_map/ppermute | solution.py:32
  155.1 3.2 %add_convert_fusion = bf16[4,104,1552]{2,1,0:T(8,128)(2,1)} fusion(f32[4,104,1552]{2,1,0:T(8,128)} %get-tuple-element.49, bf16[4,104,1552]{2,1,0:T(8,128)(2,1)S(1)} %collective-permute-done.12), kind=kLoop, calls=%fused_computation.9 | loop fusion | flops 1936896 | bytes 5165056 | tf_op jit(solution)/shard_map/convert_element_type | solution.py:693
  158.2 3.5 %all-to-all-start = ((bf16[4,104,1552]{2,1,0:T(8,128)(2,1)}), bf16[4,104,1552]{2,1,0:T(8,128)(2,1)S(1)}, u32[]{:S(2)}, u32[]{:S(2)}) async-start(bf16[4,104,1552]{2,1,0:T(8,128)(2,1)} %add_convert_fusion), calls=%async_computation | async-start | bytes 2768896 | tf_op jit(solution)/shard_map/all_to_all | solution.py:694
  161.8 2.3 %fusion.11 = (bf16[4,128,1150]{2,1,0:T(8,128)(2,1)S(1)}, bf16[4,128,1150]{2,1,0:T(8,128)(2,1)S(1)}, bf16[4,128,1150]{2,1,0:T(8,128)(2,1)S(1)}) fusion(bf16[4,400,1152]{2,1,0:T(8,128)(2,1)} %get-tuple-element.52), kind=kLoop, calls=%fused_computation.45 | loop fusion | bytes 7065600 | tf_op jit(solution)/shard_map/slice | solution.py:73
  164.1 0.9 slice.60
  165.1 9.8 %multiply_bitcast_fusion = f32[16,70,1150]{2,0,1:T(8,128)} fusion(bf16[70,64,1600]{2,1,0:T(8,128)(2,1)} %get-tuple-element.51, s32[]{:T(128)S(6)} %select_n.16, bf16[64,1150]{1,0:T(8,128)(2,1)S(1)} %bitcast.49, bf16[512,1150]{1,0:T(8,128)(2,1)S(1)} %bitcast.45, bf16[512,1150]{1,0:T(8,128)(2,1)S(1)} %bitcast.46, bf16[512,1150]{1,0:T(8,128)(2,1)S(1)} %bitcast.44, ...), kind=kOutput, calls=%fused_computation | convolution fusion | flops 4137607936 | bytes 12632964 | tf_op jit(solution)/shard_map/tsr,rk->tsk/dot_general | solution.py:699
  174.8 5.0 %all-to-all-done = bf16[4,104,1552]{2,1,0:T(8,128)(2,1)S(1)} async-done(((bf16[4,104,1552]{2,1,0:T(8,128)(2,1)}), bf16[4,104,1552]{2,1,0:T(8,128)(2,1)S(1)}, u32[]{:S(2)}, u32[]{:S(2)}) %all-to-all-start) | async-done | bytes 1291296 | tf_op jit(solution)/shard_map/all_to_all | solution.py:694
  179.8 0.2 reduce_sum.69
  180.0 1.2 broadcast_in_dim.33
  181.2 3.5 %all-to-all-start.1 = ((bf16[4,104,1552]{2,1,0:T(8,128)(2,1)}), bf16[4,104,1552]{2,1,0:T(8,128)(2,1)S(1)}, u32[]{:S(2)}, u32[]{:S(2)}) async-start(bf16[4,104,1552]{2,1,0:T(8,128)(2,1)} %broadcast_in_dim.33), calls=%async_computation.1 | async-start | bytes 2768896 | tf_op jit(solution)/shard_map/all_to_all | solution.py:705
  184.8 0.1 collective-permute-start.13
  184.9 1.6 collective-permute-done.13
  186.5 1.0 multiply_reduce_fusion.2
  187.5 2.0 pad_maximum_fusion.4
  189.5 0.1 reshape.49
  189.6 0.3 collective-permute-start.14
  189.9 1.6 collective-permute-start.15
  191.5 2.5 %collective-permute-start.16 = (f32[2,2]{1,0:T(2,128)S(1)}, f32[2,2]{1,0:T(2,128)S(1)}, u32[]{:S(2)}, u32[]{:S(2)}) collective-permute-start(f32[2,2]{1,0:T(2,128)S(1)} %reshape.49), channel_id=1, source_target_pairs={{0,3},{1,2},{2,1},{3,0},{4,7},{5,6},{6,5},{7,4},{8,11},{9,10},{10,... | collective-permute-start | bytes 56 | tf_op jit(solution)/shard_map/ppermute | solution.py:32
  194.0 0.4 collective-permute-done.15
  194.4 2.5 %collective-permute-done.16 = f32[2,2]{1,0:T(2,128)S(1)} collective-permute-done((f32[2,2]{1,0:T(2,128)S(1)}, f32[2,2]{1,0:T(2,128)S(1)}, u32[]{:S(2)}, u32[]{:S(2)}) %collective-permute-start.16) | collective-permute-done | bytes 48 | tf_op jit(solution)/shard_map/ppermute | solution.py:32
  196.9 1.9 collective-permute-start.17
  198.8 1.5 collective-permute-start.18
  200.3 0.1 collective-permute-start.19
  200.4 1.6 collective-permute-done.17
  202.0 0.2 slice_convert_fusion
  202.2 1.4 slice_bitcast_fusion
  203.6 1.0 slice_bitcast_fusion.1
  204.6 0.8 slice_reduce_fusion
  205.4 0.6 add_add_fusion
  (32 shorter events, 0.3 us)
Async XLA Ops:
  5.2 19.8 %collective-permute-start = (bf16[208,896]{1,0:T(8,128)(2,1)}, bf16[208,896]{1,0:T(8,128)(2,1)S(1)}, u32[]{:S(2)}, u32[]{:S(2)}) collective-permute-start(bf16[208,896]{1,0:T(8,128)(2,1)} %get-tuple-element.31), channel_id=1, source_target_pairs={{0,1},{1,0},{2,3},{3,2},{4,5},{5,4},{6,7},{7,6},{8,9},{9,8},{10,11... | collective-permute-start | bytes 1118216 | tf_op jit(solution)/shard_map/ppermute | solution.py:32
  8.2 19.3 %collective-permute-start.1 = (bf16[208,896]{1,0:T(8,128)(2,1)}, bf16[208,896]{1,0:T(8,128)(2,1)S(1)}, u32[]{:S(2)}, u32[]{:S(2)}) collective-permute-start(bf16[208,896]{1,0:T(8,128)(2,1)} %get-tuple-element.31), channel_id=1, source_target_pairs={{0,2},{1,3},{2,0},{3,1},{4,6},{5,7},{6,4},{7,5},{8,10},{9,11},{10,... | collective-permute-start | bytes 1118216 | tf_op jit(solution)/shard_map/ppermute | solution.py:32
  12.8 10.5 %collective-permute-start.2 = (f32[2]{0:T(128)S(1)}, f32[2]{0:T(128)S(1)}, u32[]{:S(2)}, u32[]{:S(2)}) collective-permute-start(f32[2]{0:T(128)S(1)} %select_reduce_fusion.1), channel_id=1, source_target_pairs={{0,16},{16,0},{1,17},{17,1},{2,18},{18,2},{3,19},{19,3},{4,20},{20... | collective-permute-start | bytes 32 | tf_op jit(solution)/shard_map/ppermute | solution.py:32
  27.5 10.5 %collective-permute-start.5 = (bf16[208,896]{1,0:T(8,128)(2,1)S(1)}, bf16[208,896]{1,0:T(8,128)(2,1)S(1)}, u32[]{:S(2)}, u32[]{:S(2)}) collective-permute-start(bf16[208,896]{1,0:T(8,128)(2,1)S(1)} %collective-permute-done.1), channel_id=1, source_target_pairs={{0,1},{1,0},{2,3},{3,2},{4,5},{5,4},{6,7},{7,6},{8,9},{9,8},{10,11... | collective-permute-start | bytes 1118216 | tf_op jit(solution)/shard_map/ppermute | solution.py:32
  28.0 10.0 %collective-permute-start.3 = (bf16[2,112,896]{2,1,0:T(8,128)(2,1)S(1)}, bf16[2,112,896]{2,1,0:T(8,128)(2,1)S(1)}, u32[]{:S(2)}, u32[]{:S(2)}) collective-permute-start(bf16[2,112,896]{2,1,0:T(8,128)(2,1)S(1)} %fusion.7), channel_id=1, source_target_pairs={{0,4},{4,0},{8,12},{12,8},{1,5},{5,1},{9,13},{13,9},{2,6},{6,2},{1... | collective-permute-start | bytes 1204232 | tf_op jit(solution)/shard_map/ppermute | solution.py:32
  29.6 8.4 %collective-permute-start.4 = (bf16[2,96,896]{2,1,0:T(8,128)(2,1)S(1)}, bf16[2,96,896]{2,1,0:T(8,128)(2,1)S(1)}, u32[]{:S(2)}, u32[]{:S(2)}) collective-permute-start(bf16[2,96,896]{2,1,0:T(8,128)(2,1)S(1)} %fusion.8), channel_id=1, source_target_pairs={{0,8},{4,12},{8,0},{12,4},{1,9},{5,13},{9,1},{13,5},{2,10},{6,14},... | collective-permute-start | bytes 1032200 | tf_op jit(solution)/shard_map/ppermute | solution.py:32
  31.2 6.8 %collective-permute-start.6 = (f32[2]{0:T(128)S(1)}, f32[2]{0:T(128)S(1)}, u32[]{:S(2)}, u32[]{:S(2)}) collective-permute-start(f32[2]{0:T(128)S(1)} %add.34), channel_id=1, source_target_pairs={{0,4},{4,0},{8,12},{12,8},{1,5},{5,1},{9,13},{13,9},{2,6},{6,2},{1... | collective-permute-start | bytes 32 | tf_op jit(solution)/shard_map/ppermute | solution.py:32
  31.8 16.0 %copy-start.4 = (s32[64]{0:T(128)S(1)}, s32[64]{0:T(128)}, u32[]{:S(2)}) copy-start(s32[64]{0:T(128)} %param.14) | copy-start | bytes 772
  38.1 12.2 %copy-start = (bf16[1040,896]{1,0:T(8,128)(2,1)}, bf16[1040,896]{1,0:T(8,128)(2,1)S(1)}, u32[]{:S(2)}) copy-start(bf16[1040,896]{1,0:T(8,128)(2,1)S(1)} %pad_maximum_fusion.refs_1_) | copy-start | bytes 5591044
  38.2 8.3 %collective-permute-start.9 = (bf16[1040,896]{1,0:T(8,128)(2,1)S(1)}, bf16[1040,896]{1,0:T(8,128)(2,1)S(1)}, u32[]{:S(2)}, u32[]{:S(2)}) collective-permute-start(bf16[1040,896]{1,0:T(8,128)(2,1)S(1)} %pad_maximum_fusion.refs_1_), channel_id=1, source_target_pairs={{0,16},{16,0},{1,17},{17,1},{2,18},{18,2},{3,19},{19,3},{4,20},{20... | collective-permute-start | bytes 5591048 | tf_op jit(solution)/shard_map/ppermute | solution.py:32
  38.3 8.2 %collective-permute-start.7 = (bf16[112,896]{1,0:T(8,128)(2,1)S(1)}, bf16[112,896]{1,0:T(8,128)(2,1)S(1)}, u32[]{:S(2)}, u32[]{:S(2)}) collective-permute-start(bf16[112,896]{1,0:T(8,128)(2,1)S(1)} %slice.55), channel_id=1, source_target_pairs={{0,4},{4,0},{8,12},{12,8},{1,5},{5,1},{9,13},{13,9},{2,6},{6,2},{1... | collective-permute-start | bytes 602120 | tf_op jit(solution)/shard_map/ppermute | solution.py:32
  39.8 6.6 %collective-permute-start.8 = (bf16[96,896]{1,0:T(8,128)(2,1)S(1)}, bf16[96,896]{1,0:T(8,128)(2,1)S(1)}, u32[]{:S(2)}, u32[]{:S(2)}) collective-permute-start(bf16[96,896]{1,0:T(8,128)(2,1)S(1)} %slice.56), channel_id=1, source_target_pairs={{0,8},{4,12},{8,0},{12,4},{1,9},{5,13},{9,1},{13,5},{2,10},{6,14},... | collective-permute-start | bytes 516104 | tf_op jit(solution)/shard_map/ppermute | solution.py:32
  41.4 5.0 %collective-permute-start.10 = (f32[2]{0:T(128)S(1)}, f32[2]{0:T(128)S(1)}, u32[]{:S(2)}, u32[]{:S(2)}) collective-permute-start(f32[2]{0:T(128)S(1)} %add.35), channel_id=1, source_target_pairs={{0,8},{4,12},{8,0},{12,4},{1,9},{5,13},{9,1},{13,5},{2,10},{6,14},... | collective-permute-start | bytes 32 | tf_op jit(solution)/shard_map/ppermute | solution.py:32
  46.5 1.2 copy-start.1
  47.8 2.6 %copy-start.2 = (bf16[208,896]{1,0:T(8,128)(2,1)}, bf16[208,896]{1,0:T(8,128)(2,1)S(1)}, u32[]{:S(2)}) copy-start(bf16[208,896]{1,0:T(8,128)(2,1)S(1)} %constant_dynamic-update-slice_fusion.refs_2_) | copy-start | bytes 1118212
  47.8 2.5 %collective-permute-start.11 = (bf16[208,896]{1,0:T(8,128)(2,1)S(1)}, bf16[208,896]{1,0:T(8,128)(2,1)S(1)}, u32[]{:S(2)}, u32[]{:S(2)}) collective-permute-start(bf16[208,896]{1,0:T(8,128)(2,1)S(1)} %constant_dynamic-update-slice_fusion.refs_2_), channel_id=1, source_target_pairs={{0,16},{16,0},{1,17},{17,1},{2,18},{18,2},{3,19},{19,3},{4,20},{20... | collective-permute-start | bytes 1118216 | tf_op jit(solution)/shard_map/ppermute | solution.py:32
  50.3 0.8 copy-start.3
  151.5 3.5 %collective-permute-start.12 = (bf16[4,104,1552]{2,1,0:T(8,128)(2,1)}, bf16[4,104,1552]{2,1,0:T(8,128)(2,1)S(1)}, u32[]{:S(2)}, u32[]{:S(2)}) collective-permute-start(bf16[4,104,1552]{2,1,0:T(8,128)(2,1)} %get-tuple-element.50), channel_id=1, source_target_pairs={{0,16},{16,0},{1,17},{17,1},{2,18},{18,2},{3,19},{19,3},{4,20},{20... | collective-permute-start | bytes 3873800 | tf_op jit(solution)/shard_map/ppermute | solution.py:32
  158.2 21.6 %all-to-all-start = ((bf16[4,104,1552]{2,1,0:T(8,128)(2,1)}), bf16[4,104,1552]{2,1,0:T(8,128)(2,1)S(1)}, u32[]{:S(2)}, u32[]{:S(2)}) async-start(bf16[4,104,1552]{2,1,0:T(8,128)(2,1)} %add_convert_fusion), calls=%async_computation | async-start | bytes 2768896 | tf_op jit(solution)/shard_map/all_to_all | solution.py:694
  181.2 20.8 %all-to-all-start.1 = ((bf16[4,104,1552]{2,1,0:T(8,128)(2,1)}), bf16[4,104,1552]{2,1,0:T(8,128)(2,1)S(1)}, u32[]{:S(2)}, u32[]{:S(2)}) async-start(bf16[4,104,1552]{2,1,0:T(8,128)(2,1)} %broadcast_in_dim.33), calls=%async_computation.1 | async-start | bytes 2768896 | tf_op jit(solution)/shard_map/all_to_all | solution.py:705
  184.8 1.7 collective-permute-start.13
  189.6 4.4 %collective-permute-start.14 = (f32[2,2]{1,0:T(2,128)S(1)}, f32[2,2]{1,0:T(2,128)S(1)}, u32[]{:S(2)}, u32[]{:S(2)}) collective-permute-start(f32[2,2]{1,0:T(2,128)S(1)} %reshape.49), channel_id=1, source_target_pairs={{0,1},{1,0},{2,3},{3,2},{4,5},{5,4},{6,7},{7,6},{8,9},{9,8},{10,11... | collective-permute-start | bytes 56 | tf_op jit(solution)/shard_map/ppermute | solution.py:32
  189.9 4.5 %collective-permute-start.15 = (f32[2,2]{1,0:T(2,128)S(1)}, f32[2,2]{1,0:T(2,128)S(1)}, u32[]{:S(2)}, u32[]{:S(2)}) collective-permute-start(f32[2,2]{1,0:T(2,128)S(1)} %reshape.49), channel_id=1, source_target_pairs={{0,2},{1,3},{2,0},{3,1},{4,6},{5,7},{6,4},{7,5},{8,10},{9,11},{10,... | collective-permute-start | bytes 56 | tf_op jit(solution)/shard_map/ppermute | solution.py:32
  191.5 5.4 %collective-permute-start.16 = (f32[2,2]{1,0:T(2,128)S(1)}, f32[2,2]{1,0:T(2,128)S(1)}, u32[]{:S(2)}, u32[]{:S(2)}) collective-permute-start(f32[2,2]{1,0:T(2,128)S(1)} %reshape.49), channel_id=1, source_target_pairs={{0,3},{1,2},{2,1},{3,0},{4,7},{5,6},{6,5},{7,4},{8,11},{9,10},{10,... | collective-permute-start | bytes 56 | tf_op jit(solution)/shard_map/ppermute | solution.py:32
  196.9 5.1 %collective-permute-start.17 = (f32[2,2]{1,0:T(2,128)S(1)}, f32[2,2]{1,0:T(2,128)S(1)}, u32[]{:S(2)}, u32[]{:S(2)}) collective-permute-start(f32[2,2]{1,0:T(2,128)S(1)} %add_add_fusion.1), channel_id=1, source_target_pairs={{0,4},{4,0},{8,12},{12,8},{1,5},{5,1},{9,13},{13,9},{2,6},{6,2},{1... | collective-permute-start | bytes 56 | tf_op jit(solution)/shard_map/ppermute | solution.py:32
  198.8 6.6 %collective-permute-start.18 = (f32[2,2]{1,0:T(2,128)S(1)}, f32[2,2]{1,0:T(2,128)S(1)}, u32[]{:S(2)}, u32[]{:S(2)}) collective-permute-start(f32[2,2]{1,0:T(2,128)S(1)} %add_add_fusion.1), channel_id=1, source_target_pairs={{0,8},{4,12},{8,0},{12,4},{1,9},{5,13},{9,1},{13,5},{2,10},{6,14},... | collective-permute-start | bytes 56 | tf_op jit(solution)/shard_map/ppermute | solution.py:32
  200.3 5.1 %collective-permute-start.19 = (f32[2,2]{1,0:T(2,128)S(1)}, f32[2,2]{1,0:T(2,128)S(1)}, u32[]{:S(2)}, u32[]{:S(2)}) collective-permute-start(f32[2,2]{1,0:T(2,128)S(1)} %add_add_fusion.1), channel_id=1, source_target_pairs={{0,12},{4,8},{8,4},{12,0},{1,13},{5,9},{9,5},{13,1},{2,14},{6,10},... | collective-permute-start | bytes 56 | tf_op jit(solution)/shard_map/ppermute | solution.py:32

commit v5 on v4

--- a/solution.py
+++ b/solution.py
@@ -573,7 +573,7 @@
             jax.ShapeDtypeStruct((4, hidden, wide), BF16),
             jax.ShapeDtypeStruct((4, hidden, plan.columns - wide), BF16),
         ],
-        compiler_params=params(58),
+        compiler_params=params(52),
         name="forward",
     )(at, dropped, dropped, dropped, *sources)
 
@@ -648,7 +648,7 @@
         ),
         out_shape=[jax.ShapeDtypeStruct((time_steps, seq_count, cols.total), BF16)]
         + sum_shapes * own,
-        compiler_params=params(58),
+        compiler_params=params(52),
         name="backward",
     )(
         at,

time: 207 us -> 203 us (0.981)
  transfers between devices with their start and end apart: 22 -> 22, of which waited for: 10 -> 11; matrix products, arithmetic and copies ran while one was open for 12% -> 12% of each run, Pallas kernels for 5% -> 5%
where the time goes in v5:
time: 203 us
  Pallas kernels  114 us (56%)
  starting transfers between devices  28.8 us (14%)
  waiting for transfers between devices  28.8 us (14%)
  other arithmetic  11.8 us (6%)
  matrix products  9.77 us (5%)
  local copies, waits for them, and re-layouts  9.02 us (4%)
    pallas_call x1, Pallas kernels, local(): pl.pallas_call(functools.partial(backward_kernel, cols, own), grid_spec=p...  50.2 us
    pallas_call x1, Pallas kernels, local(): pl.pallas_call(functools.partial(forward_kernel, cols, plan, sub, pieced)...  49 us
    ppermute x20, waiting for transfers between devices, flip(): return lax.ppermute(block, axis, [(at, at ^ bit) for at in range(count)])  24 us
    ppermute x20, starting transfers between devices, flip(): return lax.ppermute(block, axis, [(at, at ^ bit) for at in range(count)])  21.7 us
    pallas_call x1, Pallas kernels, local(): pl.pallas_call(functools.partial(drop_kernel, width_in), grid=(blocks,),...  10.4 us
    dot_general x1, matrix products, local(): jnp.einsum('tsr,rk->tsk', own_seqs, w_in, preferred_element_type=F32)  9.77 us
    all_to_all x1, waiting for transfers between devices, local(): swapped = lax.all_to_all(block, 'seq', 0, 0, tiled=True)  4.77 us
  transfers between devices with their start and end apart: 22, of which 11 were waited for; matrix products, arithmetic and copies ran while one was open for 12% of the time, Pallas kernels for 5%

profile of v5, /device:TPU:0, one launch (start us, length us, event | category | flops | bytes accessed | tf_op | source)
XLA Modules:
  0.0 202.5 jit_solution(1990533314511489731)
XLA Ops:
  0.6 0.6 pad_add_fusion.at_ref
  1.2 3.9 %shard.1 = (bf16[400,1664]{1,0:T(8,128)(2,1)}, bf16[208,896]{1,0:T(8,128)(2,1)}) custom-call(s32[3]{0:T(128)} %pad_add_fusion.at_ref, bf16[400,1150]{1,0:T(8,128)(2,1)} %in_ref.1, bf16[400,400]{1,0:T(8,128)(2,1)} %rec_ref.1, s32[400,400]{1,0:T(8,128)} %refs_5_.1, f32[1,400]{1,0:T(1,128)} %bitcast.52), custom_call_target="tpu_custom_call" | custom-call | tf_op jit(solution)/shard_map/shard/pallas_call | solution.py:489
  5.1 3.0 %collective-permute-start = (bf16[208,896]{1,0:T(8,128)(2,1)}, bf16[208,896]{1,0:T(8,128)(2,1)S(1)}, u32[]{:S(2)}, u32[]{:S(2)}) collective-permute-start(bf16[208,896]{1,0:T(8,128)(2,1)} %get-tuple-element.31), channel_id=1, source_target_pairs={{0,1},{1,0},{2,3},{3,2},{4,5},{5,4},{6,7},{7,6},{8,9},{9,8},{10,11... | collective-permute-start | bytes 1118216 | tf_op jit(solution)/shard_map/ppermute | solution.py:32
  8.2 2.6 %collective-permute-start.1 = (bf16[208,896]{1,0:T(8,128)(2,1)}, bf16[208,896]{1,0:T(8,128)(2,1)S(1)}, u32[]{:S(2)}, u32[]{:S(2)}) collective-permute-start(bf16[208,896]{1,0:T(8,128)(2,1)} %get-tuple-element.31), channel_id=1, source_target_pairs={{0,2},{1,3},{2,0},{3,1},{4,6},{5,7},{6,4},{7,5},{8,10},{9,11},{10,... | collective-permute-start | bytes 1118216 | tf_op jit(solution)/shard_map/ppermute | solution.py:32
  10.7 0.7 convert_bitcast_fusion.1
  11.5 0.8 select_reduce_fusion.1
  12.2 0.1 collective-permute-start.2
  12.3 10.4 %drop.1.first_ref.second_ref.third_ref.refs_0_.refs_2_ = bf16[70,64,1152]{2,1,0:T(8,128)(2,1)} custom-call(bf16[70,64,1150]{2,1,0:T(8,128)(2,1)} %bitcast.35, s32[64,1150]{1,0:T(8,128)} %mask_ref.4), custom_call_target="tpu_custom_call" | custom-call | tf_op jit(solution)/shard_map/drop/pallas_call | solution.py:514
  22.7 0.0 collective-permute-done.2
  22.7 2.2 %collective-permute-done = bf16[208,896]{1,0:T(8,128)(2,1)S(1)} collective-permute-done((bf16[208,896]{1,0:T(8,128)(2,1)}, bf16[208,896]{1,0:T(8,128)(2,1)S(1)}, u32[]{:S(2)}, u32[]{:S(2)}) %collective-permute-start) | collective-permute-done | bytes 372768 | tf_op jit(solution)/shard_map/ppermute | solution.py:32
  24.9 2.6 %collective-permute-done.1 = bf16[208,896]{1,0:T(8,128)(2,1)S(1)} collective-permute-done((bf16[208,896]{1,0:T(8,128)(2,1)}, bf16[208,896]{1,0:T(8,128)(2,1)S(1)}, u32[]{:S(2)}, u32[]{:S(2)}) %collective-permute-start.1) | collective-permute-done | bytes 372768 | tf_op jit(solution)/shard_map/ppermute | solution.py:32
  27.4 0.4 collective-permute-start.5
  27.9 1.6 collective-permute-start.3
  29.5 1.6 collective-permute-start.4
  31.1 0.5 collective-permute-start.6
  31.6 0.1 pad_maximum_fusion.1
  31.7 0.0 copy-start.5
  31.7 0.0 copy-start.2
  31.7 6.1 %collective-permute-done.6 = f32[2]{0:T(128)S(1)} collective-permute-done((f32[2]{0:T(128)S(1)}, f32[2]{0:T(128)S(1)}, u32[]{:S(2)}, u32[]{:S(2)}) %collective-permute-start.6) | collective-permute-done | bytes 40 | tf_op jit(solution)/shard_map/ppermute | solution.py:32
  37.9 0.0 collective-permute-done.4
  37.9 0.1 pad_maximum_fusion.refs_1_
  38.1 0.1 collective-permute-start.9
  38.2 1.6 collective-permute-start.7
  39.7 1.6 collective-permute-start.8
  41.3 0.5 collective-permute-start.10
  41.8 4.5 %collective-permute-done.10 = f32[2]{0:T(128)S(1)} collective-permute-done((f32[2]{0:T(128)S(1)}, f32[2]{0:T(128)S(1)}, u32[]{:S(2)}, u32[]{:S(2)}) %collective-permute-start.10) | collective-permute-done | bytes 40 | tf_op jit(solution)/shard_map/ppermute | solution.py:32
  46.5 1.2 copy-done.4
  47.6 0.6 reduce_sum.67
  48.2 0.6 broadcast_divide_fusion
  48.9 0.1 select_reduce_fusion
  49.0 0.3 collective-permute-done.11.refs_4_
  49.3 49.0 %forward.1 = (f32[70,64,1600]{2,1,0:T(8,128)}, f32[70,64,400]{2,1,0:T(8,128)}, bf16[70,64,400]{2,1,0:T(8,128)(2,1)}, bf16[4,400,1152]{2,1,0:T(8,128)(2,1)}, bf16[4,400,512]{2,1,0:T(8,128)(2,1)}) custom-call(s32[3]{0:T(128)S(1)} %copy-done.2, bf16[70,64,1152]{2,1,0:T(8,128)(2,1)} %drop.1.first_ref.second_ref.third_ref.refs_0_.refs_2_, ...), custom_call_target="tpu_custom_call" | custom-call | tf_op jit(solution)/shard_map/forward/pallas_call | solution.py:538
  98.4 50.2 %backward.1 = (bf16[70,64,1600]{2,1,0:T(8,128)(2,1)}, f32[4,104,1552]{2,1,0:T(8,128)}, bf16[4,104,1552]{2,1,0:T(8,128)(2,1)}) custom-call(s32[3]{0:T(128)S(1)} %copy-done.2, f32[70,64,1600]{2,1,0:T(8,128)} %get-tuple-element.44.act_ref.act_before_ref, f32[70,64,400]{2,1,0:T(8,128)} %get-tuple-element.45.cell_ref.before_ref, ...), custom_call_target="tpu_custom_call" | custom-call | tf_op jit(solution)/shard_map/backward/pallas_call | solution.py:627
  148.6 0.2 collective-permute-start.12
  148.9 0.9 convert_multiply_fusion
  149.7 2.3 %collective-permute-done.12 = bf16[4,104,1552]{2,1,0:T(8,128)(2,1)S(1)} collective-permute-done((bf16[4,104,1552]{2,1,0:T(8,128)(2,1)}, bf16[4,104,1552]{2,1,0:T(8,128)(2,1)S(1)}, u32[]{:S(2)}, u32[]{:S(2)}) %collective-permute-start.12) | collective-permute-done | bytes 1291296 | tf_op jit(solution)/shard_map/ppermute | solution.py:32
  152.0 3.2 %add_convert_fusion = bf16[4,104,1552]{2,1,0:T(8,128)(2,1)} fusion(f32[4,104,1552]{2,1,0:T(8,128)} %get-tuple-element.49, bf16[4,104,1552]{2,1,0:T(8,128)(2,1)S(1)} %collective-permute-done.12), kind=kLoop, calls=%fused_computation.9 | loop fusion | flops 1936896 | bytes 5165056 | tf_op jit(solution)/shard_map/convert_element_type | solution.py:693
  155.2 3.5 %all-to-all-start = ((bf16[4,104,1552]{2,1,0:T(8,128)(2,1)}), bf16[4,104,1552]{2,1,0:T(8,128)(2,1)S(1)}, u32[]{:S(2)}, u32[]{:S(2)}) async-start(bf16[4,104,1552]{2,1,0:T(8,128)(2,1)} %add_convert_fusion), calls=%async_computation | async-start | bytes 2768896 | tf_op jit(solution)/shard_map/all_to_all | solution.py:694
  158.8 2.3 %fusion.11 = (bf16[4,128,1150]{2,1,0:T(8,128)(2,1)S(1)}, bf16[4,128,1150]{2,1,0:T(8,128)(2,1)S(1)}, bf16[4,128,1150]{2,1,0:T(8,128)(2,1)S(1)}) fusion(bf16[4,400,1152]{2,1,0:T(8,128)(2,1)} %get-tuple-element.52), kind=kLoop, calls=%fused_computation.45 | loop fusion | bytes 7065600 | tf_op jit(solution)/shard_map/slice | solution.py:73
  161.1 0.9 slice.60
  162.0 9.8 %multiply_bitcast_fusion = f32[16,70,1150]{2,0,1:T(8,128)} fusion(bf16[70,64,1600]{2,1,0:T(8,128)(2,1)} %get-tuple-element.51, s32[]{:T(128)S(6)} %select_n.16, bf16[64,1150]{1,0:T(8,128)(2,1)S(1)} %bitcast.50, bf16[512,1150]{1,0:T(8,128)(2,1)S(1)} %bitcast.46, bf16[512,1150]{1,0:T(8,128)(2,1)S(1)} %bitcast.47, bf16[512,1150]{1,0:T(8,128)(2,1)S(1)} %bitcast.45, ...), kind=kOutput, calls=%fused_computation | convolution fusion | flops 4137607936 | bytes 12632964 | tf_op jit(solution)/shard_map/tsr,rk->tsk/dot_general | solution.py:699
  171.8 4.8 %all-to-all-done = bf16[4,104,1552]{2,1,0:T(8,128)(2,1)S(1)} async-done(((bf16[4,104,1552]{2,1,0:T(8,128)(2,1)}), bf16[4,104,1552]{2,1,0:T(8,128)(2,1)S(1)}, u32[]{:S(2)}, u32[]{:S(2)}) %all-to-all-start) | async-done | bytes 1291296 | tf_op jit(solution)/shard_map/all_to_all | solution.py:694
  176.6 0.2 reduce_sum.69
  176.8 1.2 broadcast_in_dim.33
  178.0 3.5 %all-to-all-start.1 = ((bf16[4,104,1552]{2,1,0:T(8,128)(2,1)}), bf16[4,104,1552]{2,1,0:T(8,128)(2,1)S(1)}, u32[]{:S(2)}, u32[]{:S(2)}) async-start(bf16[4,104,1552]{2,1,0:T(8,128)(2,1)} %broadcast_in_dim.33), calls=%async_computation.1 | async-start | bytes 2768896 | tf_op jit(solution)/shard_map/all_to_all | solution.py:705
  181.5 0.1 collective-permute-start.13
  181.7 1.6 collective-permute-done.13
  183.3 1.0 multiply_reduce_fusion.2
  184.3 2.0 pad_maximum_fusion.4
  186.3 0.1 reshape.49
  186.4 0.3 collective-permute-start.14
  186.7 1.6 collective-permute-start.15
  188.3 2.5 %collective-permute-start.16 = (f32[2,2]{1,0:T(2,128)S(1)}, f32[2,2]{1,0:T(2,128)S(1)}, u32[]{:S(2)}, u32[]{:S(2)}) collective-permute-start(f32[2,2]{1,0:T(2,128)S(1)} %reshape.49), channel_id=1, source_target_pairs={{0,3},{1,2},{2,1},{3,0},{4,7},{5,6},{6,5},{7,4},{8,11},{9,10},{10,... | collective-permute-start | bytes 56 | tf_op jit(solution)/shard_map/ppermute | solution.py:32
  190.8 0.4 collective-permute-done.15
  191.2 2.5 %collective-permute-done.16 = f32[2,2]{1,0:T(2,128)S(1)} collective-permute-done((f32[2,2]{1,0:T(2,128)S(1)}, f32[2,2]{1,0:T(2,128)S(1)}, u32[]{:S(2)}, u32[]{:S(2)}) %collective-permute-start.16) | collective-permute-done | bytes 48 | tf_op jit(solution)/shard_map/ppermute | solution.py:32
  193.7 1.9 collective-permute-start.17
  195.6 1.5 collective-permute-start.18
  197.1 0.1 collective-permute-start.19
  197.2 1.4 collective-permute-done.17
  198.6 0.2 slice_convert_fusion
  198.8 1.4 slice_bitcast_fusion
  200.1 1.0 slice_bitcast_fusion.1
  201.1 0.8 slice_reduce_fusion
  202.0 0.6 add_add_fusion
  (34 shorter events, 0.3 us)
Async XLA Ops:
  5.1 19.8 %collective-permute-start = (bf16[208,896]{1,0:T(8,128)(2,1)}, bf16[208,896]{1,0:T(8,128)(2,1)S(1)}, u32[]{:S(2)}, u32[]{:S(2)}) collective-permute-start(bf16[208,896]{1,0:T(8,128)(2,1)} %get-tuple-element.31), channel_id=1, source_target_pairs={{0,1},{1,0},{2,3},{3,2},{4,5},{5,4},{6,7},{7,6},{8,9},{9,8},{10,11... | collective-permute-start | bytes 1118216 | tf_op jit(solution)/shard_map/ppermute | solution.py:32
  8.2 19.3 %collective-permute-start.1 = (bf16[208,896]{1,0:T(8,128)(2,1)}, bf16[208,896]{1,0:T(8,128)(2,1)S(1)}, u32[]{:S(2)}, u32[]{:S(2)}) collective-permute-start(bf16[208,896]{1,0:T(8,128)(2,1)} %get-tuple-element.31), channel_id=1, source_target_pairs={{0,2},{1,3},{2,0},{3,1},{4,6},{5,7},{6,4},{7,5},{8,10},{9,11},{10,... | collective-permute-start | bytes 1118216 | tf_op jit(solution)/shard_map/ppermute | solution.py:32
  12.2 10.4 %collective-permute-start.2 = (f32[2]{0:T(128)S(1)}, f32[2]{0:T(128)S(1)}, u32[]{:S(2)}, u32[]{:S(2)}) collective-permute-start(f32[2]{0:T(128)S(1)} %select_reduce_fusion.1), channel_id=1, source_target_pairs={{0,16},{16,0},{1,17},{17,1},{2,18},{18,2},{3,19},{19,3},{4,20},{20... | collective-permute-start | bytes 32 | tf_op jit(solution)/shard_map/ppermute | solution.py:32
  27.4 10.5 %collective-permute-start.5 = (bf16[208,896]{1,0:T(8,128)(2,1)S(1)}, bf16[208,896]{1,0:T(8,128)(2,1)S(1)}, u32[]{:S(2)}, u32[]{:S(2)}) collective-permute-start(bf16[208,896]{1,0:T(8,128)(2,1)S(1)} %collective-permute-done.1), channel_id=1, source_target_pairs={{0,1},{1,0},{2,3},{3,2},{4,5},{5,4},{6,7},{7,6},{8,9},{9,8},{10,11... | collective-permute-start | bytes 1118216 | tf_op jit(solution)/shard_map/ppermute | solution.py:32
  27.9 10.0 %collective-permute-start.3 = (bf16[2,112,896]{2,1,0:T(8,128)(2,1)S(1)}, bf16[2,112,896]{2,1,0:T(8,128)(2,1)S(1)}, u32[]{:S(2)}, u32[]{:S(2)}) collective-permute-start(bf16[2,112,896]{2,1,0:T(8,128)(2,1)S(1)} %fusion.7), channel_id=1, source_target_pairs={{0,4},{4,0},{8,12},{12,8},{1,5},{5,1},{9,13},{13,9},{2,6},{6,2},{1... | collective-permute-start | bytes 1204232 | tf_op jit(solution)/shard_map/ppermute | solution.py:32
  29.5 8.4 %collective-permute-start.4 = (bf16[2,96,896]{2,1,0:T(8,128)(2,1)S(1)}, bf16[2,96,896]{2,1,0:T(8,128)(2,1)S(1)}, u32[]{:S(2)}, u32[]{:S(2)}) collective-permute-start(bf16[2,96,896]{2,1,0:T(8,128)(2,1)S(1)} %fusion.8), channel_id=1, source_target_pairs={{0,8},{4,12},{8,0},{12,4},{1,9},{5,13},{9,1},{13,5},{2,10},{6,14},... | collective-permute-start | bytes 1032200 | tf_op jit(solution)/shard_map/ppermute | solution.py:32
  31.1 6.8 %collective-permute-start.6 = (f32[2]{0:T(128)S(1)}, f32[2]{0:T(128)S(1)}, u32[]{:S(2)}, u32[]{:S(2)}) collective-permute-start(f32[2]{0:T(128)S(1)} %add.34), channel_id=1, source_target_pairs={{0,4},{4,0},{8,12},{12,8},{1,5},{5,1},{9,13},{13,9},{2,6},{6,2},{1... | collective-permute-start | bytes 32 | tf_op jit(solution)/shard_map/ppermute | solution.py:32
  31.7 15.9 %copy-start.5 = (s32[64]{0:T(128)S(1)}, s32[64]{0:T(128)}, u32[]{:S(2)}) copy-start(s32[64]{0:T(128)} %param.14) | copy-start | bytes 772
  31.7 17.6 %copy-start.2 = (s32[3]{0:T(128)S(1)}, s32[3]{0:T(128)}, u32[]{:S(2)}) copy-start(s32[3]{0:T(128)} %pad_add_fusion.at_ref) | copy-start | bytes 40
  38.1 11.3 %copy-start.3 = (bf16[1040,896]{1,0:T(8,128)(2,1)}, bf16[1040,896]{1,0:T(8,128)(2,1)S(1)}, u32[]{:S(2)}) copy-start(bf16[1040,896]{1,0:T(8,128)(2,1)S(1)} %pad_maximum_fusion.refs_1_) | copy-start | bytes 5591044
  38.1 8.3 %collective-permute-start.9 = (bf16[1040,896]{1,0:T(8,128)(2,1)S(1)}, bf16[1040,896]{1,0:T(8,128)(2,1)S(1)}, u32[]{:S(2)}, u32[]{:S(2)}) collective-permute-start(bf16[1040,896]{1,0:T(8,128)(2,1)S(1)} %pad_maximum_fusion.refs_1_), channel_id=1, source_target_pairs={{0,16},{16,0},{1,17},{17,1},{2,18},{18,2},{3,19},{19,3},{4,20},{20... | collective-permute-start | bytes 5591048 | tf_op jit(solution)/shard_map/ppermute | solution.py:32
  38.2 8.2 %collective-permute-start.7 = (bf16[112,896]{1,0:T(8,128)(2,1)S(1)}, bf16[112,896]{1,0:T(8,128)(2,1)S(1)}, u32[]{:S(2)}, u32[]{:S(2)}) collective-permute-start(bf16[112,896]{1,0:T(8,128)(2,1)S(1)} %slice.55), channel_id=1, source_target_pairs={{0,4},{4,0},{8,12},{12,8},{1,5},{5,1},{9,13},{13,9},{2,6},{6,2},{1... | collective-permute-start | bytes 602120 | tf_op jit(solution)/shard_map/ppermute | solution.py:32
  39.7 6.6 %collective-permute-start.8 = (bf16[96,896]{1,0:T(8,128)(2,1)S(1)}, bf16[96,896]{1,0:T(8,128)(2,1)S(1)}, u32[]{:S(2)}, u32[]{:S(2)}) collective-permute-start(bf16[96,896]{1,0:T(8,128)(2,1)S(1)} %slice.56), channel_id=1, source_target_pairs={{0,8},{4,12},{8,0},{12,4},{1,9},{5,13},{9,1},{13,5},{2,10},{6,14},... | collective-permute-start | bytes 516104 | tf_op jit(solution)/shard_map/ppermute | solution.py:32
  41.3 5.0 %collective-permute-start.10 = (f32[2]{0:T(128)S(1)}, f32[2]{0:T(128)S(1)}, u32[]{:S(2)}, u32[]{:S(2)}) collective-permute-start(f32[2]{0:T(128)S(1)} %add.35), channel_id=1, source_target_pairs={{0,8},{4,12},{8,0},{12,4},{1,9},{5,13},{9,1},{13,5},{2,10},{6,14},... | collective-permute-start | bytes 32 | tf_op jit(solution)/shard_map/ppermute | solution.py:32
  46.4 1.2 copy-start.4
  47.6 1.7 collective-permute-start.11
  49.3 49.0 %copy-start = (s32[400,400]{1,0:T(8,128)S(1)}, s32[400,400]{1,0:T(8,128)}, u32[]{:S(2)}) copy-start(s32[400,400]{1,0:T(8,128)} %refs_5_.1) | copy-start | bytes 1920004
  49.3 49.0 %copy-start.1 = (s32[64,400]{1,0:T(8,128)S(1)}, s32[64,400]{1,0:T(8,128)}, u32[]{:S(2)}) copy-start(s32[64,400]{1,0:T(8,128)} %mask_ref.5) | copy-start | bytes 307204
  148.6 3.4 %collective-permute-start.12 = (bf16[4,104,1552]{2,1,0:T(8,128)(2,1)}, bf16[4,104,1552]{2,1,0:T(8,128)(2,1)S(1)}, u32[]{:S(2)}, u32[]{:S(2)}) collective-permute-start(bf16[4,104,1552]{2,1,0:T(8,128)(2,1)} %get-tuple-element.50), channel_id=1, source_target_pairs={{0,16},{16,0},{1,17},{17,1},{2,18},{18,2},{3,19},{19,3},{4,20},{20... | collective-permute-start | bytes 3873800 | tf_op jit(solution)/shard_map/ppermute | solution.py:32
  155.2 21.4 %all-to-all-start = ((bf16[4,104,1552]{2,1,0:T(8,128)(2,1)}), bf16[4,104,1552]{2,1,0:T(8,128)(2,1)S(1)}, u32[]{:S(2)}, u32[]{:S(2)}) async-start(bf16[4,104,1552]{2,1,0:T(8,128)(2,1)} %add_convert_fusion), calls=%async_computation | async-start | bytes 2768896 | tf_op jit(solution)/shard_map/all_to_all | solution.py:694
  178.0 20.6 %all-to-all-start.1 = ((bf16[4,104,1552]{2,1,0:T(8,128)(2,1)}), bf16[4,104,1552]{2,1,0:T(8,128)(2,1)S(1)}, u32[]{:S(2)}, u32[]{:S(2)}) async-start(bf16[4,104,1552]{2,1,0:T(8,128)(2,1)} %broadcast_in_dim.33), calls=%async_computation.1 | async-start | bytes 2768896 | tf_op jit(solution)/shard_map/all_to_all | solution.py:705
  181.5 1.7 collective-permute-start.13
  186.4 4.4 %collective-permute-start.14 = (f32[2,2]{1,0:T(2,128)S(1)}, f32[2,2]{1,0:T(2,128)S(1)}, u32[]{:S(2)}, u32[]{:S(2)}) collective-permute-start(f32[2,2]{1,0:T(2,128)S(1)} %reshape.49), channel_id=1, source_target_pairs={{0,1},{1,0},{2,3},{3,2},{4,5},{5,4},{6,7},{7,6},{8,9},{9,8},{10,11... | collective-permute-start | bytes 56 | tf_op jit(solution)/shard_map/ppermute | solution.py:32
  186.7 4.5 %collective-permute-start.15 = (f32[2,2]{1,0:T(2,128)S(1)}, f32[2,2]{1,0:T(2,128)S(1)}, u32[]{:S(2)}, u32[]{:S(2)}) collective-permute-start(f32[2,2]{1,0:T(2,128)S(1)} %reshape.49), channel_id=1, source_target_pairs={{0,2},{1,3},{2,0},{3,1},{4,6},{5,7},{6,4},{7,5},{8,10},{9,11},{10,... | collective-permute-start | bytes 56 | tf_op jit(solution)/shard_map/ppermute | solution.py:32
  188.3 5.4 %collective-permute-start.16 = (f32[2,2]{1,0:T(2,128)S(1)}, f32[2,2]{1,0:T(2,128)S(1)}, u32[]{:S(2)}, u32[]{:S(2)}) collective-permute-start(f32[2,2]{1,0:T(2,128)S(1)} %reshape.49), channel_id=1, source_target_pairs={{0,3},{1,2},{2,1},{3,0},{4,7},{5,6},{6,5},{7,4},{8,11},{9,10},{10,... | collective-permute-start | bytes 56 | tf_op jit(solution)/shard_map/ppermute | solution.py:32
  193.7 4.9 %collective-permute-start.17 = (f32[2,2]{1,0:T(2,128)S(1)}, f32[2,2]{1,0:T(2,128)S(1)}, u32[]{:S(2)}, u32[]{:S(2)}) collective-permute-start(f32[2,2]{1,0:T(2,128)S(1)} %add_add_fusion.1), channel_id=1, source_target_pairs={{0,4},{4,0},{8,12},{12,8},{1,5},{5,1},{9,13},{13,9},{2,6},{6,2},{1... | collective-permute-start | bytes 56 | tf_op jit(solution)/shard_map/ppermute | solution.py:32
  195.6 6.4 %collective-permute-start.18 = (f32[2,2]{1,0:T(2,128)S(1)}, f32[2,2]{1,0:T(2,128)S(1)}, u32[]{:S(2)}, u32[]{:S(2)}) collective-permute-start(f32[2,2]{1,0:T(2,128)S(1)} %add_add_fusion.1), channel_id=1, source_target_pairs={{0,8},{4,12},{8,0},{12,4},{1,9},{5,13},{9,1},{13,5},{2,10},{6,14},... | collective-permute-start | bytes 56 | tf_op jit(solution)/shard_map/ppermute | solution.py:32
  197.1 4.9 %collective-permute-start.19 = (f32[2,2]{1,0:T(2,128)S(1)}, f32[2,2]{1,0:T(2,128)S(1)}, u32[]{:S(2)}, u32[]{:S(2)}) collective-permute-start(f32[2,2]{1,0:T(2,128)S(1)} %add_add_fusion.1), channel_id=1, source_target_pairs={{0,12},{4,8},{8,4},{12,0},{1,13},{5,9},{9,5},{13,1},{2,14},{6,10},... | collective-permute-start | bytes 56 | tf_op jit(solution)/shard_map/ppermute | solution.py:32

commit v6 on v5

--- a/solution.py
+++ b/solution.py
@@ -379,7 +379,7 @@
     rows = keep_ref.shape[1]
     for part in range(keep_ref.shape[0]):
         span = slice(part * rows, (part + 1) * rows)
-        keep_ref[part] = sums[grp_at, span]
+        keep_ref[part] = sums[grp_at, span].astype(BF16)
         send_ref[part] = sums[1 - grp_at, span].astype(BF16)
 
 
@@ -601,10 +601,7 @@
     columns = wide + hidden
     group_row = groups.astype(F32)[None]
     sum_specs = [fixed(seq_n, part_rows, columns)] * 2
-    sum_shapes = [
-        jax.ShapeDtypeStruct((seq_n, part_rows, columns), F32),
-        jax.ShapeDtypeStruct((seq_n, part_rows, columns), BF16),
-    ]
+    sum_shapes = [jax.ShapeDtypeStruct((seq_n, part_rows, columns), BF16)] * 2
     sum_scratch = pltpu.VMEM((2, seq_n * part_rows, columns), F32)
     per_unit = pltpu.VMEM((seq_count, hidden), F32)
     own_specs, own_arrays, own_scratch = [], [], []
@@ -690,7 +687,7 @@
     keep, send = sums
 
     hold = lax.optimization_barrier
-    block = (keep + flip(send, "grp", 1).astype(F32)).astype(BF16)
+    block = (keep.astype(F32) + flip(send, "grp", 1).astype(F32)).astype(BF16)
     swapped = lax.all_to_all(block, "seq", 0, 0, tiled=True)
 
     own_seqs = lax.dynamic_slice_in_dim(grads, row_at * share, share, 1)

time: 203 us -> 202 us (level)
  no operation moved by 1% of the time
where the time goes in v6:
time: 202 us
  Pallas kernels  113 us (56%)
  starting transfers between devices  28.8 us (14%)
  waiting for transfers between devices  28.7 us (14%)
  other arithmetic  11.4 us (6%)
  matrix products  9.77 us (5%)
  local copies, waits for them, and re-layouts  9.02 us (4%)
    pallas_call x1, Pallas kernels, local(): pl.pallas_call(functools.partial(backward_kernel, cols, own), grid_spec=p...  49.8 us
    pallas_call x1, Pallas kernels, local(): pl.pallas_call(functools.partial(forward_kernel, cols, plan, sub, pieced)...  49 us
    ppermute x20, waiting for transfers between devices, flip(): return lax.ppermute(block, axis, [(at, at ^ bit) for at in range(count)])  24 us
    ppermute x20, starting transfers between devices, flip(): return lax.ppermute(block, axis, [(at, at ^ bit) for at in range(count)])  21.7 us
    pallas_call x1, Pallas kernels, local(): pl.pallas_call(functools.partial(drop_kernel, width_in), grid=(blocks,),...  10.4 us
    dot_general x1, matrix products, local(): jnp.einsum('tsr,rk->tsk', own_seqs, w_in, preferred_element_type=F32)  9.77 us
    all_to_all x1, waiting for transfers between devices, local(): swapped = lax.all_to_all(block, 'seq', 0, 0, tiled=True)  4.75 us
  transfers between devices with their start and end apart: 22, of which 11 were waited for; matrix products, arithmetic and copies ran while one was open for 12% of the time, Pallas kernels for 5%

profile of v6, /device:TPU:0, one launch (start us, length us, event | category | flops | bytes accessed | tf_op | source)
XLA Modules:
  0.0 201.7 jit_solution(2368210912380534327)
XLA Ops:
  0.6 0.6 pad_add_fusion.at_ref
  1.2 3.9 %shard.1 = (bf16[400,1664]{1,0:T(8,128)(2,1)}, bf16[208,896]{1,0:T(8,128)(2,1)}) custom-call(s32[3]{0:T(128)} %pad_add_fusion.at_ref, bf16[400,1150]{1,0:T(8,128)(2,1)} %in_ref.1, bf16[400,400]{1,0:T(8,128)(2,1)} %rec_ref.1, s32[400,400]{1,0:T(8,128)} %refs_5_.1, f32[1,400]{1,0:T(1,128)} %bitcast.52), custom_call_target="tpu_custom_call" | custom-call | tf_op jit(solution)/shard_map/shard/pallas_call | solution.py:489
  5.1 3.0 %collective-permute-start = (bf16[208,896]{1,0:T(8,128)(2,1)}, bf16[208,896]{1,0:T(8,128)(2,1)S(1)}, u32[]{:S(2)}, u32[]{:S(2)}) collective-permute-start(bf16[208,896]{1,0:T(8,128)(2,1)} %get-tuple-element.31), channel_id=1, source_target_pairs={{0,1},{1,0},{2,3},{3,2},{4,5},{5,4},{6,7},{7,6},{8,9},{9,8},{10,11... | collective-permute-start | bytes 1118216 | tf_op jit(solution)/shard_map/ppermute | solution.py:32
  8.2 2.6 %collective-permute-start.1 = (bf16[208,896]{1,0:T(8,128)(2,1)}, bf16[208,896]{1,0:T(8,128)(2,1)S(1)}, u32[]{:S(2)}, u32[]{:S(2)}) collective-permute-start(bf16[208,896]{1,0:T(8,128)(2,1)} %get-tuple-element.31), channel_id=1, source_target_pairs={{0,2},{1,3},{2,0},{3,1},{4,6},{5,7},{6,4},{7,5},{8,10},{9,11},{10,... | collective-permute-start | bytes 1118216 | tf_op jit(solution)/shard_map/ppermute | solution.py:32
  10.7 0.7 convert_bitcast_fusion.1
  11.5 0.8 select_reduce_fusion.1
  12.2 0.1 collective-permute-start.2
  12.3 10.4 %drop.1.first_ref.second_ref.third_ref.refs_0_.refs_2_ = bf16[70,64,1152]{2,1,0:T(8,128)(2,1)} custom-call(bf16[70,64,1150]{2,1,0:T(8,128)(2,1)} %bitcast.35, s32[64,1150]{1,0:T(8,128)} %mask_ref.4), custom_call_target="tpu_custom_call" | custom-call | tf_op jit(solution)/shard_map/drop/pallas_call | solution.py:514
  22.7 0.0 collective-permute-done.2
  22.7 2.2 %collective-permute-done = bf16[208,896]{1,0:T(8,128)(2,1)S(1)} collective-permute-done((bf16[208,896]{1,0:T(8,128)(2,1)}, bf16[208,896]{1,0:T(8,128)(2,1)S(1)}, u32[]{:S(2)}, u32[]{:S(2)}) %collective-permute-start) | collective-permute-done | bytes 372768 | tf_op jit(solution)/shard_map/ppermute | solution.py:32
  24.9 2.6 %collective-permute-done.1 = bf16[208,896]{1,0:T(8,128)(2,1)S(1)} collective-permute-done((bf16[208,896]{1,0:T(8,128)(2,1)}, bf16[208,896]{1,0:T(8,128)(2,1)S(1)}, u32[]{:S(2)}, u32[]{:S(2)}) %collective-permute-start.1) | collective-permute-done | bytes 372768 | tf_op jit(solution)/shard_map/ppermute | solution.py:32
  27.4 0.4 collective-permute-start.5
  27.9 1.6 collective-permute-start.3
  29.5 1.6 collective-permute-start.4
  31.1 0.5 collective-permute-start.6
  31.6 0.1 pad_maximum_fusion.1
  31.7 0.0 copy-start.5
  31.7 0.0 copy-start.2
  31.7 6.1 %collective-permute-done.6 = f32[2]{0:T(128)S(1)} collective-permute-done((f32[2]{0:T(128)S(1)}, f32[2]{0:T(128)S(1)}, u32[]{:S(2)}, u32[]{:S(2)}) %collective-permute-start.6) | collective-permute-done | bytes 40 | tf_op jit(solution)/shard_map/ppermute | solution.py:32
  37.9 0.0 collective-permute-done.4
  37.9 0.1 pad_maximum_fusion.refs_1_
  38.1 0.1 collective-permute-start.9
  38.2 1.6 collective-permute-start.7
  39.7 1.6 collective-permute-start.8
  41.3 0.5 collective-permute-start.10
  41.8 4.5 %collective-permute-done.10 = f32[2]{0:T(128)S(1)} collective-permute-done((f32[2]{0:T(128)S(1)}, f32[2]{0:T(128)S(1)}, u32[]{:S(2)}, u32[]{:S(2)}) %collective-permute-start.10) | collective-permute-done | bytes 40 | tf_op jit(solution)/shard_map/ppermute | solution.py:32
  46.5 1.2 copy-done.4
  47.6 0.6 reduce_sum.67
  48.2 0.6 broadcast_divide_fusion
  48.9 0.1 select_reduce_fusion
  49.0 0.3 collective-permute-done.11.refs_4_
  49.3 49.0 %forward.1 = (f32[70,64,1600]{2,1,0:T(8,128)}, f32[70,64,400]{2,1,0:T(8,128)}, bf16[70,64,400]{2,1,0:T(8,128)(2,1)}, bf16[4,400,1152]{2,1,0:T(8,128)(2,1)}, bf16[4,400,512]{2,1,0:T(8,128)(2,1)}) custom-call(s32[3]{0:T(128)S(1)} %copy-done.2, bf16[70,64,1152]{2,1,0:T(8,128)(2,1)} %drop.1.first_ref.second_ref.third_ref.refs_0_.refs_2_, ...), custom_call_target="tpu_custom_call" | custom-call | tf_op jit(solution)/shard_map/forward/pallas_call | solution.py:538
  98.4 49.8 %backward.1 = (bf16[70,64,1600]{2,1,0:T(8,128)(2,1)}, bf16[4,104,1552]{2,1,0:T(8,128)(2,1)}, bf16[4,104,1552]{2,1,0:T(8,128)(2,1)}) custom-call(s32[3]{0:T(128)S(1)} %copy-done.2, f32[70,64,1600]{2,1,0:T(8,128)} %get-tuple-element.44.act_ref.act_before_ref, f32[70,64,400]{2,1,0:T(8,128)} %get-tuple-element.45.cell_ref.before_ref, ...), custom_call_target="tpu_custom_call" | custom-call | tf_op jit(solution)/shard_map/backward/pallas_call | solution.py:624
  148.2 0.2 collective-permute-start.12
  148.4 0.9 convert_multiply_fusion
  149.3 2.3 %collective-permute-done.12 = bf16[4,104,1552]{2,1,0:T(8,128)(2,1)S(1)} collective-permute-done((bf16[4,104,1552]{2,1,0:T(8,128)(2,1)}, bf16[4,104,1552]{2,1,0:T(8,128)(2,1)S(1)}, u32[]{:S(2)}, u32[]{:S(2)}) %collective-permute-start.12) | collective-permute-done | bytes 1291296 | tf_op jit(solution)/shard_map/ppermute | solution.py:32
  151.6 2.7 %add_convert_fusion = bf16[4,104,1552]{2,1,0:T(8,128)(2,1)} fusion(bf16[4,104,1552]{2,1,0:T(8,128)(2,1)S(1)} %collective-permute-done.12, bf16[4,104,1552]{2,1,0:T(8,128)(2,1)} %get-tuple-element.49), kind=kLoop, calls=%fused_computation.9 | loop fusion | flops 2582528 | bytes 3873792 | tf_op jit(solution)/shard_map/convert_element_type | solution.py:690
  154.4 3.5 %all-to-all-start = ((bf16[4,104,1552]{2,1,0:T(8,128)(2,1)}), bf16[4,104,1552]{2,1,0:T(8,128)(2,1)S(1)}, u32[]{:S(2)}, u32[]{:S(2)}) async-start(bf16[4,104,1552]{2,1,0:T(8,128)(2,1)} %add_convert_fusion), calls=%async_computation | async-start | bytes 2768896 | tf_op jit(solution)/shard_map/all_to_all | solution.py:691
  157.9 2.3 %fusion.11 = (bf16[4,128,1150]{2,1,0:T(8,128)(2,1)S(1)}, bf16[4,128,1150]{2,1,0:T(8,128)(2,1)S(1)}, bf16[4,128,1150]{2,1,0:T(8,128)(2,1)S(1)}) fusion(bf16[4,400,1152]{2,1,0:T(8,128)(2,1)} %get-tuple-element.52), kind=kLoop, calls=%fused_computation.45 | loop fusion | bytes 7065600 | tf_op jit(solution)/shard_map/slice | solution.py:73
  160.3 0.9 slice.60
  161.2 9.8 %multiply_bitcast_fusion = f32[16,70,1150]{2,0,1:T(8,128)} fusion(bf16[70,64,1600]{2,1,0:T(8,128)(2,1)} %get-tuple-element.51, s32[]{:T(128)S(6)} %select_n.16, bf16[64,1150]{1,0:T(8,128)(2,1)S(1)} %bitcast.50, bf16[512,1150]{1,0:T(8,128)(2,1)S(1)} %bitcast.46, bf16[512,1150]{1,0:T(8,128)(2,1)S(1)} %bitcast.47, bf16[512,1150]{1,0:T(8,128)(2,1)S(1)} %bitcast.45, ...), kind=kOutput, calls=%fused_computation | convolution fusion | flops 4137607936 | bytes 12632964 | tf_op jit(solution)/shard_map/tsr,rk->tsk/dot_general | solution.py:696
  171.0 4.8 %all-to-all-done = bf16[4,104,1552]{2,1,0:T(8,128)(2,1)S(1)} async-done(((bf16[4,104,1552]{2,1,0:T(8,128)(2,1)}), bf16[4,104,1552]{2,1,0:T(8,128)(2,1)S(1)}, u32[]{:S(2)}, u32[]{:S(2)}) %all-to-all-start) | async-done | bytes 1291296 | tf_op jit(solution)/shard_map/all_to_all | solution.py:691
  175.7 0.2 reduce_sum.69
  176.0 1.2 broadcast_in_dim.33
  177.1 3.5 %all-to-all-start.1 = ((bf16[4,104,1552]{2,1,0:T(8,128)(2,1)}), bf16[4,104,1552]{2,1,0:T(8,128)(2,1)S(1)}, u32[]{:S(2)}, u32[]{:S(2)}) async-start(bf16[4,104,1552]{2,1,0:T(8,128)(2,1)} %broadcast_in_dim.33), calls=%async_computation.1 | async-start | bytes 2768896 | tf_op jit(solution)/shard_map/all_to_all | solution.py:702
  180.7 0.1 collective-permute-start.13
  180.8 1.6 collective-permute-done.13
  182.4 1.0 multiply_reduce_fusion.2
  183.4 2.0 pad_maximum_fusion.4
  185.4 0.1 reshape.49
  185.5 0.3 collective-permute-start.14
  185.8 1.6 collective-permute-start.15
  187.5 2.5 %collective-permute-start.16 = (f32[2,2]{1,0:T(2,128)S(1)}, f32[2,2]{1,0:T(2,128)S(1)}, u32[]{:S(2)}, u32[]{:S(2)}) collective-permute-start(f32[2,2]{1,0:T(2,128)S(1)} %reshape.49), channel_id=1, source_target_pairs={{0,3},{1,2},{2,1},{3,0},{4,7},{5,6},{6,5},{7,4},{8,11},{9,10},{10,... | collective-permute-start | bytes 56 | tf_op jit(solution)/shard_map/ppermute | solution.py:32
  189.9 0.4 collective-permute-done.15
  190.3 2.5 %collective-permute-done.16 = f32[2,2]{1,0:T(2,128)S(1)} collective-permute-done((f32[2,2]{1,0:T(2,128)S(1)}, f32[2,2]{1,0:T(2,128)S(1)}, u32[]{:S(2)}, u32[]{:S(2)}) %collective-permute-start.16) | collective-permute-done | bytes 48 | tf_op jit(solution)/shard_map/ppermute | solution.py:32
  192.8 1.9 collective-permute-start.17
  194.8 1.5 collective-permute-start.18
  196.2 0.1 collective-permute-start.19
  196.3 1.4 collective-permute-done.17
  197.8 0.2 slice_convert_fusion
  197.9 1.4 slice_bitcast_fusion
  199.3 1.0 slice_bitcast_fusion.1
  200.3 0.8 slice_reduce_fusion
  201.1 0.6 add_add_fusion
  (34 shorter events, 0.3 us)
Async XLA Ops:
  5.1 19.8 %collective-permute-start = (bf16[208,896]{1,0:T(8,128)(2,1)}, bf16[208,896]{1,0:T(8,128)(2,1)S(1)}, u32[]{:S(2)}, u32[]{:S(2)}) collective-permute-start(bf16[208,896]{1,0:T(8,128)(2,1)} %get-tuple-element.31), channel_id=1, source_target_pairs={{0,1},{1,0},{2,3},{3,2},{4,5},{5,4},{6,7},{7,6},{8,9},{9,8},{10,11... | collective-permute-start | bytes 1118216 | tf_op jit(solution)/shard_map/ppermute | solution.py:32
  8.2 19.3 %collective-permute-start.1 = (bf16[208,896]{1,0:T(8,128)(2,1)}, bf16[208,896]{1,0:T(8,128)(2,1)S(1)}, u32[]{:S(2)}, u32[]{:S(2)}) collective-permute-start(bf16[208,896]{1,0:T(8,128)(2,1)} %get-tuple-element.31), channel_id=1, source_target_pairs={{0,2},{1,3},{2,0},{3,1},{4,6},{5,7},{6,4},{7,5},{8,10},{9,11},{10,... | collective-permute-start | bytes 1118216 | tf_op jit(solution)/shard_map/ppermute | solution.py:32
  12.2 10.4 %collective-permute-start.2 = (f32[2]{0:T(128)S(1)}, f32[2]{0:T(128)S(1)}, u32[]{:S(2)}, u32[]{:S(2)}) collective-permute-start(f32[2]{0:T(128)S(1)} %select_reduce_fusion.1), channel_id=1, source_target_pairs={{0,16},{16,0},{1,17},{17,1},{2,18},{18,2},{3,19},{19,3},{4,20},{20... | collective-permute-start | bytes 32 | tf_op jit(solution)/shard_map/ppermute | solution.py:32
  27.4 10.5 %collective-permute-start.5 = (bf16[208,896]{1,0:T(8,128)(2,1)S(1)}, bf16[208,896]{1,0:T(8,128)(2,1)S(1)}, u32[]{:S(2)}, u32[]{:S(2)}) collective-permute-start(bf16[208,896]{1,0:T(8,128)(2,1)S(1)} %collective-permute-done.1), channel_id=1, source_target_pairs={{0,1},{1,0},{2,3},{3,2},{4,5},{5,4},{6,7},{7,6},{8,9},{9,8},{10,11... | collective-permute-start | bytes 1118216 | tf_op jit(solution)/shard_map/ppermute | solution.py:32
  27.9 10.0 %collective-permute-start.3 = (bf16[2,112,896]{2,1,0:T(8,128)(2,1)S(1)}, bf16[2,112,896]{2,1,0:T(8,128)(2,1)S(1)}, u32[]{:S(2)}, u32[]{:S(2)}) collective-permute-start(bf16[2,112,896]{2,1,0:T(8,128)(2,1)S(1)} %fusion.7), channel_id=1, source_target_pairs={{0,4},{4,0},{8,12},{12,8},{1,5},{5,1},{9,13},{13,9},{2,6},{6,2},{1... | collective-permute-start | bytes 1204232 | tf_op jit(solution)/shard_map/ppermute | solution.py:32
  29.5 8.4 %collective-permute-start.4 = (bf16[2,96,896]{2,1,0:T(8,128)(2,1)S(1)}, bf16[2,96,896]{2,1,0:T(8,128)(2,1)S(1)}, u32[]{:S(2)}, u32[]{:S(2)}) collective-permute-start(bf16[2,96,896]{2,1,0:T(8,128)(2,1)S(1)} %fusion.8), channel_id=1, source_target_pairs={{0,8},{4,12},{8,0},{12,4},{1,9},{5,13},{9,1},{13,5},{2,10},{6,14},... | collective-permute-start | bytes 1032200 | tf_op jit(solution)/shard_map/ppermute | solution.py:32
  31.1 6.8 %collective-permute-start.6 = (f32[2]{0:T(128)S(1)}, f32[2]{0:T(128)S(1)}, u32[]{:S(2)}, u32[]{:S(2)}) collective-permute-start(f32[2]{0:T(128)S(1)} %add.34), channel_id=1, source_target_pairs={{0,4},{4,0},{8,12},{12,8},{1,5},{5,1},{9,13},{13,9},{2,6},{6,2},{1... | collective-permute-start | bytes 32 | tf_op jit(solution)/shard_map/ppermute | solution.py:32
  31.7 15.9 %copy-start.5 = (s32[64]{0:T(128)S(1)}, s32[64]{0:T(128)}, u32[]{:S(2)}) copy-start(s32[64]{0:T(128)} %param.14) | copy-start | bytes 772
  31.7 17.6 %copy-start.2 = (s32[3]{0:T(128)S(1)}, s32[3]{0:T(128)}, u32[]{:S(2)}) copy-start(s32[3]{0:T(128)} %pad_add_fusion.at_ref) | copy-start | bytes 40
  38.1 11.3 %copy-start.3 = (bf16[1040,896]{1,0:T(8,128)(2,1)}, bf16[1040,896]{1,0:T(8,128)(2,1)S(1)}, u32[]{:S(2)}) copy-start(bf16[1040,896]{1,0:T(8,128)(2,1)S(1)} %pad_maximum_fusion.refs_1_) | copy-start | bytes 5591044
  38.1 8.3 %collective-permute-start.9 = (bf16[1040,896]{1,0:T(8,128)(2,1)S(1)}, bf16[1040,896]{1,0:T(8,128)(2,1)S(1)}, u32[]{:S(2)}, u32[]{:S(2)}) collective-permute-start(bf16[1040,896]{1,0:T(8,128)(2,1)S(1)} %pad_maximum_fusion.refs_1_), channel_id=1, source_target_pairs={{0,16},{16,0},{1,17},{17,1},{2,18},{18,2},{3,19},{19,3},{4,20},{20... | collective-permute-start | bytes 5591048 | tf_op jit(solution)/shard_map/ppermute | solution.py:32
  38.2 8.2 %collective-permute-start.7 = (bf16[112,896]{1,0:T(8,128)(2,1)S(1)}, bf16[112,896]{1,0:T(8,128)(2,1)S(1)}, u32[]{:S(2)}, u32[]{:S(2)}) collective-permute-start(bf16[112,896]{1,0:T(8,128)(2,1)S(1)} %slice.55), channel_id=1, source_target_pairs={{0,4},{4,0},{8,12},{12,8},{1,5},{5,1},{9,13},{13,9},{2,6},{6,2},{1... | collective-permute-start | bytes 602120 | tf_op jit(solution)/shard_map/ppermute | solution.py:32
  39.7 6.6 %collective-permute-start.8 = (bf16[96,896]{1,0:T(8,128)(2,1)S(1)}, bf16[96,896]{1,0:T(8,128)(2,1)S(1)}, u32[]{:S(2)}, u32[]{:S(2)}) collective-permute-start(bf16[96,896]{1,0:T(8,128)(2,1)S(1)} %slice.56), channel_id=1, source_target_pairs={{0,8},{4,12},{8,0},{12,4},{1,9},{5,13},{9,1},{13,5},{2,10},{6,14},... | collective-permute-start | bytes 516104 | tf_op jit(solution)/shard_map/ppermute | solution.py:32
  41.3 5.0 %collective-permute-start.10 = (f32[2]{0:T(128)S(1)}, f32[2]{0:T(128)S(1)}, u32[]{:S(2)}, u32[]{:S(2)}) collective-permute-start(f32[2]{0:T(128)S(1)} %add.35), channel_id=1, source_target_pairs={{0,8},{4,12},{8,0},{12,4},{1,9},{5,13},{9,1},{13,5},{2,10},{6,14},... | collective-permute-start | bytes 32 | tf_op jit(solution)/shard_map/ppermute | solution.py:32
  46.4 1.2 copy-start.4
  47.6 1.7 collective-permute-start.11
  49.3 49.0 %copy-start = (s32[400,400]{1,0:T(8,128)S(1)}, s32[400,400]{1,0:T(8,128)}, u32[]{:S(2)}) copy-start(s32[400,400]{1,0:T(8,128)} %refs_5_.1) | copy-start | bytes 1920004
  49.3 49.1 %copy-start.1 = (s32[64,400]{1,0:T(8,128)S(1)}, s32[64,400]{1,0:T(8,128)}, u32[]{:S(2)}) copy-start(s32[64,400]{1,0:T(8,128)} %mask_ref.5) | copy-start | bytes 307204
  148.2 3.4 %collective-permute-start.12 = (bf16[4,104,1552]{2,1,0:T(8,128)(2,1)}, bf16[4,104,1552]{2,1,0:T(8,128)(2,1)S(1)}, u32[]{:S(2)}, u32[]{:S(2)}) collective-permute-start(bf16[4,104,1552]{2,1,0:T(8,128)(2,1)} %get-tuple-element.50), channel_id=1, source_target_pairs={{0,16},{16,0},{1,17},{17,1},{2,18},{18,2},{3,19},{19,3},{4,20},{20... | collective-permute-start | bytes 3873800 | tf_op jit(solution)/shard_map/ppermute | solution.py:32
  154.4 21.4 %all-to-all-start = ((bf16[4,104,1552]{2,1,0:T(8,128)(2,1)}), bf16[4,104,1552]{2,1,0:T(8,128)(2,1)S(1)}, u32[]{:S(2)}, u32[]{:S(2)}) async-start(bf16[4,104,1552]{2,1,0:T(8,128)(2,1)} %add_convert_fusion), calls=%async_computation | async-start | bytes 2768896 | tf_op jit(solution)/shard_map/all_to_all | solution.py:691
  177.1 20.6 %all-to-all-start.1 = ((bf16[4,104,1552]{2,1,0:T(8,128)(2,1)}), bf16[4,104,1552]{2,1,0:T(8,128)(2,1)S(1)}, u32[]{:S(2)}, u32[]{:S(2)}) async-start(bf16[4,104,1552]{2,1,0:T(8,128)(2,1)} %broadcast_in_dim.33), calls=%async_computation.1 | async-start | bytes 2768896 | tf_op jit(solution)/shard_map/all_to_all | solution.py:702
  180.7 1.7 collective-permute-start.13
  185.5 4.4 %collective-permute-start.14 = (f32[2,2]{1,0:T(2,128)S(1)}, f32[2,2]{1,0:T(2,128)S(1)}, u32[]{:S(2)}, u32[]{:S(2)}) collective-permute-start(f32[2,2]{1,0:T(2,128)S(1)} %reshape.49), channel_id=1, source_target_pairs={{0,1},{1,0},{2,3},{3,2},{4,5},{5,4},{6,7},{7,6},{8,9},{9,8},{10,11... | collective-permute-start | bytes 56 | tf_op jit(solution)/shard_map/ppermute | solution.py:32
  185.8 4.5 %collective-permute-start.15 = (f32[2,2]{1,0:T(2,128)S(1)}, f32[2,2]{1,0:T(2,128)S(1)}, u32[]{:S(2)}, u32[]{:S(2)}) collective-permute-start(f32[2,2]{1,0:T(2,128)S(1)} %reshape.49), channel_id=1, source_target_pairs={{0,2},{1,3},{2,0},{3,1},{4,6},{5,7},{6,4},{7,5},{8,10},{9,11},{10,... | collective-permute-start | bytes 56 | tf_op jit(solution)/shard_map/ppermute | solution.py:32
  187.5 5.4 %collective-permute-start.16 = (f32[2,2]{1,0:T(2,128)S(1)}, f32[2,2]{1,0:T(2,128)S(1)}, u32[]{:S(2)}, u32[]{:S(2)}) collective-permute-start(f32[2,2]{1,0:T(2,128)S(1)} %reshape.49), channel_id=1, source_target_pairs={{0,3},{1,2},{2,1},{3,0},{4,7},{5,6},{6,5},{7,4},{8,11},{9,10},{10,... | collective-permute-start | bytes 56 | tf_op jit(solution)/shard_map/ppermute | solution.py:32
  192.8 4.9 %collective-permute-start.17 = (f32[2,2]{1,0:T(2,128)S(1)}, f32[2,2]{1,0:T(2,128)S(1)}, u32[]{:S(2)}, u32[]{:S(2)}) collective-permute-start(f32[2,2]{1,0:T(2,128)S(1)} %add_add_fusion.1), channel_id=1, source_target_pairs={{0,4},{4,0},{8,12},{12,8},{1,5},{5,1},{9,13},{13,9},{2,6},{6,2},{1... | collective-permute-start | bytes 56 | tf_op jit(solution)/shard_map/ppermute | solution.py:32
  194.8 6.3 %collective-permute-start.18 = (f32[2,2]{1,0:T(2,128)S(1)}, f32[2,2]{1,0:T(2,128)S(1)}, u32[]{:S(2)}, u32[]{:S(2)}) collective-permute-start(f32[2,2]{1,0:T(2,128)S(1)} %add_add_fusion.1), channel_id=1, source_target_pairs={{0,8},{4,12},{8,0},{12,4},{1,9},{5,13},{9,1},{13,5},{2,10},{6,14},... | collective-permute-start | bytes 56 | tf_op jit(solution)/shard_map/ppermute | solution.py:32
  196.2 4.9 %collective-permute-start.19 = (f32[2,2]{1,0:T(2,128)S(1)}, f32[2,2]{1,0:T(2,128)S(1)}, u32[]{:S(2)}, u32[]{:S(2)}) collective-permute-start(f32[2,2]{1,0:T(2,128)S(1)} %add_add_fusion.1), channel_id=1, source_target_pairs={{0,12},{4,8},{8,4},{12,0},{1,13},{5,9},{9,5},{13,1},{2,14},{6,10},... | collective-permute-start | bytes 56 | tf_op jit(solution)/shard_map/ppermute | solution.py:32
